TPU v7x, 128 devices: a whole 4x4x4 slice. The times are simulated.
128 devices in a mesh: grp: 8 (over z, core), tok: 16 (over y, x).
Axes of the slice: x: 4, y: 4, z: 4, core: 2. Of those that a mesh axis runs over, the one named last changes fastest.
Arguments:
- guess_symbol_ids: int32 [4096], replicated, may hold values from 0 to 32767
- symbol_vector_lookup: bfloat16 [32768, 4096], P('tok', 'grp'), may hold values from -6 to 6
- prior_attention_normed: bfloat16 [256, 4096], P('tok', 'grp'), may hold values from -6 to 6
- prior_feedforward_normed: bfloat16 [256, 4096], P('tok', 'grp'), may hold values from -6 to 6
- layernorm_scales: float32 [3, 4096], replicated, may hold values from 0.25 to 1.75
- lagged_blend_ratios: float32 [7, 4096], replicated, may hold values from 0.05 to 0.95
- attention_matrices: bfloat16 [4, 4096, 4096], P(None, None, 'grp'), may hold values from -0.09375 to 0.09375
- forgetting_baseline_vector: float32 [4096], replicated, may hold values from -6 to -0.5
- forgetting_narrow_matrix: bfloat16 [4096, 128], replicated, may hold values from -0.09375 to 0.09375
- forgetting_widen_matrix: bfloat16 [128, 4096], P(None, 'grp'), may hold values from -0.5 to 0.5
- diagonal_boost: float32 [4096], replicated, may hold values from -3 to 3
- attention_result_matrix: bfloat16 [4096, 4096], P('grp', 'tok'), may hold values from -0.09375 to 0.09375
- feedforward_lookup_matrix: bfloat16 [4096, 7168], P('tok', 'grp'), may hold values from -0.09375 to 0.09375
- feedforward_content_matrix: bfloat16 [7168, 4096], P('grp', 'tok'), may hold values from -0.0625 to 0.0625
- feedforward_gating_matrix: bfloat16 [4096, 4096], P('tok', 'grp'), may hold values from -0.09375 to 0.09375
- memory_matrix_store: float32 [256, 64, 4096], P('tok', 'grp'), may hold values from -6 to 6
- query_memory_slot: int32 [128], replicated, may hold values from 0 to 255, as said below
- candidate_tally_each_query: int32 [16, 8], replicated, may hold values from 1 to 4, 16 in all within a row
- kept_guess_tally: int32 [256], P('tok'), may hold values from 0 to 16
Outputs:
- layer_out: bfloat16 [4096, 4096], P('tok', 'grp')
- shift_att_out: bfloat16 [256, 4096], P('tok', 'grp')
- shift_ffn_out: bfloat16 [256, 4096], P('tok', 'grp')
- store_out: float32 [256, 64, 4096], P('tok', 'grp')
Inputs may be any that keep to these rules, and one draw needn't show every extreme that they name: `query_memory_slot`: pages of different requests differ. Page p lies on tok index p // 16, slot p % 16. The 8 requests r * 8 onward, whose branches are branches r * 16 onward, have pages on pairwise different tok indices. `candidate_tally_each_query`: row r holds the branch counts of requests r * 8 onward, in order; each row sums to 16.
All inputs are finite; a program needn't handle non-finite values.
Results may differ from a plain program's by a relative error of at most 0.02.
Values may be sent and summed in bfloat16 or wider, within the bound.
A program may use at most 192 MiB of HBM per device.

v0:
```python
import jax
import jax.numpy as jnp
from jax import lax
from jax.sharding import PartitionSpec as P

HIDDEN_BREADTH = 4096
PART_BREADTH = 64
GUESS_SYMBOLS = 16


EPSILON = 1e-05
HEAD_EPSILON = 0.00064


def normalize(tensor, gain_row, eps_value):
    row_mean = jnp.mean(tensor, axis=-1, keepdims=True)
    centered = tensor - row_mean
    spread = jnp.mean(centered * centered, axis=-1, keepdims=True)
    return centered * lax.rsqrt(spread + eps_value) * gain_row


def shifted(normed, carried):
    return jnp.concatenate([carried.astype(jnp.float32)[:, None, :], normed[:, :-1, :]], axis=1)


def mix_input(normed, before, coeff):
    return (normed + (before - normed) * coeff).reshape(-1, normed.shape[-1]).astype(jnp.bfloat16)


def memory_matrix_sweep(
    gating_vectors,
    lookup_vectors,
    content_vectors,
    forgetting_multiplier,
    extra_head_rows,
    initial_memory_matrix,
    accepted_count,
    draft_length,
):

    def scan_step(carry_state, inputs):
        wkv_state, chosen_candidate = carry_state
        current_receptance, current_key, current_value, decay_now, step_index = inputs
        current_token_term = (
            jnp.sum(current_receptance * extra_head_rows * current_key, axis=-1, keepdims=True)
            * current_value
        )
        head_out = (
            jnp.einsum(
                "bhi,bhij->bhj", current_receptance, wkv_state, precision=lax.Precision.HIGHEST
            )
            + current_token_term
        )
        wkv_state = (
            decay_now[..., None] * wkv_state + current_key[..., None] * current_value[..., None, :]
        )
        chosen_candidate = jnp.where(
            (accepted_count == step_index + 1)[:, None, None, None], wkv_state, chosen_candidate
        )
        return ((wkv_state, chosen_candidate), head_out)

    step_ids = jnp.arange(draft_length, dtype=jnp.int32)
    (final_state, chosen_candidate), attention_part_results = lax.scan(
        scan_step,
        (initial_memory_matrix, initial_memory_matrix),
        (gating_vectors, lookup_vectors, content_vectors, forgetting_multiplier, step_ids),
    )
    return (attention_part_results, chosen_candidate)


def keep_shift(normed, carried, kept_guess_tally, first_vector_slice, hidden_breadth):
    last_index = jnp.maximum(kept_guess_tally - 1, 0)
    picked = jnp.take_along_axis(normed, last_index[:, None, None], axis=1)[:, 0]
    picked = lax.dynamic_slice_in_dim(picked, first_vector_slice, hidden_breadth, 1)
    return jnp.where((kept_guess_tally > 0)[:, None], picked, carried.astype(jnp.float32)).astype(
        jnp.bfloat16
    )


def add_rows(operand, piece):
    return jnp.dot(operand, piece, preferred_element_type=jnp.float32)


def body(
    guess_symbol_ids,
    symbol_vector_lookup,
    prior_attention_normed,
    prior_feedforward_normed,
    layernorm_scales,
    lagged_blend_ratios,
    attention_matrices,
    forgetting_baseline_vector,
    forgetting_narrow_matrix,
    forgetting_widen_matrix,
    diagonal_boost,
    attention_result_matrix,
    feedforward_lookup_matrix,
    feedforward_content_matrix,
    feedforward_gating_matrix,
    memory_matrix_store,
    query_memory_slot,
    candidate_tally_each_query,
    kept_guess_tally,
):
    tok_count = lax.axis_size("tok")
    tok_at = lax.axis_index("tok")
    grp_at = lax.axis_index("grp")
    branch_local, hidden_breadth = prior_attention_normed.shape
    row_count = branch_local * GUESS_SYMBOLS
    vocab_rows = symbol_vector_lookup.shape[0]
    first_vector_slice = grp_at * hidden_breadth
    head_local_output = hidden_breadth // PART_BREADTH
    wanted = guess_symbol_ids - tok_at * vocab_rows
    inside = (wanted >= 0) & (wanted < vocab_rows)
    found = jnp.take(symbol_vector_lookup, jnp.clip(wanted, 0, vocab_rows - 1), axis=0)
    embedded = lax.psum_scatter(
        jnp.where(inside[:, None], found.astype(jnp.float32), 0.0).astype(jnp.bfloat16),
        "tok",
        scatter_dimension=0,
        tiled=True,
    )
    whole_x, whole_att, whole_ffn = (
        lax.all_gather(embedded, "grp", axis=1, tiled=True),
        lax.all_gather(prior_attention_normed, "grp", axis=1, tiled=True),
        lax.all_gather(prior_feedforward_normed, "grp", axis=1, tiled=True),
    )
    base_values = whole_x.astype(jnp.float32)
    normed = normalize(base_values, layernorm_scales[0], EPSILON).reshape(
        branch_local, GUESS_SYMBOLS, HIDDEN_BREADTH
    )
    before = shifted(normed, whole_att)

    def project(index, weight):
        return jnp.dot(
            mix_input(normed, before, lagged_blend_ratios[index]),
            weight,
            preferred_element_type=jnp.float32,
        )

    gating_vectors = project(0, attention_matrices[0])
    lookup_vectors = project(1, attention_matrices[1])
    content_vectors = project(2, attention_matrices[2])
    gate_proj = jax.nn.silu(project(3, attention_matrices[3]))
    lowrank = jnp.tanh(project(4, forgetting_narrow_matrix)).astype(jnp.bfloat16)
    base_decay = lax.dynamic_slice_in_dim(
        forgetting_baseline_vector, first_vector_slice, hidden_breadth, 0
    )
    forgetting_multiplier = jnp.exp(
        -jnp.exp(
            base_decay
            + jnp.dot(lowrank, forgetting_widen_matrix, preferred_element_type=jnp.float32)
        )
    )
    slot_count = memory_matrix_store.shape[0]
    req_local = candidate_tally_each_query.shape[1]
    owners = (query_memory_slot // slot_count).reshape(tok_count, req_local)
    places = (query_memory_slot % slot_count).reshape(tok_count, req_local)
    owned_here = owners == tok_at
    send_slot = jnp.sum(jnp.where(owned_here, places, 0), axis=1)
    sending = jnp.any(owned_here, axis=1)
    outgoing = jnp.where(
        sending[:, None, None], jnp.take(memory_matrix_store, send_slot, axis=0), 0.0
    )
    incoming = lax.all_to_all(
        outgoing.astype(jnp.bfloat16), "tok", split_axis=0, concat_axis=0, tiled=True
    ).astype(outgoing.dtype)
    my_owners = lax.dynamic_index_in_dim(owners, tok_at, 0, keepdims=False)
    my_pages = jnp.take(incoming, my_owners, axis=0)
    my_counts = lax.dynamic_index_in_dim(candidate_tally_each_query, tok_at, 0, keepdims=False)
    request_ends = jnp.cumsum(my_counts)
    local_ids = jnp.arange(branch_local, dtype=jnp.int32)
    request_of = jnp.sum((request_ends[None, :] <= local_ids[:, None]).astype(jnp.int32), axis=1)
    initial_memory_matrix = jnp.take(my_pages, request_of, axis=0).reshape(
        branch_local, head_local_output, PART_BREADTH, PART_BREADTH
    )

    def divide_among_parts(tensor):
        return tensor.reshape(
            branch_local, GUESS_SYMBOLS, head_local_output, PART_BREADTH
        ).transpose(1, 0, 2, 3)

    surplus_nearby_entries = lax.dynamic_slice_in_dim(
        diagonal_boost, first_vector_slice, hidden_breadth, 0
    ).reshape(head_local_output, PART_BREADTH)
    attention_part_results, chosen_candidate = memory_matrix_sweep(
        divide_among_parts(gating_vectors),
        divide_among_parts(lookup_vectors),
        divide_among_parts(content_vectors),
        divide_among_parts(forgetting_multiplier),
        surplus_nearby_entries,
        initial_memory_matrix,
        kept_guess_tally,
        GUESS_SYMBOLS,
    )
    head_gain = lax.dynamic_slice_in_dim(
        layernorm_scales[2], first_vector_slice, hidden_breadth, 0
    ).reshape(head_local_output, PART_BREADTH)
    head_normed = (
        normalize(attention_part_results, head_gain, HEAD_EPSILON)
        .transpose(1, 0, 2, 3)
        .reshape(row_count, hidden_breadth)
    )
    attended = (head_normed * gate_proj).astype(jnp.bfloat16)
    partial_att = jnp.dot(
        attended,
        lax.all_gather(attention_result_matrix, "tok", axis=1, tiled=True),
        preferred_element_type=jnp.float32,
    )
    shares = lax.psum_scatter(
        partial_att.astype(jnp.bfloat16), "grp", scatter_dimension=1, tiled=True
    ).astype(jnp.float32)
    own_x = lax.dynamic_slice_in_dim(base_values, first_vector_slice, hidden_breadth, 1)
    residual = (own_x + shares).astype(jnp.bfloat16)
    whole_res = lax.all_gather(residual, "grp", axis=1, tiled=True)
    residual_values = whole_res.astype(jnp.float32)
    normed2 = normalize(residual_values, layernorm_scales[1], EPSILON).reshape(
        branch_local, GUESS_SYMBOLS, HIDDEN_BREADTH
    )
    before2 = shifted(normed2, whole_ffn)
    key_in = mix_input(normed2, before2, lagged_blend_ratios[5])
    rec_in = mix_input(normed2, before2, lagged_blend_ratios[6])
    key_sum = add_rows(key_in, lax.all_gather(feedforward_lookup_matrix, "tok", axis=0, tiled=True))
    rec_sum = add_rows(rec_in, lax.all_gather(feedforward_gating_matrix, "tok", axis=0, tiled=True))
    hidden = jnp.square(jax.nn.relu(key_sum)).astype(jnp.bfloat16)
    partial_ffn = jnp.dot(
        hidden,
        lax.all_gather(feedforward_content_matrix, "tok", axis=1, tiled=True),
        preferred_element_type=jnp.float32,
    )
    ffn_share = lax.psum_scatter(
        partial_ffn.astype(jnp.bfloat16), "grp", scatter_dimension=1, tiled=True
    ).astype(jnp.float32)
    layer_out = (residual.astype(jnp.float32) + jax.nn.sigmoid(rec_sum) * ffn_share).astype(
        jnp.bfloat16
    )
    shift_att_out = keep_shift(
        normed, prior_attention_normed, kept_guess_tally, first_vector_slice, hidden_breadth
    )
    shift_ffn_out = keep_shift(
        normed2, prior_feedforward_normed, kept_guess_tally, first_vector_slice, hidden_breadth
    )
    branch_score = kept_guess_tally * branch_local + (branch_local - 1 - local_ids)
    member = request_of[None, :] == jnp.arange(req_local, dtype=jnp.int32)[:, None]
    best_score = jnp.max(jnp.where(member, branch_score[None, :], -1), axis=1)
    winner = branch_local - 1 - best_score % branch_local
    new_pages = jnp.take(chosen_candidate, winner, axis=0).reshape(
        req_local, head_local_output, PART_BREADTH * PART_BREADTH
    )
    targets = my_owners[None, :] == jnp.arange(tok_count, dtype=jnp.int32)[:, None]
    pick_index = jnp.sum(
        jnp.where(targets, jnp.arange(req_local, dtype=jnp.int32)[None, :], 0), axis=1
    )
    going = jnp.any(targets, axis=1)
    outgoing_back = jnp.where(going[:, None, None], jnp.take(new_pages, pick_index, axis=0), 0.0)
    returned = lax.all_to_all(
        outgoing_back.astype(jnp.bfloat16), "tok", split_axis=0, concat_axis=0, tiled=True
    ).astype(outgoing_back.dtype)
    writes = (
        (send_slot[None, :] == jnp.arange(slot_count, dtype=jnp.int32)[:, None]) & sending[None, :]
    ).astype(jnp.float32)
    placed = jnp.dot(
        writes, returned.reshape(tok_count, -1), precision=lax.Precision.HIGHEST
    ).reshape(memory_matrix_store.shape)
    store_out = jnp.where(
        (jnp.sum(writes, axis=1) > 0.5)[:, None, None], placed, memory_matrix_store
    )
    return (layer_out, shift_att_out, shift_ffn_out, store_out)


def solution(mesh):
    in_specs = (
        P(),
        P("tok", "grp"),
        P("tok", "grp"),
        P("tok", "grp"),
        P(),
        P(),
        P(None, None, "grp"),
        P(),
        P(),
        P(None, "grp"),
        P(),
        P("grp", "tok"),
        P("tok", "grp"),
        P("grp", "tok"),
        P("tok", "grp"),
        P("tok", "grp", None),
        P(),
        P(),
        P("tok"),
    )
    out_specs = (P("tok", "grp"), P("tok", "grp"), P("tok", "grp"), P("tok", "grp", None))
    return jax.shard_map(body, mesh=mesh, in_specs=in_specs, out_specs=out_specs, check_vma=False)
```

profile of v0, /device:TPU:1, one launch (start us, length us, event | category | flops | bytes accessed | tf_op | source)
XLA Modules:
  0.0 821.4 jit_solution(9953232027514825805)
XLA Ops:
  8.9 17.3 %gather_fusion = bf16[4096,512]{1,0:T(8,128)(2,1)} fusion(bf16[2048,512]{1,0:T(8,128)(2,1)S(1)} %copy-done, s32[4096]{0:T(1024)S(1)} %fusion.51), kind=kCustom, calls=%fused_computation.4 | custom fusion | bytes 8404992 | tf_op jit(solution)/shard_map/jit(_take)/gather | solution.py:115
  31.5 79.1 %reduce-scatter.4.cloned.1.call-done = bf16[256,512]{1,0:T(8,128)(2,1)} async-done(((bf16[4096,512]{1,0:T(8,128)(2,1)}), bf16[256,512]{1,0:T(8,128)(2,1)}) %reduce-scatter.4.cloned.1.call-update) | async-done | bytes 262160 | tf_op jit(solution)/shard_map/reduce_scatter | solution.py:116
  119.4 15.6 %all_gather.25 = bf16[16,4096]{1,0:T(8,128)(2,1)S(1)} all-gather(bf16[16,512]{1,0:T(8,128)(2,1)S(1)} %copy-done.16), channel_id=1, replica_groups=mesh['grp'=8,'tok'=16] {'grp'}, dimensions={1}, use_global_device_ids=true | all-gather | bytes 147456 | tf_op jit(solution)/shard_map/all_gather | solution.py:124
  136.0 9.1 %slice_bitcast_fusion = (bf16[512,4096]{0,1:T(8,128)(2,1)}, bf16[512,4096]{0,1:T(8,128)(2,1)}, bf16[512,4096]{0,1:T(8,128)(2,1)}) fusion(bf16[4,4096,512]{2,1,0:T(8,128)(2,1)} %param.31), kind=kLoop, calls=%fused_computation.44 | loop fusion | bytes 25165824 | tf_op jit(solution)/shard_map/dot_general | solution.py:134
  145.1 6.4 copy.47
  151.5 6.4 copy.46
  157.9 6.5 copy.45
  188.9 5.6 add_convert_fusion.3
  204.3 6.3 convolution_bitcast_fusion
  217.4 284.8 %while.14 = (s32[]{:T(128)}, f32[16,8,64,64]{3,2,1,0:T(8,128)}, bf16[16,8,64,64]{3,2,1,0:T(8,128)(2,1)S(1)}, f32[16,16,8,64]{3,2,1,0:T(8,128)S(1)}, f32[16,16,8,...) while((s32[]{:T(128)}, f32[16,8,64,64]{3,2,1,0:T(8,128)}, ...), condition=%wide.region_9.11_spmd, body=%wide.region_7.10_spmd.sunk | while | flops 8421586 | bytes 9150729 | solution.py:63
  218.7 5.3 fusion.91
  228.6 6.6 broadcast_select_fusion.5
  236.5 5.3 fusion.91
  246.4 6.6 broadcast_select_fusion.5
  254.3 5.3 fusion.91
  264.2 6.6 broadcast_select_fusion.5
  272.0 5.3 fusion.91
  282.0 6.6 broadcast_select_fusion.5
  289.8 5.3 fusion.91
  299.8 6.6 broadcast_select_fusion.5
  307.6 5.3 fusion.91
  317.5 6.6 broadcast_select_fusion.5
  325.4 5.3 fusion.91
  335.3 6.6 broadcast_select_fusion.5
  343.2 5.3 fusion.91
  353.1 6.6 broadcast_select_fusion.5
  361.0 5.3 fusion.91
  370.9 6.6 broadcast_select_fusion.5
  378.8 5.3 fusion.91
  388.7 6.6 broadcast_select_fusion.5
  396.6 5.3 fusion.91
  406.5 6.6 broadcast_select_fusion.5
  424.3 6.6 broadcast_select_fusion.5
  442.1 6.6 broadcast_select_fusion.5
  459.9 6.6 broadcast_select_fusion.5
  477.7 6.6 broadcast_select_fusion.5
  495.5 6.6 broadcast_select_fusion.5
  505.1 9.2 %convolution_convert_fusion.1 = bf16[256,4096]{1,0:T(8,128)(2,1)} fusion(bf16[512,4096]{1,0:T(8,128)(2,1)} %all-gather.9.cloned.1.call-done, f32[256,512]{1,0:T(8,128)} %reshape.318, bf16[4,4096,512]{2,1,0:T(8,128)(2,1)} %param.31, f32[256,4096]{1,0:T(8,128)} %get-tuple-element.145, f32[4096]{0:T(1024)S(1)} %bitcast.225, ...), kind=kOutput, calls=%fused_computation.28 | convolution fusion | flops 2156658688 | bytes 17336320 | tf_op jit(solution)/shard_map/dot_general | solution.py:204
  518.5 27.3 %reduce-scatter.6.cloned.1.call-done = bf16[256,512]{1,0:T(8,128)(2,1)} async-done(((bf16[256,4096]{1,0:T(8,128)(2,1)}), bf16[256,512]{1,0:T(8,128)(2,1)}) %reduce-scatter.6.cloned.1.call-update) | async-done | bytes 262160 | tf_op jit(solution)/shard_map/reduce_scatter | solution.py:209
  549.8 16.4 %all_gather.28 = bf16[16,4096]{1,0:T(8,128)(2,1)S(1)} all-gather(bf16[16,512]{1,0:T(8,128)(2,1)S(1)} %copy-done.18), channel_id=1, replica_groups=mesh['grp'=8,'tok'=16] {'grp'}, dimensions={1}, use_global_device_ids=true | all-gather | bytes 147456 | tf_op jit(solution)/shard_map/all_gather | solution.py:125
  566.6 9.2 %all-gather.11.cloned.1.call-done = bf16[256,4096]{1,0:T(8,128)(2,1)} async-done(((bf16[256,512]{1,0:T(8,128)(2,1)}), bf16[256,4096]{1,0:T(8,128)(2,1)}) %all-gather.11.cloned.1.call-update) | async-done | bytes 2097168 | tf_op jit(solution)/shard_map/all_gather | solution.py:214
  586.3 57.6 %all-gather.15.cloned.1.call-done = bf16[4096,896]{1,0:T(8,128)(2,1)} async-done(((bf16[256,896]{1,0:T(8,128)(2,1)}), bf16[4096,896]{1,0:T(8,128)(2,1)}) %all-gather.15.cloned.1.call-update) | async-done | bytes 7340048 | tf_op jit(solution)/shard_map/all_gather | solution.py:222
  643.9 74.1 %all-gather.17.cloned.1.call-done = bf16[896,4096]{1,0:T(8,128)(2,1)} async-done(((bf16[896,256]{1,0:T(8,128)(2,1)}), bf16[896,4096]{1,0:T(8,128)(2,1)}) %all-gather.17.cloned.1.call-update) | async-done | bytes 7340048 | tf_op jit(solution)/shard_map/all_gather | solution.py:227
  718.0 12.9 %convolution_convert_fusion = bf16[256,4096]{1,0:T(8,128)(2,1)} fusion(bf16[896,4096]{1,0:T(8,128)(2,1)} %all-gather.17.cloned.1.call-done, bf16[4096,896]{1,0:T(8,128)(2,1)} %all-gather.15.cloned.1.call-done, f32[256,4096]{1,0:T(8,128)} %bitcast_subtract_fusion, f32[4096]{0:T(1024)S(1)} %bitcast.224, bf16[256,4096]{1,0:T(8,128)(2,1)} %all-gather.11.cloned.1.call-done, ...), kind=kOutput, calls=%fused_computation.27 | convolution fusion | flops 3767173120 | bytes 23103488 | tf_op jit(solution)/shard_map/dot_general | solution.py:225
  742.6 12.3 %all-to-all-done.1 = bf16[16,8,4096]{2,1,0:T(8,128)(2,1)S(1)} async-done(((bf16[16,8,4096]{2,1,0:T(8,128)(2,1)}), bf16[16,8,4096]{2,1,0:T(8,128)(2,1)S(1)}, u32[]{:S(2)}, u32[]{:S(2)}) %all-to-all-start.1) | async-done | bytes 1048608 | tf_op jit(solution)/shard_map/all_to_all | solution.py:255
  764.0 11.4 %all-gather.13.cloned.1.call-done = bf16[4096,512]{1,0:T(8,128)(2,1)} async-done(((bf16[256,512]{1,0:T(8,128)(2,1)}), bf16[4096,512]{1,0:T(8,128)(2,1)}) %all-gather.13.cloned.1.call-update) | async-done | bytes 4194320 | tf_op jit(solution)/shard_map/all_gather | solution.py:223
  775.3 33.0 %reduce-scatter.8.cloned.1.call-done = bf16[256,512]{1,0:T(8,128)(2,1)} async-done(((bf16[256,4096]{1,0:T(8,128)(2,1)}), bf16[256,512]{1,0:T(8,128)(2,1)}) %reduce-scatter.8.cloned.1.call-update) | async-done | bytes 262160 | tf_op jit(solution)/shard_map/reduce_scatter | solution.py:230
  808.3 6.3 fusion.34
  (290 shorter events, 210.2 us)
Async XLA Ops:
  7.2 1.7 copy-start
  7.2 103.5 %reduce-scatter.4.cloned.1.call-start = ((), (), s32[]{:S(2)}) async-start(), calls=%async_computation.5 | async-start | bytes 4456448 | tf_op jit(solution)/shard_map/reduce_scatter | solution.py:116
  31.4 79.3 %copy-start.28 = (s32[128]{0:T(128)S(1)}, s32[128]{0:T(128)}, u32[]{:S(2)}) copy-start(s32[128]{0:T(128)} %param.41) | copy-start | bytes 1540
  31.4 79.7 %copy-start.6 = (f32[16,8,4096]{2,1,0:T(8,128)S(1)}, f32[16,8,4096]{2,1,0:T(8,128)}, u32[]{:S(2)}) copy-start(f32[16,8,4096]{2,1,0:T(8,128)} %param.40) | copy-start | bytes 6291460
  31.4 80.4 %copy-start.26 = (s32[16]{0:T(128)S(1)}, s32[16]{0:T(128)}, u32[]{:S(2)}) copy-start(s32[16]{0:T(128)} %param.43) | copy-start | bytes 196
  31.5 87.9 %copy-start.20 = (f32[3,4096]{1,0:T(4,128)S(1)}, f32[3,4096]{1,0:T(4,128)}, u32[]{:S(2)}) copy-start(f32[3,4096]{1,0:T(4,128)} %param.29) | copy-start | bytes 147460
  31.5 87.9 %copy-start.16 = (bf16[16,512]{1,0:T(8,128)(2,1)S(1)}, bf16[16,512]{1,0:T(8,128)(2,1)}, u32[]{:S(2)}) copy-start(bf16[16,512]{1,0:T(8,128)(2,1)} %param.27) | copy-start | bytes 49156
  31.5 150.0 %all-gather.7.cloned.1.call-start = ((), (), s32[]{:S(2)}) async-start(), calls=%async_computation.6 | async-start | bytes 2359296 | tf_op jit(solution)/shard_map/all_gather | solution.py:123
  111.0 628.7 %copy-start.22 = (pred[16]{0:T(512)(128)(4,1)}, pred[16]{0:T(512)(128)(4,1)S(1)}, u32[]{:S(2)}) copy-start(pred[16]{0:T(512)(128)(4,1)S(1)} %get-tuple-element.137) | copy-start | bytes 52
  113.7 53.6 %all-to-all-start = ((bf16[16,8,4096]{2,1,0:T(8,128)(2,1)}), bf16[16,8,4096]{2,1,0:T(8,128)(2,1)}, u32[]{:S(2)}, u32[]{:S(2)}) async-start(bf16[16,8,4096]{2,1,0:T(8,128)(2,1)} %select_convert_fusion.1), calls=%async_computation.1 | async-start | bytes 2097152 | tf_op jit(solution)/shard_map/all_to_all | solution.py:164
  118.5 386.6 %all-gather.9.cloned.1.call-start = ((), (), s32[]{:S(2)}) async-start(), calls=%async_computation.7 | async-start | bytes 4456448 | tf_op jit(solution)/shard_map/all_gather | solution.py:206
  119.2 426.5 %reduce-scatter.6.cloned.1.call-start = ((), (), s32[]{:S(2)}) async-start(), calls=%async_computation.8 | async-start | bytes 2359296 | tf_op jit(solution)/shard_map/reduce_scatter | solution.py:209
  119.4 598.6 %copy-start.13 = (f32[1,4096]{1,0:T(1,128)}, f32[1,4096]{1,0:T(1,128)S(1)}, u32[]{:S(2)}) copy-start(f32[1,4096]{1,0:T(1,128)S(1)} %get-tuple-element.155) | copy-start | bytes 49156
  157.9 6.5 copy-start.23
  157.9 8.7 %copy-start.15 = (f32[7,4096]{1,0:T(8,128)S(1)}, f32[7,4096]{1,0:T(8,128)}, u32[]{:S(2)}) copy-start(f32[7,4096]{1,0:T(8,128)} %param.30) | copy-start | bytes 344068
  181.5 4.6 copy-start.2
  183.6 3.3 copy-start.11
  186.9 2.0 copy-start.4
  188.9 5.6 copy-start.27
  204.3 6.4 copy-start.8
  204.3 6.4 copy-start.10
  210.7 3.4 copy-start.7
  210.7 3.4 copy-start.9
  514.4 35.4 %copy-start.18 = (bf16[16,512]{1,0:T(8,128)(2,1)S(1)}, bf16[16,512]{1,0:T(8,128)(2,1)}, u32[]{:S(2)}) copy-start(bf16[16,512]{1,0:T(8,128)(2,1)} %param.28) | copy-start | bytes 49156
  514.4 61.4 %all-gather.11.cloned.1.call-start = ((), (), s32[]{:S(2)}) async-start(), calls=%async_computation.9 | async-start | bytes 2359296 | tf_op jit(solution)/shard_map/all_gather | solution.py:214
  547.7 96.2 %all-gather.15.cloned.1.call-start = ((), (), s32[]{:S(2)}) async-start(), calls=%async_computation.11 | async-start | bytes 7798784 | tf_op jit(solution)/shard_map/all_gather | solution.py:222
  548.3 169.7 %all-gather.17.cloned.1.call-start = ((), (), s32[]{:S(2)}) async-start(), calls=%async_computation.12 | async-start | bytes 7798784 | tf_op jit(solution)/shard_map/all_gather | solution.py:227
  549.0 226.3 %all-gather.13.cloned.1.call-start = ((), (), s32[]{:S(2)}) async-start(), calls=%async_computation.10 | async-start | bytes 4456448 | tf_op jit(solution)/shard_map/all_gather | solution.py:223
  549.8 258.6 %reduce-scatter.8.cloned.1.call-start = ((), (), s32[]{:S(2)}) async-start(), calls=%async_computation.13 | async-start | bytes 2359296 | tf_op jit(solution)/shard_map/reduce_scatter | solution.py:230
  575.8 4.4 copy-start.3
  581.0 2.1 copy-start.5
  734.8 20.1 %all-to-all-start.1 = ((bf16[16,8,4096]{2,1,0:T(8,128)(2,1)}), bf16[16,8,4096]{2,1,0:T(8,128)(2,1)S(1)}, u32[]{:S(2)}, u32[]{:S(2)}) async-start(bf16[16,8,4096]{2,1,0:T(8,128)(2,1)} %fusion.17), calls=%async_computation.4 | async-start | bytes 2097152 | tf_op jit(solution)/shard_map/all_to_all | solution.py:255
  755.0 53.4 %copy-start.12 = (bf16[256,512]{1,0:T(8,128)(2,1)S(1)}, bf16[256,512]{1,0:T(8,128)(2,1)}, u32[]{:S(2)}) copy-start(bf16[256,512]{1,0:T(8,128)(2,1)} %add_convert_fusion.39) | copy-start | bytes 786436
  759.0 4.3 copy-start.17
  759.0 4.3 copy-start.19
  759.0 4.3 copy-start.24
  759.0 4.3 copy-start.25
  759.0 49.3 %copy-start.14 = (f32[1,4096]{1,0:T(1,128)S(1)}, f32[1,4096]{1,0:T(1,128)}, u32[]{:S(2)}) copy-start(f32[1,4096]{1,0:T(1,128)} %copy-done.13) | copy-start | bytes 49156
  759.0 49.3 %copy-start.21 = (f32[1,4096]{1,0:T(1,128)S(1)}, f32[1,4096]{1,0:T(1,128)}, u32[]{:S(2)}) copy-start(f32[1,4096]{1,0:T(1,128)} %get-tuple-element.154) | copy-start | bytes 49156
  808.3 6.3 copy-start.1
Sparse Core Ops, SparseCore 0:
  31.6 79.0 reduce-scatter.3
  112.5 27.0 all-gather.6
  141.9 56.3 all-gather.8
  514.5 31.2 reduce-scatter.5
  548.0 27.7 all-gather.10
  578.0 65.8 all-gather.14
  646.2 71.7 all-gather.16
  720.3 54.9 all-gather.12
  777.9 30.4 reduce-scatter.7
where the time goes:
time: 836 us; the launch traced here: 821 us
  waiting for transfers between devices  307 us (37%)
  other arithmetic  176 us (21%)
  local copies, waits for them, and re-layouts  136 us (16%)
  matrix products  135 us (16%)
  blocking collectives  32.1 us (4%)
  between operations  14.7 us (2%)
  loops' own time  11 us (1%)
  starting transfers between devices  10 us (1%)
    select_n x16, other arithmetic, scan_step(): jnp.where((accepted_count == step_index + 1)[:, None, None, None], wkv_st...  105 us
    dot_general x16, matrix products, scan_step(): jnp.einsum('bhi,bhij->bhj', current_receptance, wkv_state, precision=lax....  84.5 us
    reduce_scatter x1, waiting for transfers between devices, body(): lax.psum_scatter(jnp.where(inside[:, None], found.astype(jnp.float32), 0....  79.1 us
    all_gather x1, waiting for transfers between devices, body(): lax.all_gather(feedforward_content_matrix, 'tok', axis=1, tiled=True)  74.1 us
    all_gather x1, waiting for transfers between devices, body(): lax.all_gather(feedforward_lookup_matrix, 'tok', axis=0, tiled=True)  57.6 us
    dynamic_slice x48, local copies, waits for them, and re-layouts, memory_matrix_sweep(): lax.scan(scan_step, (initial_memory_matrix, initial_memory_matrix), (gati...  47.6 us
    reduce_scatter x1, waiting for transfers between devices, body(): lax.psum_scatter(partial_ffn.astype(jnp.bfloat16), 'grp', scatter_dimensi...  33 us
    dot_general x4, local copies, waits for them, and re-layouts, project(): jnp.dot(mix_input(normed, before, lagged_blend_ratios[index]), weight, pr...  28.5 us
  transfers between devices with their start and end apart: 11, of which 8 were waited for; matrix products, arithmetic and copies ran while one was open for 49% of the time, Pallas kernels for 0%

commit v1 on v0

v1 whole, which is shorter than its diff:
```python
import functools

import jax
import jax.numpy as jnp
from jax import lax
from jax.experimental import pallas as pl
from jax.experimental.pallas import tpu as pltpu
from jax.sharding import PartitionSpec as P

HIDDEN = 4096
HEAD = 64
DRAFT = 16
BRANCH = 16
ROWS = BRANCH * DRAFT
WIDTH = 512
TOK = 16
GRP = 8
REQ = 8
PAIRS = 4
KEYS = 896
EPSILON = 1e-05
HEAD_EPSILON = 0.00064
F32 = jnp.float32
BF16 = jnp.bfloat16
MESH = pl.DeviceIdType.MESH
ANY = pl.BlockSpec(memory_space=pl.ANY)
VMEM = pl.BlockSpec(memory_space=pltpu.VMEM)


def remote(src, dst, send, recv, device):
    return pltpu.make_async_remote_copy(
        src_ref=src, dst_ref=dst, send_sem=send, recv_sem=recv, device_id=device, device_id_type=MESH
    )


def greet(devices):
    barrier = pltpu.get_barrier_semaphore()
    for device in devices:
        pl.semaphore_signal(barrier, inc=1, device_id=device, device_id_type=MESH)
    pl.semaphore_wait(barrier, len(devices))


def grp_places():
    g = lax.axis_index("grp")
    z, core = g // 2, g % 2
    up = lax.rem(z + 1, 4) * 2 + core
    down = lax.rem(z + 3, 4) * 2 + core
    far = lax.rem(z + 2, 4) * 2 + core
    mate = z * 2 + 1 - core
    return g, up, down, far, mate


def block_of(g):
    return pl.ds(pl.multiple_of(g * WIDTH, WIDTH), WIDTH)


def flip(g):
    return g + 1 - 2 * lax.rem(g, 2)


def gather_grp(own, out, send, recv, local):
    rows = out.shape[0]
    half = rows // 2
    g, up, down, far, mate = grp_places()
    first, last, whole = pl.ds(0, half), pl.ds(half, rows - half), pl.ds(0, rows)
    at = lambda part, g_of: out.at[part, block_of(g_of)]
    keep = pltpu.make_async_copy(own, at(whole, g), local)
    keep.start()
    started = []

    def go(index, src, part, g_of, target):
        copy = remote(src, at(part, g_of), send.at[index], recv.at[index], {"grp": target})
        copy.start()
        started.append(copy)

    def came(index, part, g_of):
        remote(at(part, g_of), at(part, g_of), send.at[index], recv.at[index], {"grp": mate}).wait_recv()

    go(0, own, whole, g, up)
    go(1, own, whole, g, down)
    go(2, own, whole, g, mate)
    came(0, whole, down)
    go(3, at(first, down), first, down, up)
    go(5, at(whole, down), whole, down, mate)
    came(1, whole, up)
    go(4, at(last, up), last, up, down)
    go(6, at(whole, up), whole, up, mate)
    came(3, first, far)
    go(7, at(first, far), first, far, mate)
    came(4, last, far)
    go(8, at(last, far), last, far, mate)
    came(2, whole, mate)
    came(5, whole, flip(down))
    came(6, whole, flip(up))
    came(7, first, flip(far))
    came(8, last, flip(far))
    keep.wait()
    for copy in started:
        copy.wait_send()


def reduce_grp(part, mated, sums, halves, full, send, recv):
    g, up, down, far, mate = grp_places()
    half = ROWS // 2
    started = []

    def go(index, src, dst, target):
        copy = remote(src, dst, send.at[index], recv.at[index], {"grp": target})
        copy.start()
        started.append(copy)

    def came(index, dst):
        remote(dst, dst, send.at[index], recv.at[index], {"grp": mate}).wait_recv()

    order = (far, up, down, g)
    for k in range(4):
        go(k, part.at[:, block_of(flip(order[k]))], mated.at[k], mate)

    def own(k):
        return part[:, block_of(order[k])].astype(F32) + mated[k].astype(F32)

    came(0, mated.at[0])
    sums[0] = own(0).astype(BF16)
    go(4, sums.at[0, pl.ds(0, half)], halves.at[0], up)
    go(5, sums.at[0, pl.ds(half, half)], halves.at[1], down)
    came(1, mated.at[1])
    came(4, halves.at[0])
    sums[1, :half] = (own(1)[:half] + halves[0].astype(F32)).astype(BF16)
    sums[1, half:] = own(1)[half:].astype(BF16)
    go(6, sums.at[1], full.at[0], up)
    came(2, mated.at[2])
    came(5, halves.at[1])
    sums[2, :half] = own(2)[:half].astype(BF16)
    sums[2, half:] = (own(2)[half:] + halves[1].astype(F32)).astype(BF16)
    go(7, sums.at[2], full.at[1], down)
    came(3, mated.at[3])
    came(6, full.at[0])
    came(7, full.at[1])
    total = own(3) + full[0].astype(F32) + full[1].astype(F32)
    for copy in started:
        copy.wait_send()
    return total


REDUCE_SCRATCH = [
    pltpu.VMEM((4, ROWS, WIDTH), BF16),
    pltpu.VMEM((3, ROWS, WIDTH), BF16),
    pltpu.VMEM((2, ROWS // 2, WIDTH), BF16),
    pltpu.VMEM((2, ROWS, WIDTH), BF16),
    pltpu.SemaphoreType.DMA((8,)),
    pltpu.SemaphoreType.DMA((8,)),
]


def grp_peers():
    _, up, down, _, mate = grp_places()
    return [{"grp": up}, {"grp": down}, {"grp": mate}]


def tok_peers():
    t = lax.axis_index("tok")
    return [{"tok": lax.rem(t + k, TOK)} for k in range(1, TOK)]


def trade_start(out_pages, in_pages, send, recv, local):
    t = lax.axis_index("tok")
    keep = pltpu.make_async_copy(out_pages.at[t], in_pages.at[t], local)
    keep.start()
    for k in range(1, TOK):
        peer = lax.rem(t + k, TOK)
        remote(out_pages.at[peer], in_pages.at[t], send.at[k - 1], recv.at[k - 1], {"tok": peer}).start()
    return keep


def trade_end(out_pages, in_pages, send, recv, keep):
    t = lax.axis_index("tok")
    keep.wait()
    for k in range(1, TOK):
        peer = lax.rem(t + k, TOK)
        origin = lax.rem(t + TOK - k, TOK)
        copy = remote(out_pages.at[peer], in_pages.at[origin], send.at[k - 1], recv.at[k - 1], {"tok": peer})
        copy.wait_recv()
        copy.wait_send()


TRADE_SEMAPHORES = [
    pltpu.SemaphoreType.DMA((TOK - 1,)),
    pltpu.SemaphoreType.DMA((TOK - 1,)),
    pltpu.SemaphoreType.DMA,
]


def embed_kernel(found, priors, out_pages, whole, in_pages, own, a1h, a1s, a1f, b1h, b1s, b1f, a2, a2h, a2s, a2f, b2, b2h, b2s, b2f, xsend, xrecv, gsend, grecv, glocal, tsend, trecv, tlocal):
    t = lax.axis_index("tok")
    y, x = t // 4, lax.rem(t, 4)
    xu, xd, xf = [lax.rem(x + k, 4) for k in (1, 3, 2)]
    yu, yd, yf = [lax.rem(y + k, 4) for k in (1, 3, 2)]
    along_x = lambda x_of: {"tok": y * 4 + x_of}
    along_y = lambda y_of: {"tok": y_of * 4 + x}
    greet(tok_peers() + grp_peers())
    started = []

    def go(index, src, dst, target):
        copy = remote(src, dst, xsend.at[index], xrecv.at[index], target)
        copy.start()
        started.append(copy)

    def came(index, dst):
        remote(dst, dst, xsend.at[index], xrecv.at[index], along_x(xu)).wait_recv()

    h = WIDTH // 2
    left, right = pl.ds(0, h), pl.ds(h, h)
    low, high = pl.ds(0, 2), pl.ds(2, 2)
    go(0, found.at[low, xf, :, left], a1h.at[0], along_x(xu))
    go(1, found.at[high, xf, :, left], a1h.at[1], along_x(xd))
    go(2, found.at[yf, low, :, right], b1h.at[0], along_y(yu))
    go(3, found.at[yf, high, :, right], b1h.at[1], along_y(yd))
    keep = trade_start(out_pages, in_pages, tsend, trecv, tlocal)
    own[ROWS:] = priors[...]
    came(0, a1h.at[0])
    a1s[0, :2] = found[:2, xu, :, :h] + a1h[0]
    a1s[0, 2:] = found[2:, xu, :, :h]
    go(4, a1s.at[0], a1f.at[0], along_x(xu))
    came(1, a1h.at[1])
    a1s[1, :2] = found[:2, xd, :, :h]
    a1s[1, 2:] = found[2:, xd, :, :h] + a1h[1]
    go(5, a1s.at[1], a1f.at[1], along_x(xd))
    came(2, b1h.at[0])
    b1s[0, :2] = found[yu, :2, :, h:] + b1h[0]
    b1s[0, 2:] = found[yu, 2:, :, h:]
    go(6, b1s.at[0], b1f.at[0], along_y(yu))
    came(3, b1h.at[1])
    b1s[1, :2] = found[yd, :2, :, h:]
    b1s[1, 2:] = found[yd, 2:, :, h:] + b1h[1]
    go(7, b1s.at[1], b1f.at[1], along_y(yd))
    m = ROWS // 2
    top, bottom = pl.ds(0, m), pl.ds(m, m)
    came(4, a1f.at[0])
    came(5, a1f.at[1])
    a2[...] = found[:, x, :, :h] + a1f[0] + a1f[1]
    go(8, a2.at[yf, top], a2h.at[0], along_y(yu))
    go(9, a2.at[yf, bottom], a2h.at[1], along_y(yd))
    came(6, b1f.at[0])
    came(7, b1f.at[1])
    b2[...] = found[y, :, :, h:] + b1f[0] + b1f[1]
    go(10, b2.at[xf, top], b2h.at[0], along_x(xu))
    go(11, b2.at[xf, bottom], b2h.at[1], along_x(xd))
    came(8, a2h.at[0])
    a2s[0, :m] = a2[yu, :m] + a2h[0]
    a2s[0, m:] = a2[yu, m:]
    go(12, a2s.at[0], a2f.at[0], along_y(yu))
    came(9, a2h.at[1])
    a2s[1, :m] = a2[yd, :m]
    a2s[1, m:] = a2[yd, m:] + a2h[1]
    go(13, a2s.at[1], a2f.at[1], along_y(yd))
    came(10, b2h.at[0])
    b2s[0, :m] = b2[xu, :m] + b2h[0]
    b2s[0, m:] = b2[xu, m:]
    go(14, b2s.at[0], b2f.at[0], along_x(xu))
    came(11, b2h.at[1])
    b2s[1, :m] = b2[xd, :m]
    b2s[1, m:] = b2[xd, m:] + b2h[1]
    go(15, b2s.at[1], b2f.at[1], along_x(xd))
    came(12, a2f.at[0])
    came(13, a2f.at[1])
    own[:ROWS, :h] = a2[y] + a2f[0] + a2f[1]
    came(14, b2f.at[0])
    came(15, b2f.at[1])
    own[:ROWS, h:] = b2[x] + b2f[0] + b2f[1]
    gather_grp(own, whole, gsend, grecv, glocal)
    for copy in started:
        copy.wait_send()
    trade_end(out_pages, in_pages, tsend, trecv, keep)


def embed_exchange(found, priors, out_pages):
    rows = ROWS + 2 * BRANCH
    h, m = WIDTH // 2, ROWS // 2
    return pl.pallas_call(
        embed_kernel,
        out_shape=(
            jax.ShapeDtypeStruct((rows, HIDDEN), BF16),
            jax.ShapeDtypeStruct((TOK, REQ, HIDDEN), BF16),
        ),
        in_specs=[VMEM, VMEM, ANY],
        out_specs=(ANY, ANY),
        scratch_shapes=[
            pltpu.VMEM((rows, WIDTH), BF16),
            pltpu.VMEM((2, 2, ROWS, h), BF16),
            pltpu.VMEM((2, 4, ROWS, h), BF16),
            pltpu.VMEM((2, 4, ROWS, h), BF16),
            pltpu.VMEM((2, 2, ROWS, h), BF16),
            pltpu.VMEM((2, 4, ROWS, h), BF16),
            pltpu.VMEM((2, 4, ROWS, h), BF16),
            pltpu.VMEM((4, ROWS, h), BF16),
            pltpu.VMEM((2, m, h), BF16),
            pltpu.VMEM((2, ROWS, h), BF16),
            pltpu.VMEM((2, ROWS, h), BF16),
            pltpu.VMEM((4, ROWS, h), BF16),
            pltpu.VMEM((2, m, h), BF16),
            pltpu.VMEM((2, ROWS, h), BF16),
            pltpu.VMEM((2, ROWS, h), BF16),
            pltpu.SemaphoreType.DMA((16,)),
            pltpu.SemaphoreType.DMA((16,)),
            pltpu.SemaphoreType.DMA((9,)),
            pltpu.SemaphoreType.DMA((9,)),
            pltpu.SemaphoreType.DMA,
            *TRADE_SEMAPHORES,
        ],
        compiler_params=pltpu.CompilerParams(
            collective_id=1, has_side_effects=True, vmem_limit_bytes=40 << 20
        ),
        cost_estimate=pl.CostEstimate(flops=0, transcendentals=0, bytes_accessed=100 << 20),
        name="embed_exchange",
    )(found, priors, out_pages)


def residual_kernel(part, base, out_pages, whole, own_out, in_pages, mated, sums, halves, full, rsend, rrecv, own, gsend, grecv, glocal, tsend, trecv, tlocal):
    greet(tok_peers() + grp_peers())
    keep = trade_start(out_pages, in_pages, tsend, trecv, tlocal)
    total = reduce_grp(part, mated, sums, halves, full, rsend, rrecv)
    own[...] = (base[...].astype(F32) + total).astype(BF16)
    own_out[...] = own[...]
    gather_grp(own, whole, gsend, grecv, glocal)
    trade_end(out_pages, in_pages, tsend, trecv, keep)


def residual_exchange(part, base, out_pages):
    return pl.pallas_call(
        residual_kernel,
        out_shape=(
            jax.ShapeDtypeStruct((ROWS, HIDDEN), BF16),
            jax.ShapeDtypeStruct((ROWS, WIDTH), BF16),
            jax.ShapeDtypeStruct((TOK, REQ, HIDDEN), BF16),
        ),
        in_specs=[VMEM, VMEM, ANY],
        out_specs=(ANY, VMEM, ANY),
        scratch_shapes=[
            *REDUCE_SCRATCH,
            pltpu.VMEM((ROWS, WIDTH), BF16),
            pltpu.SemaphoreType.DMA((9,)),
            pltpu.SemaphoreType.DMA((9,)),
            pltpu.SemaphoreType.DMA,
            *TRADE_SEMAPHORES,
        ],
        compiler_params=pltpu.CompilerParams(
            collective_id=2, has_side_effects=True, vmem_limit_bytes=40 << 20
        ),
        cost_estimate=pl.CostEstimate(flops=0, transcendentals=0, bytes_accessed=80 << 20),
        name="residual_exchange",
    )(part, base, out_pages)


def final_kernel(part, base, gate, out, mated, sums, halves, full, rsend, rrecv):
    greet(grp_peers())
    total = reduce_grp(part, mated, sums, halves, full, rsend, rrecv)
    out[...] = (base[...].astype(F32) + gate[...] * total).astype(BF16)


def final_exchange(part, base, gate):
    return pl.pallas_call(
        final_kernel,
        out_shape=jax.ShapeDtypeStruct((ROWS, WIDTH), BF16),
        in_specs=[VMEM, VMEM, VMEM],
        out_specs=VMEM,
        scratch_shapes=REDUCE_SCRATCH,
        compiler_params=pltpu.CompilerParams(
            collective_id=3, has_side_effects=True, vmem_limit_bytes=40 << 20
        ),
        cost_estimate=pl.CostEstimate(flops=0, transcendentals=0, bytes_accessed=40 << 20),
        name="final_exchange",
    )(part, base, gate)


def dot(a, b):
    return jnp.dot(a, b, preferred_element_type=F32)


def row_stats(rows_of, mean, scale):
    value = rows_of.astype(F32)
    middle = jnp.mean(value, axis=-1, keepdims=True)
    centered = value - middle
    spread = jnp.mean(centered * centered, axis=-1, keepdims=True)
    mean[...] = middle
    scale[...] = lax.rsqrt(spread + EPSILON)


def normed_and_step(block, prior, mean, scale, gain):
    normed = (block.astype(F32) - mean) * scale * gain
    row = lax.broadcasted_iota(jnp.int32, (ROWS, WIDTH), 0)
    spread = (
        lax.broadcasted_iota(jnp.int32, (ROWS, BRANCH), 0) // DRAFT
        == lax.broadcasted_iota(jnp.int32, (ROWS, BRANCH), 1)
    )
    carried = dot(spread.astype(BF16), prior)
    before = jnp.where(lax.rem(row, DRAFT) == 0, carried, pltpu.roll(normed, 1, axis=0))
    return normed, before - normed


def kept_row(normed, prior, kept_column):
    column = lax.broadcasted_iota(jnp.int32, (BRANCH, ROWS), 1)
    branch = lax.broadcasted_iota(jnp.int32, (BRANCH, ROWS), 0)
    pick = (column == branch * DRAFT + kept_column - 1) & (kept_column > 0)
    picked = dot(pick.astype(BF16), normed.astype(BF16))
    return jnp.where(kept_column > 0, picked, prior.astype(F32)).astype(BF16)


def head_ones(size):
    return (
        lax.broadcasted_iota(jnp.int32, (size, size), 0) // HEAD
        == lax.broadcasted_iota(jnp.int32, (size, size), 1) // HEAD
    ).astype(BF16)


def per_head(value):
    ones = head_ones(256)
    return jnp.concatenate([dot(value[:, :256], ones), dot(value[:, 256:], ones)], axis=1)


def per_head_fine(value):
    top = value.astype(BF16)
    rest = (value - top.astype(F32)).astype(BF16)
    return per_head(top) + per_head(rest)


def attention_kernel(
    place, request_of, winner, kept,
    xw, gain1, blend, weights, narrow, widen, baseline, boost, gain2, kept_column, pages,
    attended, chosen, shift,
    mean, scale, acc, low, r_s, k_s, v_s, w_s, y_s, p_s,
):
    step = pl.program_id(0)

    @pl.when(step == 0)
    def _():
        row_stats(xw[:ROWS], mean, scale)
        acc[...] = jnp.zeros_like(acc)
        low[...] = jnp.zeros_like(low)

    columns = pl.ds(pl.multiple_of(step * WIDTH, WIDTH), WIDTH)
    prior = xw[ROWS : ROWS + BRANCH, columns]
    normed, delta = normed_and_step(xw[:ROWS, columns], prior, mean[...], scale[...], gain1[0:1])

    @pl.when(step == place[0])
    def _():
        shift[...] = kept_row(normed, prior, kept_column[...])

    for c in range(4):
        acc[c] += dot((normed + delta * blend[c : c + 1]).astype(BF16), weights[c])
    low[...] += dot((normed + delta * blend[4:5]).astype(BF16), narrow[...])

    @pl.when(step == GRP - 1)
    def _():
        lowrank = jnp.tanh(low[...]).astype(BF16)
        w_s[...] = jnp.exp(-jnp.exp(baseline[...] + dot(lowrank, widen[...])))
        r_s[...] = acc[0]
        k_s[...] = acc[1]
        v_s[...] = acc[2]
        shape3 = (BRANCH, DRAFT, WIDTH)
        r3, k3 = r_s[...].reshape(shape3), k_s[...].reshape(shape3)
        v3, w3 = v_s[...].reshape(shape3), w_s[...].reshape(shape3)
        position = lax.broadcasted_iota(jnp.int32, shape3, 1)
        y_s[...] = per_head_fine(r_s[...] * boost[...] * k_s[...]) * v_s[...]
        p_s[...] = jnp.ones_like(p_s)
        for s in range(DRAFT - 2, -1, -1):
            decay = jnp.where(position > s + 1, p_s[...].reshape(shape3) * w3[:, s + 1 : s + 2], 1.0)
            p_s[...] = decay.reshape(ROWS, WIDTH)
            term = jnp.where(position > s, r3 * decay * k3[:, s : s + 1], 0.0)
            score = per_head(term.reshape(ROWS, WIDTH).astype(BF16)).reshape(shape3)
            y_s[...] += (score * v3[:, s : s + 1]).reshape(ROWS, WIDTH)
        decay = jnp.where(position > 0, p_s[...].reshape(shape3) * w3[:, 0:1], 1.0)
        p_s[...] = r_s[...] * decay.reshape(ROWS, WIDTH)
        for b in range(BRANCH):
            rows = pl.ds(b * DRAFT, DRAFT)
            for pair in range(PAIRS):
                lanes = pl.ds(pair * 128, 128)
                y_s[rows, lanes] += dot(p_s[rows, lanes].astype(BF16), pages[request_of[b], pair])
        y = y_s[...]
        centered = y - per_head_fine(y) * (1.0 / HEAD)
        spread = per_head_fine(centered * centered) * (1.0 / HEAD)
        gate = acc[3]
        gate = gate * jax.nn.sigmoid(gate)
        attended[...] = (centered * lax.rsqrt(spread + HEAD_EPSILON) * gain2[...] * gate).astype(BF16)
        eye = (
            lax.broadcasted_iota(jnp.int32, (128, 128), 0)
            == lax.broadcasted_iota(jnp.int32, (128, 128), 1)
        )
        spot = lax.broadcasted_iota(jnp.int32, (DRAFT, WIDTH), 0)
        for q in range(REQ):
            b = winner[q]
            count = kept[b]
            rows = pl.ds(pl.multiple_of(b * DRAFT, DRAFT), DRAFT)
            live = spot < count
            tail = jnp.where(live, w_s[rows], 1.0)
            for hop in (1, 2, 4, 8):
                later = pltpu.roll(tail, DRAFT - hop, axis=0)
                tail = tail * jnp.where(spot < DRAFT - hop, later, 1.0)
            after = jnp.where(spot < DRAFT - 1, pltpu.roll(tail, DRAFT - 1, axis=0), 1.0)
            keys = jnp.where(live, k_s[rows], 0.0) * after
            values = v_s[rows].astype(BF16)
            for pair in range(PAIRS):
                lanes = slice(pair * 128, pair * 128 + 128)
                fade = jnp.where(eye, tail[0:1, lanes], 0.0)
                left = jnp.concatenate([keys[:, lanes], fade], axis=0).astype(BF16)
                right = jnp.concatenate([values[:, lanes], pages[q, pair]], axis=0)
                chosen[q, pair] = lax.dot_general(
                    left, right, (((0,), (0,)), ((), ())), preferred_element_type=F32
                ).astype(BF16)


def attention(place, request_of, winner, kept, xw, scales, blends, weights, narrow, widen, baseline, boost, pages):
    rows = xw.shape[0]
    full = lambda *shape: pl.BlockSpec(shape, lambda k, *_: (0,) * len(shape))
    mine = pl.BlockSpec((1, WIDTH), lambda k, at, *_: (0, at[0]))
    return pl.pallas_call(
        attention_kernel,
        out_shape=(
            jax.ShapeDtypeStruct((ROWS, WIDTH), BF16),
            jax.ShapeDtypeStruct((REQ, PAIRS, 128, 128), BF16),
            jax.ShapeDtypeStruct((BRANCH, WIDTH), BF16),
        ),
        grid_spec=pltpu.PrefetchScalarGridSpec(
            num_scalar_prefetch=4,
            grid=(GRP,),
            in_specs=[
                full(rows, HIDDEN),
                pl.BlockSpec((3, WIDTH), lambda k, *_: (0, k)),
                pl.BlockSpec((7, WIDTH), lambda k, *_: (0, k)),
                pl.BlockSpec((4, WIDTH, WIDTH), lambda k, *_: (0, k, 0)),
                pl.BlockSpec((WIDTH, 128), lambda k, *_: (k, 0)),
                full(128, WIDTH),
                mine,
                mine,
                mine,
                full(BRANCH, 1),
                full(REQ, PAIRS, 128, 128),
            ],
            out_specs=(
                full(ROWS, WIDTH),
                full(REQ, PAIRS, 128, 128),
                full(BRANCH, WIDTH),
            ),
            scratch_shapes=[
                pltpu.VMEM((ROWS, 1), F32),
                pltpu.VMEM((ROWS, 1), F32),
                pltpu.VMEM((4, ROWS, WIDTH), F32),
                pltpu.VMEM((ROWS, 128), F32),
            ]
            + [pltpu.VMEM((ROWS, WIDTH), F32)] * 6,
        ),
        compiler_params=pltpu.CompilerParams(vmem_limit_bytes=52 << 20),
        cost_estimate=pl.CostEstimate(flops=6 << 30, transcendentals=1 << 20, bytes_accessed=24 << 20),
        name="attention",
    )(
        place, request_of, winner, kept,
        xw, scales, blends, weights, narrow, widen,
        baseline.reshape(1, HIDDEN), boost.reshape(1, HIDDEN), scales[2:3],
        kept.reshape(BRANCH, 1), pages,
    )


def feedforward_kernel(place, rw, prior_ref, gain, blend, keyed, content, kept_column, part, gate, shift, mean, scale, acc):
    step = pl.program_id(0)

    @pl.when(step == 0)
    def _():
        row_stats(rw[...], mean, scale)
        acc[...] = jnp.zeros_like(acc)

    columns = pl.ds(pl.multiple_of(step * WIDTH, WIDTH), WIDTH)
    prior = prior_ref[...]
    normed, delta = normed_and_step(rw[:, columns], prior, mean[...], scale[...], gain[1:2])

    @pl.when(step == place[0])
    def _():
        shift[...] = kept_row(normed, prior, kept_column[...])

    acc[:, :KEYS] += dot((normed + delta * blend[5:6]).astype(BF16), keyed[:, :KEYS])
    acc[:, KEYS:] += dot((normed + delta * blend[6:7]).astype(BF16), keyed[:, KEYS:])

    @pl.when(step == GRP - 1)
    def _():
        gate[...] = jax.nn.sigmoid(acc[:, KEYS:])
        hidden = jnp.square(jnp.maximum(acc[:, :KEYS], 0.0)).astype(BF16)
        for g in range(GRP):
            lanes = slice(g * WIDTH, g * WIDTH + WIDTH)
            part[:, lanes] = dot(hidden, content[:, lanes]).astype(BF16)


def feedforward(place, rw, prior, scales, blends, keyed, content, kept):
    full = lambda *shape: pl.BlockSpec(shape, lambda k, *_: (0,) * len(shape))
    return pl.pallas_call(
        feedforward_kernel,
        out_shape=(
            jax.ShapeDtypeStruct((ROWS, HIDDEN), BF16),
            jax.ShapeDtypeStruct((ROWS, WIDTH), F32),
            jax.ShapeDtypeStruct((BRANCH, WIDTH), BF16),
        ),
        grid_spec=pltpu.PrefetchScalarGridSpec(
            num_scalar_prefetch=1,
            grid=(GRP,),
            in_specs=[
                full(ROWS, HIDDEN),
                pl.BlockSpec((BRANCH, WIDTH), lambda k, *_: (0, k)),
                pl.BlockSpec((3, WIDTH), lambda k, *_: (0, k)),
                pl.BlockSpec((7, WIDTH), lambda k, *_: (0, k)),
                pl.BlockSpec((WIDTH, KEYS + WIDTH), lambda k, *_: (k, 0)),
                full(KEYS, HIDDEN),
                full(BRANCH, 1),
            ],
            out_specs=(full(ROWS, HIDDEN), full(ROWS, WIDTH), full(BRANCH, WIDTH)),
            scratch_shapes=[
                pltpu.VMEM((ROWS, 1), F32),
                pltpu.VMEM((ROWS, 1), F32),
                pltpu.VMEM((ROWS, KEYS + WIDTH), F32),
            ],
        ),
        compiler_params=pltpu.CompilerParams(vmem_limit_bytes=52 << 20),
        cost_estimate=pl.CostEstimate(flops=5 << 30, transcendentals=1 << 18, bytes_accessed=24 << 20),
        name="feedforward",
    )(place, rw, prior, scales, blends, keyed, content, kept.reshape(BRANCH, 1))


def body(
    guess_symbol_ids,
    symbol_vector_lookup,
    prior_attention_normed,
    prior_feedforward_normed,
    layernorm_scales,
    lagged_blend_ratios,
    attention_matrices,
    forgetting_baseline_vector,
    forgetting_narrow_matrix,
    forgetting_widen_matrix,
    diagonal_boost,
    attention_result_matrix,
    feedforward_lookup_matrix,
    feedforward_content_matrix,
    feedforward_gating_matrix,
    memory_matrix_store,
    query_memory_slot,
    candidate_tally_each_query,
    kept_guess_tally,
):
    tok_at = lax.axis_index("tok")
    grp_at = lax.axis_index("grp")
    place = grp_at.reshape(1)
    vocab_rows = symbol_vector_lookup.shape[0]
    slot_count = memory_matrix_store.shape[0]

    result_matrix = lax.all_gather(attention_result_matrix, "tok", axis=1, tiled=True)
    keyed = lax.all_gather(
        jnp.concatenate([feedforward_lookup_matrix, feedforward_gating_matrix], axis=1),
        "tok",
        axis=0,
        tiled=True,
    )
    content = lax.all_gather(feedforward_content_matrix, "tok", axis=1, tiled=True)

    wanted = guess_symbol_ids - tok_at * vocab_rows
    inside = (wanted >= 0) & (wanted < vocab_rows)
    found = jnp.take(symbol_vector_lookup, jnp.clip(wanted, 0, vocab_rows - 1), axis=0)
    found = jnp.where(inside[:, None], found, jnp.zeros((), BF16)).reshape(4, 4, ROWS, WIDTH)
    priors = jnp.concatenate([prior_attention_normed, prior_feedforward_normed], axis=0)

    owners = (query_memory_slot // slot_count).reshape(TOK, REQ)
    places = (query_memory_slot % slot_count).reshape(TOK, REQ)
    owned_here = owners == tok_at
    send_slot = jnp.sum(jnp.where(owned_here, places, 0), axis=1)
    sending = jnp.any(owned_here, axis=1)
    outgoing = jnp.where(
        sending[:, None, None], jnp.take(memory_matrix_store, send_slot, axis=0), 0.0
    ).astype(BF16)

    whole, incoming = embed_exchange(found, priors, outgoing)

    my_owners = lax.dynamic_index_in_dim(owners, tok_at, 0, keepdims=False)
    my_counts = lax.dynamic_index_in_dim(candidate_tally_each_query, tok_at, 0, keepdims=False)
    local_ids = jnp.arange(BRANCH, dtype=jnp.int32)
    request_ends = jnp.cumsum(my_counts)
    request_of = jnp.sum((request_ends[None, :] <= local_ids[:, None]).astype(jnp.int32), axis=1)
    branch_score = kept_guess_tally * BRANCH + (BRANCH - 1 - local_ids)
    member = request_of[None, :] == jnp.arange(REQ, dtype=jnp.int32)[:, None]
    best_score = jnp.max(jnp.where(member, branch_score[None, :], -1), axis=1)
    winner = BRANCH - 1 - best_score % BRANCH

    diagonal = (
        lax.broadcasted_iota(jnp.int32, (128, 128), 0) // HEAD
        == lax.broadcasted_iota(jnp.int32, (128, 128), 1) // HEAD
    )
    my_pages = jnp.take(incoming, my_owners, axis=0).reshape(REQ, PAIRS, 128, HEAD)
    pages = jnp.where(diagonal, jnp.concatenate([my_pages, my_pages], axis=-1), jnp.zeros((), BF16))

    attended, chosen, shift_att_out = attention(
        place, request_of, winner, kept_guess_tally,
        whole, layernorm_scales, lagged_blend_ratios, attention_matrices,
        forgetting_narrow_matrix, forgetting_widen_matrix,
        forgetting_baseline_vector, diagonal_boost, pages,
    )
    partial_att = dot(attended, result_matrix).astype(BF16)

    half = lax.broadcasted_iota(jnp.int32, (128, HEAD), 0) < HEAD
    new_pages = jnp.where(half, chosen[..., :HEAD], chosen[..., HEAD:]).reshape(REQ, REQ, HIDDEN)
    targets = my_owners[None, :] == jnp.arange(TOK, dtype=jnp.int32)[:, None]
    pick_index = jnp.sum(
        jnp.where(targets, jnp.arange(REQ, dtype=jnp.int32)[None, :], 0), axis=1
    )
    outgoing_back = jnp.take(new_pages, pick_index, axis=0)

    own_x = lax.dynamic_slice(whole, (0, grp_at * WIDTH), (ROWS, WIDTH))
    residual_whole, residual, returned = residual_exchange(partial_att, own_x, outgoing_back)

    partial_ffn, gate, shift_ffn_out = feedforward(
        place, residual_whole, whole[ROWS + BRANCH :], layernorm_scales, lagged_blend_ratios,
        keyed, content, kept_guess_tally,
    )
    layer_out = final_exchange(partial_ffn, residual, gate)

    hit = (send_slot[None, :] == jnp.arange(slot_count, dtype=jnp.int32)[:, None]) & sending[None, :]
    source = jnp.sum(jnp.where(hit, jnp.arange(TOK, dtype=jnp.int32)[None, :], 0), axis=1)
    store_out = jnp.where(
        jnp.any(hit, axis=1)[:, None, None],
        jnp.take(returned, source, axis=0).astype(F32),
        memory_matrix_store,
    )
    return (layer_out, shift_att_out, shift_ffn_out, store_out)


def solution(mesh):
    in_specs = (
        P(),
        P("tok", "grp"),
        P("tok", "grp"),
        P("tok", "grp"),
        P(),
        P(),
        P(None, None, "grp"),
        P(),
        P(),
        P(None, "grp"),
        P(),
        P("grp", "tok"),
        P("tok", "grp"),
        P("grp", "tok"),
        P("tok", "grp"),
        P("tok", "grp", None),
        P(),
        P(),
        P("tok"),
    )
    out_specs = (P("tok", "grp"), P("tok", "grp"), P("tok", "grp"), P("tok", "grp", None))
    return jax.shard_map(body, mesh=mesh, in_specs=in_specs, out_specs=out_specs, check_vma=False)
```

time: 836 us -> 311 us (0.37); the launches traced: 821 us -> 310 us
  waiting for transfers between devices: 307 us -> 84.2 us
  Pallas kernels: 0 us -> 162 us
  other arithmetic: 176 us -> 14.1 us
  matrix products: 135 us -> 3.62 us
  local copies, waits for them, and re-layouts: 136 us -> 31.8 us
  blocking collectives: 32.1 us -> 0 us
  loops' own time: 11 us -> 0 us
  starting transfers between devices: 10 us -> 0.11 us
    pallas_call x0 -> x5, Pallas kernels: none -> 162 us  [the longest x1 76.7 us: embed_exchange(): pl.pallas_call(embed_kernel, out_shape=(jax.ShapeDtypeStruct((rows, HIDDE...]
    reduce_scatter x3 -> x0, waiting for transfers between devices: 139 us -> none  [the longest x1 79.1 us: body(): lax.psum_scatter(jnp.where(inside[:, None], found.astype(jnp.float32), 0....]
    dot_general x24 -> x1, matrix products: 135 us -> 3.62 us  [dot(): return jnp.dot(a, b, preferred_element_type=F32)]
    select_n x25 -> x9, other arithmetic: 109 us -> 10.5 us  [the longest x1 3.59 us: body(): jnp.where(inside[:, None], found, jnp.zeros((), BF16))]
    all_gather x1, waiting for transfers between devices: 74.1 us -> 0.01 us  [body(): lax.all_gather(feedforward_content_matrix, 'tok', axis=1, tiled=True)]
    dynamic_slice x51 -> x1, local copies, waits for them, and re-layouts: 49.2 us -> 0.97 us  [body(): own_x = lax.dynamic_slice(whole, (0, grp_at * WIDTH), (ROWS, WIDTH))]
    all_gather x2 -> x0, blocking collectives: 32.1 us -> none  [the longest x1 16.4 us: body(): lax.all_gather(prior_feedforward_normed, 'grp', axis=1, tiled=True)]
    dot_general x4 -> x0, local copies, waits for them, and re-layouts: 28.5 us -> none  [project(): jnp.dot(mix_input(normed, before, lagged_blend_ratios[index]), weight, pr...]
  transfers between devices with their start and end apart: 11 -> 3, of which waited for: 8 -> 1; matrix products, arithmetic and copies ran while one was open for 49% -> 14% of each run, Pallas kernels for 0% -> 41%
where the time goes in v1:
time: 311 us; the launch traced here: 310 us
  Pallas kernels  162 us (52%)
  waiting for transfers between devices  84.2 us (27%)
  local copies, waits for them, and re-layouts  31.8 us (10%)
  other arithmetic  14.1 us (5%)
  between operations  14.1 us (5%)
  matrix products  3.62 us (1%)
    all_gather x1, waiting for transfers between devices, body(): lax.all_gather(jnp.concatenate([feedforward_lookup_matrix, feedforward_ga...  82.8 us
    pallas_call x1, Pallas kernels, embed_exchange(): pl.pallas_call(embed_kernel, out_shape=(jax.ShapeDtypeStruct((rows, HIDDE...  76.7 us
    pallas_call x1, Pallas kernels, residual_exchange(): pl.pallas_call(residual_kernel, out_shape=(jax.ShapeDtypeStruct((ROWS, HI...  31.2 us
    pallas_call x1, Pallas kernels, attention(): pl.pallas_call(attention_kernel, out_shape=(jax.ShapeDtypeStruct((ROWS, W...  19.8 us
    pallas_call x1, Pallas kernels, feedforward(): pl.pallas_call(feedforward_kernel, out_shape=(jax.ShapeDtypeStruct((ROWS,...  17.8 us
    gather x1, local copies, waits for them, and re-layouts, body(): jnp.take(symbol_vector_lookup, jnp.clip(wanted, 0, vocab_rows - 1), axis=0)  17.4 us
    pallas_call x1, Pallas kernels, final_exchange(): pl.pallas_call(final_kernel, out_shape=jax.ShapeDtypeStruct((ROWS, WIDTH)...  17 us
  transfers between devices with their start and end apart: 3, of which 1 were waited for; matrix products, arithmetic and copies ran while one was open for 14% of the time, Pallas kernels for 41%

profile of v1, /device:TPU:1, one launch (start us, length us, event | category | flops | bytes accessed | tf_op | source)
XLA Modules:
  0.0 310.5 jit_solution(2448724947721926359)
XLA Ops:
  7.2 0.0 all-gather.4.cloned.1.call-start
  7.2 0.7 all-gather.4.cloned.1.call-update
  7.9 0.0 all-gather.8.cloned.1.call-start
  8.0 0.7 all-gather.8.cloned.1.call-update
  8.7 0.0 all-gather.6.cloned.1.call-start
  8.7 2.0 pad_maximum_fusion
  10.8 0.0 all-gather.6.cloned.1.call-update
  10.8 0.1 reshape.171
  10.9 0.1 reshape.172
  11.1 0.1 select_reduce_fusion.1
  11.2 0.1 fusion.11
  11.3 0.1 select_reduce_fusion.2
  11.5 2.2 gather_fusion.1
  13.8 17.4 %gather_fusion = bf16[4096,512]{1,0:T(8,128)(2,1)} fusion(bf16[2048,512]{1,0:T(8,128)(2,1)S(1)} %copy-done, s32[4096]{0:T(1024)S(1)} %fusion), kind=kCustom, calls=%fused_computation | custom fusion | bytes 8404992 | tf_op jit(solution)/shard_map/jit(_take)/gather | solution.py:662
  31.2 3.6 %select_select_fusion.found = bf16[4,4,256,512]{3,2,1,0:T(8,128)(2,1)S(1)} fusion(bf16[4,4,256,512]{3,2,1,0:T(8,128)(2,1)} %bitcast.33, pred[4,4,256]{2,1,0:T(4,128)(4,1)S(1)} %broadcast_in_dim.155, pred[4,4,256]{2,1,0:T(4,128)(4,1)S(1)} %broadcast_in_dim.153), kind=kLoop, calls=%fused_computation.6 | loop fusion | flops 4194304 | bytes 8396800 | tf_op jit(solution)/shard_map/jit(_where)/select_n | solution.py:663
  34.8 0.4 select_convert_fusion.out_pages
  35.2 76.7 %embed_exchange.1 = (bf16[288,4096]{1,0:T(8,128)(2,1)S(1)}, bf16[16,8,4096]{2,1,0:T(8,128)(2,1)S(1)}) custom-call(bf16[4,4,256,512]{3,2,1,0:T(8,128)(2,1)S(1)} %select_select_fusion.found, bf16[32,512]{1,0:T(8,128)(2,1)S(1)} %pad_maximum_fusion.1.priors, bf16[16,8,4096]{2,1,0:T(8,128)(2,1)S(1)} %select_convert_fusion.out_pages), custom_call_target="tpu_custom_call" | custom-call | bytes 104857600 | tf_op jit(solution)/shard_map/embed_exchange/pallas_call | solution.py:279
  111.9 1.4 copy-done.6
  113.3 0.6 gather_fusion.2
  113.9 1.1 gather.28
  115.1 0.2 dynamic-slice_reduce_fusion
  115.3 0.2 reduce-window.8
  115.5 0.1 copy.27.kept_column
  115.6 0.9 slice.15.prior_ref
  116.5 0.1 convert_reduce_fusion.request_of
  116.6 0.1 select_reduce_fusion.3
  116.7 0.1 select_compare_fusion
  116.9 0.2 broadcast_select_fusion.1
  117.1 1.6 maximum_select_fusion.pages
  118.7 19.8 %attention.1 = (bf16[256,512]{1,0:T(8,128)(2,1)S(1)}, bf16[8,4,128,128]{3,2,1,0:T(8,128)(2,1)S(1)}, bf16[16,512]{1,0:T(8,128)(2,1)}) custom-call(s32[1]{0:T(128)} %bitcast.place, s32[16]{0:T(128)S(1)} %convert_reduce_fusion.request_of, s32[8]{0:T(128)S(1)} %fusion.3.winner, s32[16]{0:T(128)S(1)} %copy-done.7, bf16[288,4096]{1,0:T(8,128)(2,1)} %copy-done.6, ...), custom_call_target="tpu_custom_call" | custom-call | flops 6442450944 | bytes 25165824 | tf_op jit(solution)/shard_map/attention/pallas_call | solution.py:515
  138.5 0.4 slice_select_fusion
  138.9 0.8 reshape.176
  139.7 1.6 gather_fusion.3
  141.3 0.1 select_reduce_fusion
  141.4 0.1 fusion.2
  141.5 1.0 constant_dynamic-slice_fusion.base
  142.5 1.4 broadcast_select_fusion.out_pages
  143.9 0.0 all-gather.4.cloned.1.call-done
  144.0 3.6 %convolution_convert_fusion.part = bf16[256,4096]{1,0:T(8,128)(2,1)S(1)} fusion(bf16[256,512]{1,0:T(8,128)(2,1)S(1)} %get-tuple-element.17, bf16[512,4096]{1,0:T(8,128)(2,1)} %all-gather.4.cloned.1.call-done), kind=kOutput, calls=%fused_computation.5 | convolution fusion | flops 1074790400 | bytes 6553600 | tf_op jit(solution)/shard_map/dot_general | solution.py:376
  147.6 31.2 %residual_exchange.1 = (bf16[256,4096]{1,0:T(8,128)(2,1)S(1)}, bf16[256,512]{1,0:T(8,128)(2,1)S(1)}, bf16[16,8,4096]{2,1,0:T(8,128)(2,1)S(1)}) custom-call(bf16[256,4096]{1,0:T(8,128)(2,1)S(1)} %convolution_convert_fusion.part, bf16[256,512]{1,0:T(8,128)(2,1)S(1)} %constant_dynamic-slice_fusion.base, bf16[16,8,4096]{2,1,0:T(8,128)(2,1)S(1)} %broadcast_select_fusion.out_pages), custom_call_target="tpu_custom_call" | custom-call | bytes 83886080 | tf_op jit(solution)/shard_map/residual_exchange/pallas_call | solution.py:329
  178.8 1.3 copy-done.3
  180.1 0.6 gather_fusion.4
  180.7 3.3 %convert_select_fusion = f32[16,8,4096]{2,1,0:T(8,128)} fusion(f32[16,8,4096]{2,1,0:T(8,128)} %param.34, bf16[16,8,4096]{2,1,0:T(8,128)(2,1)S(1)} %gather_fusion.4, pred[16]{0:T(512)(128)(4,1)S(1)} %compare_and_fusion.2, pred[16]{0:T(512)(128)(4,1)S(1)} %fusion.2), kind=kLoop, calls=%fused_computation.7 | loop fusion | flops 1572864 | bytes 5242912 | tf_op jit(solution)/shard_map/jit(_where)/select_n | solution.py:721
  184.0 82.8 %all-gather.6.cloned.1.call-done.keyed = bf16[4096,1408]{1,0:T(8,128)(2,1)} async-done(((bf16[256,1408]{1,0:T(8,128)(2,1)}), bf16[4096,1408]{1,0:T(8,128)(2,1)}) %all-gather.6.cloned.1.call-update) | async-done | bytes 11534352 | tf_op jit(solution)/shard_map/all_gather | solution.py:652
  266.8 17.8 %feedforward.1 = (bf16[256,4096]{1,0:T(8,128)(2,1)}, f32[256,512]{1,0:T(8,128)S(1)}, bf16[16,512]{1,0:T(8,128)(2,1)}) custom-call(s32[1]{0:T(128)} %bitcast.place, bf16[256,4096]{1,0:T(8,128)(2,1)} %copy-done.3, bf16[16,4096]{1,0:T(8,128)(2,1)S(1)} %slice.15.prior_ref, f32[3,4096]{1,0:T(4,128)S(1)} %copy-done.5, f32[7,4096]{1,0:T(8,128)S(1)} %copy-done.4, ...), custom_call_target="tpu_custom_call" | custom-call | flops 5368709120 | bytes 25165824 | tf_op jit(solution)/shard_map/feedforward/pallas_call | solution.py:592
  284.6 1.6 copy-done.2
  286.2 17.0 %final_exchange.1 = bf16[256,512]{1,0:T(8,128)(2,1)S(1)} custom-call(bf16[256,4096]{1,0:T(8,128)(2,1)S(1)} %copy-done.2, bf16[256,512]{1,0:T(8,128)(2,1)S(1)} %get-tuple-element.21.base, f32[256,512]{1,0:T(8,128)S(1)} %get-tuple-element.22.gate), custom_call_target="tpu_custom_call" | custom-call | bytes 41943040 | tf_op jit(solution)/shard_map/final_exchange/pallas_call | solution.py:361
  303.2 0.7 copy.30
  (53 shorter events, 0.3 us)
Async XLA Ops:
  7.2 6.6 %copy-start = (bf16[2048,512]{1,0:T(8,128)(2,1)S(1)}, bf16[2048,512]{1,0:T(8,128)(2,1)}, u32[]{:S(2)}) copy-start(bf16[2048,512]{1,0:T(8,128)(2,1)} %param.20) | copy-start | bytes 6291460
  7.2 3.6 %copy-start.15 = (s32[128]{0:T(128)S(1)}, s32[128]{0:T(128)}, u32[]{:S(2)}) copy-start(s32[128]{0:T(128)} %param.35) | copy-start | bytes 1540
  7.2 3.8 %copy-start.11 = (s32[4096]{0:T(1024)S(1)}, s32[4096]{0:T(1024)}, u32[]{:S(2)}) copy-start(s32[4096]{0:T(1024)} %param.19) | copy-start | bytes 49156
  7.2 136.8 %all-gather.4.cloned.1.call-start = ((), (), s32[]{:S(2)}) async-start(), calls=%async_computation | async-start | bytes 4456448 | tf_op jit(solution)/shard_map/all_gather | solution.py:651
  7.9 176.1 %all-gather.8.cloned.1.call-start = ((), (), s32[]{:S(2)}) async-start(), calls=%async_computation.2 | async-start | bytes 7798784 | tf_op jit(solution)/shard_map/all_gather | solution.py:658
  8.7 258.1 %all-gather.6.cloned.1.call-start = ((), (), s32[]{:S(2)}) async-start(), calls=%async_computation.1 | async-start | bytes 12255232 | tf_op jit(solution)/shard_map/all_gather | solution.py:652
  13.7 17.4 %copy-start.12 = (bf16[16,512]{1,0:T(8,128)(2,1)S(1)}, bf16[16,512]{1,0:T(8,128)(2,1)}, u32[]{:S(2)}) copy-start(bf16[16,512]{1,0:T(8,128)(2,1)} %param.22) | copy-start | bytes 49156
  13.8 17.4 %copy-start.13 = (bf16[16,512]{1,0:T(8,128)(2,1)S(1)}, bf16[16,512]{1,0:T(8,128)(2,1)}, u32[]{:S(2)}) copy-start(bf16[16,512]{1,0:T(8,128)(2,1)} %param.21) | copy-start | bytes 49156
  111.9 1.4 copy-start.6
  113.3 1.8 copy-start.14
  113.3 2.1 copy-start.7
  113.3 2.2 copy-start.5
  116.9 1.8 copy-start.4
  116.9 1.8 copy-start.8
  116.9 1.8 copy-start.9
  116.9 1.8 copy-start.10
  178.8 1.3 copy-start.3
  266.8 37.1 %copy-start.1 = (bf16[2048,512]{1,0:T(8,128)(2,1)S(1)}, bf16[2048,512]{1,0:T(8,128)(2,1)}, u32[]{:S(2)}) copy-start(bf16[2048,512]{1,0:T(8,128)(2,1)} %param.20) | copy-start | bytes 6291460
  284.6 1.6 copy-start.2
Sparse Core Ops, SparseCore 0:
  10.2 84.9 all-gather.3
  97.3 80.2 all-gather.7
  179.7 87.0 all-gather.5

commit v2 on v1

--- a/solution.py
+++ b/solution.py
@@ -18,6 +18,7 @@
 REQ = 8
 PAIRS = 4
 KEYS = 896
+SPACE = 48
 EPSILON = 1e-05
 HEAD_EPSILON = 0.00064
 F32 = jnp.float32
@@ -58,7 +59,13 @@
     return g + 1 - 2 * lax.rem(g, 2)
 
 
-def gather_grp(own, out, send, recv, local):
+def gather_grp(own, out, send, recv, local, between=()):
+    between = list(between)
+
+    def aside():
+        if between:
+            between.pop(0)()
+
     rows = out.shape[0]
     half = rows // 2
     g, up, down, far, mate = grp_places()
@@ -79,12 +86,14 @@
     go(0, own, whole, g, up)
     go(1, own, whole, g, down)
     go(2, own, whole, g, mate)
+    aside()
     came(0, whole, down)
     go(3, at(first, down), first, down, up)
     go(5, at(whole, down), whole, down, mate)
     came(1, whole, up)
     go(4, at(last, up), last, up, down)
     go(6, at(whole, up), whole, up, mate)
+    aside()
     came(3, first, far)
     go(7, at(first, far), first, far, mate)
     came(4, last, far)
@@ -94,12 +103,14 @@
     came(6, whole, flip(up))
     came(7, first, flip(far))
     came(8, last, flip(far))
+    while between:
+        aside()
     keep.wait()
     for copy in started:
         copy.wait_send()
 
 
-def reduce_grp(part, mated, sums, halves, full, send, recv):
+def reduce_grp(part, mated, sums, halves, full, send, recv, meanwhile=lambda: None):
     g, up, down, far, mate = grp_places()
     half = ROWS // 2
     started = []
@@ -133,6 +144,7 @@
     sums[2, :half] = own(2)[:half].astype(BF16)
     sums[2, half:] = (own(2)[half:] + halves[1].astype(F32)).astype(BF16)
     go(7, sums.at[2], full.at[1], down)
+    meanwhile()
     came(3, mated.at[3])
     came(6, full.at[0])
     came(7, full.at[1])
@@ -152,6 +164,81 @@
 ]
 
 
+def gather_tok(own, out, first_rows, last_rows, send, recv, local):
+    t = lax.axis_index("tok")
+    y, x = t // 4, lax.rem(t, 4)
+    xu, xd, xf = [lax.rem(x + k, 4) for k in (1, 3, 2)]
+    yu, yd, yf = [lax.rem(y + k, 4) for k in (1, 3, 2)]
+    along_x = lambda x_of: {"tok": y * 4 + x_of}
+    along_y = lambda y_of: {"tok": y_of * 4 + x}
+    cols = lambda x_of: pl.ds(pl.multiple_of(x_of * 256, 256), 256)
+    one = lambda rows, y_of, x_of: out.at[y_of, rows, cols(x_of)]
+    wide = lambda rows, y_of: out.at[y_of, rows]
+    tall = lambda rows, x_of: out.at[:, rows, cols(x_of)]
+    f0, f1 = first_rows, last_rows
+    fa, fb = [pl.ds(f0.start + k * (f0.size // 2), f0.size // 2) for k in (0, 1)]
+    la, lb = [pl.ds(f1.start + k * (f1.size // 2), f1.size // 2) for k in (0, 1)]
+    started = []
+
+    def go(index, src, dst, target):
+        copy = remote(src, dst, send.at[index], recv.at[index], target)
+        copy.start()
+        started.append(copy)
+
+    def came(index, dst):
+        remote(dst, dst, send.at[index], recv.at[index], along_x(xu)).wait_recv()
+
+    keep = pltpu.make_async_copy(own, one(pl.ds(0, own.shape[0]), y, x), local)
+
+    def begin():
+        keep.start()
+        go(0, own.at[f0], one(f0, y, x), along_x(xu))
+        go(1, own.at[f0], one(f0, y, x), along_x(xd))
+        go(2, own.at[f1], one(f1, y, x), along_y(yu))
+        go(3, own.at[f1], one(f1, y, x), along_y(yd))
+
+    def relay():
+        came(0, one(f0, y, xd))
+        go(4, one(fa, y, xd), one(fa, y, xd), along_x(xu))
+        came(2, one(f1, yd, x))
+        go(6, one(la, yd, x), one(la, yd, x), along_y(yu))
+        came(1, one(f0, y, xu))
+        go(5, one(fb, y, xu), one(fb, y, xu), along_x(xd))
+        came(3, one(f1, yu, x))
+        go(7, one(lb, yu, x), one(lb, yu, x), along_y(yd))
+
+    def turn():
+        keep.wait()
+        came(4, one(fa, y, xf))
+        came(5, one(fb, y, xf))
+        go(8, wide(f0, y), wide(f0, y), along_y(yu))
+        go(9, wide(f0, y), wide(f0, y), along_y(yd))
+        came(6, one(la, yf, x))
+        came(7, one(lb, yf, x))
+        go(10, tall(f1, x), tall(f1, x), along_x(xu))
+        go(11, tall(f1, x), tall(f1, x), along_x(xd))
+
+    def last():
+        came(8, wide(f0, yd))
+        go(12, wide(fa, yd), wide(fa, yd), along_y(yu))
+        came(10, tall(f1, xd))
+        go(14, tall(la, xd), tall(la, xd), along_x(xu))
+        came(9, wide(f0, yu))
+        go(13, wide(fb, yu), wide(fb, yu), along_y(yd))
+        came(11, tall(f1, xu))
+        go(15, tall(lb, xu), tall(lb, xu), along_x(xd))
+
+    def end():
+        came(12, wide(fa, yf))
+        came(13, wide(fb, yf))
+        came(14, tall(la, xf))
+        came(15, tall(lb, xf))
+        for copy in started:
+            copy.wait_send()
+
+    return begin, relay, turn, last, end
+
+
 def grp_peers():
     _, up, down, _, mate = grp_places()
     return [{"grp": up}, {"grp": down}, {"grp": mate}]
@@ -160,6 +247,48 @@
 def tok_peers():
     t = lax.axis_index("tok")
     return [{"tok": lax.rem(t + k, TOK)} for k in range(1, TOK)]
+
+
+def page_masks():
+    even = lax.rem(lax.broadcasted_iota(jnp.int32, (8, 128), 0), 2) == 0
+    left = lax.broadcasted_iota(jnp.int32, (8, 128), 1) < HEAD
+    return even, left
+
+
+def pair_page(page, put):
+    even, left = page_masks()
+    for block in range(4):
+        rows = [[] for _ in range(PAIRS)]
+        for group in (2 * block, 2 * block + 1):
+            pieces = []
+            for m in range(4 * group, 4 * group + 4):
+                here = page[:, m * 128 : m * 128 + 128]
+                swapped = pltpu.roll(here, HEAD, axis=1)
+                pieces += [jnp.where(even, here, swapped), jnp.where(even, swapped, here)]
+            turned = jnp.swapaxes(jnp.stack(pieces), 0, 1)
+            for pair in range(PAIRS):
+                rows[pair].append(jnp.where(left, turned[2 * pair], turned[2 * pair + 1]))
+        for pair in range(PAIRS):
+            put(pair, 16 * block, jnp.concatenate(rows[pair], axis=0))
+
+
+def flat_page(page, put):
+    even, left = page_masks()
+    for group in range(8):
+        rows = [page[pair, 8 * group : 8 * group + 8] for pair in range(PAIRS)]
+        turned = jnp.swapaxes(jnp.stack([rows[h // 2] for h in range(8)]), 0, 1)
+        for m in range(4):
+            first, second = turned[2 * m], turned[2 * m + 1]
+            swapped_first = pltpu.roll(first, HEAD, axis=1)
+            swapped_second = pltpu.roll(second, HEAD, axis=1)
+            put(
+                (4 * group + m) * 128,
+                jnp.where(
+                    left,
+                    jnp.where(even, first, swapped_first),
+                    jnp.where(even, swapped_second, second),
+                ),
+            )
 
 
 def trade_start(out_pages, in_pages, send, recv, local):
@@ -190,14 +319,13 @@
 ]
 
 
-def embed_kernel(found, priors, out_pages, whole, in_pages, own, a1h, a1s, a1f, b1h, b1s, b1f, a2, a2h, a2s, a2f, b2, b2h, b2s, b2f, xsend, xrecv, gsend, grecv, glocal, tsend, trecv, tlocal):
+def dense_rows(found, own, begin, a1h, a1s, a1f, b1h, b1s, b1f, a2, a2h, a2s, a2f, b2, b2h, b2s, b2f, xsend, xrecv):
     t = lax.axis_index("tok")
     y, x = t // 4, lax.rem(t, 4)
     xu, xd, xf = [lax.rem(x + k, 4) for k in (1, 3, 2)]
     yu, yd, yf = [lax.rem(y + k, 4) for k in (1, 3, 2)]
     along_x = lambda x_of: {"tok": y * 4 + x_of}
     along_y = lambda y_of: {"tok": y_of * 4 + x}
-    greet(tok_peers() + grp_peers())
     started = []
 
     def go(index, src, dst, target):
@@ -215,8 +343,7 @@
     go(1, found.at[high, xf, :, left], a1h.at[1], along_x(xd))
     go(2, found.at[yf, low, :, right], b1h.at[0], along_y(yu))
     go(3, found.at[yf, high, :, right], b1h.at[1], along_y(yd))
-    keep = trade_start(out_pages, in_pages, tsend, trecv, tlocal)
-    own[ROWS:] = priors[...]
+    begin()
     came(0, a1h.at[0])
     a1s[0, :2] = found[:2, xu, :, :h] + a1h[0]
     a1s[0, 2:] = found[2:, xu, :, :h]
@@ -267,25 +394,73 @@
     came(14, b2f.at[0])
     came(15, b2f.at[1])
     own[:ROWS, h:] = b2[x] + b2f[0] + b2f[1]
-    gather_grp(own, whole, gsend, grecv, glocal)
     for copy in started:
         copy.wait_send()
-    trade_end(out_pages, in_pages, tsend, trecv, keep)
-
-
-def embed_exchange(found, priors, out_pages):
+
+
+def sparse_rows(packed, spot, own, begin, parcels, psend, precv, plocal):
+    t = lax.axis_index("tok")
+    keep = pltpu.make_async_copy(packed.at[t], parcels.at[t], plocal)
+    keep.start()
+    copies = []
+    for k in range(1, TOK):
+        peer = lax.rem(t + k, TOK)
+        copy = remote(packed.at[peer], parcels.at[t], psend.at[k - 1], precv.at[k - 1], {"tok": peer})
+        copy.start()
+        copies.append(copy)
+    begin()
+    slots = lax.broadcasted_iota(jnp.int32, (ROWS, TOK * SPACE), 1)
+    pick = (slots == spot[...]).astype(BF16)
+    keep.wait()
+    for k in range(1, TOK):
+        origin = lax.rem(t + TOK - k, TOK)
+        remote(packed.at[t], parcels.at[origin], psend.at[k - 1], precv.at[k - 1], {"tok": origin}).wait_recv()
+    own[:ROWS] = dot(pick, parcels[...].reshape(TOK * SPACE, WIDTH)).astype(BF16)
+    for copy in copies:
+        copy.wait_send()
+
+
+def embed_kernel(sparse, count, *refs):
+    slots, store, *refs = refs
+    inputs, refs = refs[:count], refs[count:]
+    priors, result, whole, in_pages, results, own, gsend, grecv, glocal, out_pages, tsend, trecv, tlocal, wsend, wrecv, wlocal, *rest = refs
+    greet(tok_peers() + grp_peers())
+    steps = gather_tok(result, results, pl.ds(0, 256), pl.ds(256, 256), wsend, wrecv, wlocal)
+    keeps = []
+
+    def begin():
+        steps[0]()
+        own[ROWS:] = priors[...]
+
+        @pl.loop(0, TOK)
+        def _(peer):
+            page = store[slots[peer]]
+
+            def put(pair, row, value):
+                out_pages[peer, pair, pl.ds(row, 16)] = value.astype(BF16)
+
+            pair_page(page, put)
+
+        keeps.append(trade_start(out_pages, in_pages, tsend, trecv, tlocal))
+
+    (sparse_rows if sparse else dense_rows)(*inputs, own, begin, *rest)
+    gather_grp(own, whole, gsend, grecv, glocal, steps[1:4])
+    steps[4]()
+    trade_end(out_pages, in_pages, tsend, trecv, keeps[0])
+
+
+def embed_exchange(sparse, slots, store, inputs, priors, result):
     rows = ROWS + 2 * BRANCH
     h, m = WIDTH // 2, ROWS // 2
-    return pl.pallas_call(
-        embed_kernel,
-        out_shape=(
-            jax.ShapeDtypeStruct((rows, HIDDEN), BF16),
-            jax.ShapeDtypeStruct((TOK, REQ, HIDDEN), BF16),
-        ),
-        in_specs=[VMEM, VMEM, ANY],
-        out_specs=(ANY, ANY),
-        scratch_shapes=[
-            pltpu.VMEM((rows, WIDTH), BF16),
+    if sparse:
+        scratch = [
+            pltpu.VMEM((TOK, SPACE, WIDTH), BF16),
+            pltpu.SemaphoreType.DMA((TOK - 1,)),
+            pltpu.SemaphoreType.DMA((TOK - 1,)),
+            pltpu.SemaphoreType.DMA,
+        ]
+    else:
+        scratch = [
             pltpu.VMEM((2, 2, ROWS, h), BF16),
             pltpu.VMEM((2, 4, ROWS, h), BF16),
             pltpu.VMEM((2, 4, ROWS, h), BF16),
@@ -302,17 +477,100 @@
             pltpu.VMEM((2, ROWS, h), BF16),
             pltpu.SemaphoreType.DMA((16,)),
             pltpu.SemaphoreType.DMA((16,)),
+        ]
+    return pl.pallas_call(
+        functools.partial(embed_kernel, sparse, len(inputs)),
+        out_shape=(
+            jax.ShapeDtypeStruct((rows, HIDDEN), BF16),
+            jax.ShapeDtypeStruct((TOK, PAIRS, HEAD, 128), BF16),
+            jax.ShapeDtypeStruct((4, WIDTH, 1024), BF16),
+        ),
+        in_specs=[pl.BlockSpec(memory_space=pltpu.SMEM)] + [VMEM] * (len(inputs) + 2) + [ANY],
+        out_specs=(ANY, ANY, ANY),
+        scratch_shapes=[
+            pltpu.VMEM((rows, WIDTH), BF16),
             pltpu.SemaphoreType.DMA((9,)),
             pltpu.SemaphoreType.DMA((9,)),
             pltpu.SemaphoreType.DMA,
+            pltpu.VMEM((TOK, PAIRS, HEAD, 128), BF16),
             *TRADE_SEMAPHORES,
+            pltpu.SemaphoreType.DMA((16,)),
+            pltpu.SemaphoreType.DMA((16,)),
+            pltpu.SemaphoreType.DMA,
+            *scratch,
         ],
         compiler_params=pltpu.CompilerParams(
-            collective_id=1, has_side_effects=True, vmem_limit_bytes=40 << 20
+            collective_id=1 if sparse else 4, has_side_effects=True, vmem_limit_bytes=40 << 20
         ),
         cost_estimate=pl.CostEstimate(flops=0, transcendentals=0, bytes_accessed=100 << 20),
-        name="embed_exchange",
-    )(found, priors, out_pages)
+        name="embed_sparse" if sparse else "embed_dense",
+    )(slots, store, *inputs, priors, result)
+
+
+def pack_kernel(place, ids, table, packed, spot, most, slot_s):
+    t_at = place[0]
+    shape = (ROWS, ROWS)
+    sub = lax.broadcasted_iota(jnp.int32, shape, 0)
+    lane = lax.broadcasted_iota(jnp.int32, shape, 1)
+    vocab_rows = table.shape[0]
+    base = t_at * vocab_rows
+
+    def column(row):
+        return jnp.sum(jnp.where(sub == lane, jnp.broadcast_to(row, shape), 0), axis=1, keepdims=True)
+
+    def ranks(row):
+        col = column(row)
+        same = col == row
+        first_col = 1 - jnp.max(jnp.where(same & (lane < sub), 1, 0), axis=1, keepdims=True)
+        first_row = 1 - jnp.max(jnp.where(same & (sub < lane), 1, 0), axis=0, keepdims=True)
+        start = row - lax.rem(row, vocab_rows)
+        ahead = (col < row) & (col >= start)
+        rank = jnp.sum(jnp.where(ahead, first_col, 0), axis=0, keepdims=True)
+        return first_row, start, rank
+
+    def one(t, top):
+        row = ids[pl.ds(t, 1), :]
+        first_row, start, rank = ranks(row)
+        mine = (first_row > 0) & (start == base)
+        slot = lax.broadcasted_iota(jnp.int32, (SPACE, ROWS), 0)
+        hit = (slot == rank) & mine
+        slot_s[pl.ds(pl.multiple_of(t * SPACE, SPACE), SPACE)] = (
+            jnp.sum(jnp.where(hit, row - base + 1, 0), axis=1, keepdims=True) - 1
+        )
+
+        @pl.when(t == t_at)
+        def _():
+            owner = start // vocab_rows
+            spot[...] = column(owner * SPACE + rank)
+
+        return jnp.maximum(top, rank)
+
+    top = lax.fori_loop(0, TOK, one, jnp.zeros((1, ROWS), jnp.int32))
+    most[...] = jnp.broadcast_to(jnp.max(top, axis=1, keepdims=True) + 1, (8, 128))
+    step = 256
+    for k in range(TOK * SPACE // step):
+        rows = pl.ds(k * step, step)
+        pick = (
+            lax.broadcasted_iota(jnp.int32, (step, vocab_rows), 1) == slot_s[rows]
+        ).astype(BF16)
+        packed[rows] = dot(pick, table[...]).astype(BF16)
+
+
+def pack(place, ids, table):
+    return pl.pallas_call(
+        pack_kernel,
+        out_shape=(
+            jax.ShapeDtypeStruct((TOK * SPACE, WIDTH), BF16),
+            jax.ShapeDtypeStruct((ROWS, 1), jnp.int32),
+            jax.ShapeDtypeStruct((8, 128), jnp.int32),
+        ),
+        in_specs=[pl.BlockSpec(memory_space=pltpu.SMEM), VMEM, VMEM],
+        out_specs=(VMEM, VMEM, VMEM),
+        scratch_shapes=[pltpu.VMEM((TOK * SPACE, 1), jnp.int32)],
+        compiler_params=pltpu.CompilerParams(vmem_limit_bytes=32 << 20),
+        cost_estimate=pl.CostEstimate(flops=2 << 30, transcendentals=0, bytes_accessed=4 << 20),
+        name="pack",
+    )(place, ids, table)
 
 
 def residual_kernel(part, base, out_pages, whole, own_out, in_pages, mated, sums, halves, full, rsend, rrecv, own, gsend, grecv, glocal, tsend, trecv, tlocal):
@@ -331,7 +589,7 @@
         out_shape=(
             jax.ShapeDtypeStruct((ROWS, HIDDEN), BF16),
             jax.ShapeDtypeStruct((ROWS, WIDTH), BF16),
-            jax.ShapeDtypeStruct((TOK, REQ, HIDDEN), BF16),
+            jax.ShapeDtypeStruct((TOK, PAIRS, HEAD, 128), BF16),
         ),
         in_specs=[VMEM, VMEM, ANY],
         out_specs=(ANY, VMEM, ANY),
@@ -351,25 +609,42 @@
     )(part, base, out_pages)
 
 
-def final_kernel(part, base, gate, out, mated, sums, halves, full, rsend, rrecv):
+def final_kernel(source, hit, part, base, gate, returned, store, out, store_out, mated, sums, halves, full, rsend, rrecv):
     greet(grp_peers())
-    total = reduce_grp(part, mated, sums, halves, full, rsend, rrecv)
+
+    def pages():
+        @pl.loop(0, TOK)
+        def _(slot):
+            page = returned[source[slot]].astype(F32)
+            taken = hit[slot] > 0
+
+            def put(column, value):
+                columns = pl.ds(column, 128)
+                store_out[slot, :, columns] = jnp.where(taken, value, store[slot, :, columns])
+
+            flat_page(page, put)
+
+    total = reduce_grp(part, mated, sums, halves, full, rsend, rrecv, pages)
     out[...] = (base[...].astype(F32) + gate[...] * total).astype(BF16)
 
 
-def final_exchange(part, base, gate):
+def final_exchange(source, hit, part, base, gate, returned, store):
+    smem = pl.BlockSpec(memory_space=pltpu.SMEM)
     return pl.pallas_call(
         final_kernel,
-        out_shape=jax.ShapeDtypeStruct((ROWS, WIDTH), BF16),
-        in_specs=[VMEM, VMEM, VMEM],
-        out_specs=VMEM,
+        out_shape=(
+            jax.ShapeDtypeStruct((ROWS, WIDTH), BF16),
+            jax.ShapeDtypeStruct(store.shape, F32),
+        ),
+        in_specs=[smem, smem, VMEM, VMEM, VMEM, VMEM, VMEM],
+        out_specs=(VMEM, VMEM),
         scratch_shapes=REDUCE_SCRATCH,
         compiler_params=pltpu.CompilerParams(
             collective_id=3, has_side_effects=True, vmem_limit_bytes=40 << 20
         ),
         cost_estimate=pl.CostEstimate(flops=0, transcendentals=0, bytes_accessed=40 << 20),
         name="final_exchange",
-    )(part, base, gate)
+    )(source, hit, part, base, gate, returned, store)
 
 
 def dot(a, b):
@@ -423,16 +698,25 @@
     return per_head(top) + per_head(rest)
 
 
+def two_heads(page):
+    side = lax.broadcasted_iota(jnp.int32, (HEAD, 128), 1) < HEAD
+    none = jnp.zeros_like(page)
+    return jnp.concatenate([jnp.where(side, page, none), jnp.where(side, none, page)], axis=0)
+
+
 def attention_kernel(
-    place, request_of, winner, kept,
-    xw, gain1, blend, weights, narrow, widen, baseline, boost, gain2, kept_column, pages,
-    attended, chosen, shift,
-    mean, scale, acc, low, r_s, k_s, v_s, w_s, y_s, p_s,
+    place, owner_of, request_of, winner, kept,
+    xw, gain1, blend, weights, narrow, widen, baseline, boost, gain2, kept_column, pages, results,
+    part, chosen, shift,
+    result_s, result_sem, mean, scale, acc, low, r_s, k_s, v_s, w_s, y_s, p_s,
 ):
     step = pl.program_id(0)
 
+    fetch = pltpu.make_async_copy(results, result_s, result_sem)
+
     @pl.when(step == 0)
     def _():
+        fetch.start()
         row_stats(xw[:ROWS], mean, scale)
         acc[...] = jnp.zeros_like(acc)
         low[...] = jnp.zeros_like(low)
@@ -474,13 +758,16 @@
             rows = pl.ds(b * DRAFT, DRAFT)
             for pair in range(PAIRS):
                 lanes = pl.ds(pair * 128, 128)
-                y_s[rows, lanes] += dot(p_s[rows, lanes].astype(BF16), pages[request_of[b], pair])
+                y_s[rows, lanes] += dot(p_s[rows, lanes].astype(BF16), two_heads(pages[owner_of[request_of[b]], pair]))
         y = y_s[...]
         centered = y - per_head_fine(y) * (1.0 / HEAD)
         spread = per_head_fine(centered * centered) * (1.0 / HEAD)
         gate = acc[3]
         gate = gate * jax.nn.sigmoid(gate)
-        attended[...] = (centered * lax.rsqrt(spread + HEAD_EPSILON) * gain2[...] * gate).astype(BF16)
+        attended = (centered * lax.rsqrt(spread + HEAD_EPSILON) * gain2[...] * gate).astype(BF16)
+        fetch.wait()
+        for y_of in range(4):
+            part[:, y_of * 1024 : y_of * 1024 + 1024] = dot(attended, result_s[y_of]).astype(BF16)
         eye = (
             lax.broadcasted_iota(jnp.int32, (128, 128), 0)
             == lax.broadcasted_iota(jnp.int32, (128, 128), 1)
@@ -502,25 +789,27 @@
                 lanes = slice(pair * 128, pair * 128 + 128)
                 fade = jnp.where(eye, tail[0:1, lanes], 0.0)
                 left = jnp.concatenate([keys[:, lanes], fade], axis=0).astype(BF16)
-                right = jnp.concatenate([values[:, lanes], pages[q, pair]], axis=0)
-                chosen[q, pair] = lax.dot_general(
+                right = jnp.concatenate([values[:, lanes], two_heads(pages[owner_of[q], pair])], axis=0)
+                both = lax.dot_general(
                     left, right, (((0,), (0,)), ((), ())), preferred_element_type=F32
-                ).astype(BF16)
-
-
-def attention(place, request_of, winner, kept, xw, scales, blends, weights, narrow, widen, baseline, boost, pages):
+                )
+                side = lax.broadcasted_iota(jnp.int32, (HEAD, 128), 1) < HEAD
+                chosen[q, pair] = jnp.where(side, both[:HEAD], both[HEAD:]).astype(BF16)
+
+
+def attention(place, owner_of, request_of, winner, kept, xw, scales, blends, weights, narrow, widen, baseline, boost, pages, results):
     rows = xw.shape[0]
     full = lambda *shape: pl.BlockSpec(shape, lambda k, *_: (0,) * len(shape))
     mine = pl.BlockSpec((1, WIDTH), lambda k, at, *_: (0, at[0]))
     return pl.pallas_call(
         attention_kernel,
         out_shape=(
-            jax.ShapeDtypeStruct((ROWS, WIDTH), BF16),
-            jax.ShapeDtypeStruct((REQ, PAIRS, 128, 128), BF16),
+            jax.ShapeDtypeStruct((ROWS, HIDDEN), BF16),
+            jax.ShapeDtypeStruct((REQ, PAIRS, HEAD, 128), BF16),
             jax.ShapeDtypeStruct((BRANCH, WIDTH), BF16),
         ),
         grid_spec=pltpu.PrefetchScalarGridSpec(
-            num_scalar_prefetch=4,
+            num_scalar_prefetch=5,
             grid=(GRP,),
             in_specs=[
                 full(rows, HIDDEN),
@@ -533,14 +822,17 @@
                 mine,
                 mine,
                 full(BRANCH, 1),
-                full(REQ, PAIRS, 128, 128),
+                full(TOK, PAIRS, HEAD, 128),
+                ANY,
             ],
             out_specs=(
-                full(ROWS, WIDTH),
-                full(REQ, PAIRS, 128, 128),
+                full(ROWS, HIDDEN),
+                full(REQ, PAIRS, HEAD, 128),
                 full(BRANCH, WIDTH),
             ),
             scratch_shapes=[
+                pltpu.VMEM((4, WIDTH, 1024), BF16),
+                pltpu.SemaphoreType.DMA,
                 pltpu.VMEM((ROWS, 1), F32),
                 pltpu.VMEM((ROWS, 1), F32),
                 pltpu.VMEM((4, ROWS, WIDTH), F32),
@@ -552,14 +844,14 @@
         cost_estimate=pl.CostEstimate(flops=6 << 30, transcendentals=1 << 20, bytes_accessed=24 << 20),
         name="attention",
     )(
-        place, request_of, winner, kept,
+        place, owner_of, request_of, winner, kept,
         xw, scales, blends, weights, narrow, widen,
         baseline.reshape(1, HIDDEN), boost.reshape(1, HIDDEN), scales[2:3],
-        kept.reshape(BRANCH, 1), pages,
+        kept.reshape(BRANCH, 1), pages, results,
     )
 
 
-def feedforward_kernel(place, rw, prior_ref, gain, blend, keyed, content, kept_column, part, gate, shift, mean, scale, acc):
+def feedforward_kernel(place, rw, prior_ref, gain, blend, weights, kept_column, part, gate, shift, mean, scale, acc, content):
     step = pl.program_id(0)
 
     @pl.when(step == 0)
@@ -575,8 +867,9 @@
     def _():
         shift[...] = kept_row(normed, prior, kept_column[...])
 
-    acc[:, :KEYS] += dot((normed + delta * blend[5:6]).astype(BF16), keyed[:, :KEYS])
-    acc[:, KEYS:] += dot((normed + delta * blend[6:7]).astype(BF16), keyed[:, KEYS:])
+    acc[:, :KEYS] += dot((normed + delta * blend[5:6]).astype(BF16), weights[:, KEYS : 2 * KEYS])
+    acc[:, KEYS:] += dot((normed + delta * blend[6:7]).astype(BF16), weights[:, 2 * KEYS :])
+    content[columns] = weights[:, :KEYS]
 
     @pl.when(step == GRP - 1)
     def _():
@@ -584,10 +877,12 @@
         hidden = jnp.square(jnp.maximum(acc[:, :KEYS], 0.0)).astype(BF16)
         for g in range(GRP):
             lanes = slice(g * WIDTH, g * WIDTH + WIDTH)
-            part[:, lanes] = dot(hidden, content[:, lanes]).astype(BF16)
-
-
-def feedforward(place, rw, prior, scales, blends, keyed, content, kept):
+            part[:, lanes] = lax.dot_general(
+                hidden, content[lanes], (((1,), (1,)), ((), ())), preferred_element_type=F32
+            ).astype(BF16)
+
+
+def feedforward(place, rw, prior, scales, blends, weights, kept):
     full = lambda *shape: pl.BlockSpec(shape, lambda k, *_: (0,) * len(shape))
     return pl.pallas_call(
         feedforward_kernel,
@@ -604,8 +899,7 @@
                 pl.BlockSpec((BRANCH, WIDTH), lambda k, *_: (0, k)),
                 pl.BlockSpec((3, WIDTH), lambda k, *_: (0, k)),
                 pl.BlockSpec((7, WIDTH), lambda k, *_: (0, k)),
-                pl.BlockSpec((WIDTH, KEYS + WIDTH), lambda k, *_: (k, 0)),
-                full(KEYS, HIDDEN),
+                pl.BlockSpec((WIDTH, 2 * KEYS + WIDTH), lambda k, *_: (k, 0)),
                 full(BRANCH, 1),
             ],
             out_specs=(full(ROWS, HIDDEN), full(ROWS, WIDTH), full(BRANCH, WIDTH)),
@@ -613,12 +907,13 @@
                 pltpu.VMEM((ROWS, 1), F32),
                 pltpu.VMEM((ROWS, 1), F32),
                 pltpu.VMEM((ROWS, KEYS + WIDTH), F32),
+                pltpu.VMEM((HIDDEN, KEYS), BF16),
             ],
         ),
         compiler_params=pltpu.CompilerParams(vmem_limit_bytes=52 << 20),
         cost_estimate=pl.CostEstimate(flops=5 << 30, transcendentals=1 << 18, bytes_accessed=24 << 20),
         name="feedforward",
-    )(place, rw, prior, scales, blends, keyed, content, kept.reshape(BRANCH, 1))
+    )(place, rw, prior, scales, blends, weights, kept.reshape(BRANCH, 1))
 
 
 def body(
@@ -648,19 +943,14 @@
     vocab_rows = symbol_vector_lookup.shape[0]
     slot_count = memory_matrix_store.shape[0]
 
-    result_matrix = lax.all_gather(attention_result_matrix, "tok", axis=1, tiled=True)
-    keyed = lax.all_gather(
-        jnp.concatenate([feedforward_lookup_matrix, feedforward_gating_matrix], axis=1),
+    weights = lax.all_gather(
+        jnp.concatenate(
+            [feedforward_content_matrix.T, feedforward_lookup_matrix, feedforward_gating_matrix], axis=1
+        ),
         "tok",
         axis=0,
         tiled=True,
     )
-    content = lax.all_gather(feedforward_content_matrix, "tok", axis=1, tiled=True)
-
-    wanted = guess_symbol_ids - tok_at * vocab_rows
-    inside = (wanted >= 0) & (wanted < vocab_rows)
-    found = jnp.take(symbol_vector_lookup, jnp.clip(wanted, 0, vocab_rows - 1), axis=0)
-    found = jnp.where(inside[:, None], found, jnp.zeros((), BF16)).reshape(4, 4, ROWS, WIDTH)
     priors = jnp.concatenate([prior_attention_normed, prior_feedforward_normed], axis=0)
 
     owners = (query_memory_slot // slot_count).reshape(TOK, REQ)
@@ -668,11 +958,26 @@
     owned_here = owners == tok_at
     send_slot = jnp.sum(jnp.where(owned_here, places, 0), axis=1)
     sending = jnp.any(owned_here, axis=1)
-    outgoing = jnp.where(
-        sending[:, None, None], jnp.take(memory_matrix_store, send_slot, axis=0), 0.0
-    ).astype(BF16)
-
-    whole, incoming = embed_exchange(found, priors, outgoing)
+    packed, spot, most = pack(
+        tok_at.reshape(1), guess_symbol_ids.reshape(TOK, ROWS), symbol_vector_lookup
+    )
+
+    def sparse(_):
+        return embed_exchange(
+            True, send_slot, memory_matrix_store, (packed.reshape(TOK, SPACE, WIDTH), spot), priors,
+            attention_result_matrix,
+        )
+
+    def dense(_):
+        wanted = guess_symbol_ids - tok_at * vocab_rows
+        inside = (wanted >= 0) & (wanted < vocab_rows)
+        found = jnp.take(symbol_vector_lookup, jnp.clip(wanted, 0, vocab_rows - 1), axis=0)
+        found = jnp.where(inside[:, None], found, jnp.zeros((), BF16)).reshape(4, 4, ROWS, WIDTH)
+        return embed_exchange(
+            False, send_slot, memory_matrix_store, (found,), priors, attention_result_matrix
+        )
+
+    whole, pages, results = lax.cond(most[0, 0] <= SPACE, sparse, dense, 0)
 
     my_owners = lax.dynamic_index_in_dim(owners, tok_at, 0, keepdims=False)
     my_counts = lax.dynamic_index_in_dim(candidate_tally_each_query, tok_at, 0, keepdims=False)
@@ -684,23 +989,13 @@
     best_score = jnp.max(jnp.where(member, branch_score[None, :], -1), axis=1)
     winner = BRANCH - 1 - best_score % BRANCH
 
-    diagonal = (
-        lax.broadcasted_iota(jnp.int32, (128, 128), 0) // HEAD
-        == lax.broadcasted_iota(jnp.int32, (128, 128), 1) // HEAD
-    )
-    my_pages = jnp.take(incoming, my_owners, axis=0).reshape(REQ, PAIRS, 128, HEAD)
-    pages = jnp.where(diagonal, jnp.concatenate([my_pages, my_pages], axis=-1), jnp.zeros((), BF16))
-
-    attended, chosen, shift_att_out = attention(
-        place, request_of, winner, kept_guess_tally,
+    partial_att, new_pages, shift_att_out = attention(
+        place, my_owners, request_of, winner, kept_guess_tally,
         whole, layernorm_scales, lagged_blend_ratios, attention_matrices,
         forgetting_narrow_matrix, forgetting_widen_matrix,
-        forgetting_baseline_vector, diagonal_boost, pages,
+        forgetting_baseline_vector, diagonal_boost, pages, results,
     )
-    partial_att = dot(attended, result_matrix).astype(BF16)
-
-    half = lax.broadcasted_iota(jnp.int32, (128, HEAD), 0) < HEAD
-    new_pages = jnp.where(half, chosen[..., :HEAD], chosen[..., HEAD:]).reshape(REQ, REQ, HIDDEN)
+
     targets = my_owners[None, :] == jnp.arange(TOK, dtype=jnp.int32)[:, None]
     pick_index = jnp.sum(
         jnp.where(targets, jnp.arange(REQ, dtype=jnp.int32)[None, :], 0), axis=1
@@ -712,15 +1007,12 @@
 
     partial_ffn, gate, shift_ffn_out = feedforward(
         place, residual_whole, whole[ROWS + BRANCH :], layernorm_scales, lagged_blend_ratios,
-        keyed, content, kept_guess_tally,
+        weights, kept_guess_tally,
     )
-    layer_out = final_exchange(partial_ffn, residual, gate)
-
     hit = (send_slot[None, :] == jnp.arange(slot_count, dtype=jnp.int32)[:, None]) & sending[None, :]
     source = jnp.sum(jnp.where(hit, jnp.arange(TOK, dtype=jnp.int32)[None, :], 0), axis=1)
-    store_out = jnp.where(
-        jnp.any(hit, axis=1)[:, None, None],
-        jnp.take(returned, source, axis=0).astype(F32),
+    layer_out, store_out = final_exchange(
+        source, jnp.any(hit, axis=1).astype(jnp.int32), partial_ffn, residual, gate, returned,
         memory_matrix_store,
     )
     return (layer_out, shift_att_out, shift_ffn_out, store_out)

time: 311 us -> 225 us (0.72)
  waiting for transfers between devices: 84.2 us -> 10.8 us
  local copies, waits for them, and re-layouts: 31.8 us -> 13.5 us
  Pallas kernels: 162 us -> 179 us
  other arithmetic: 14.1 us -> 5.8 us
  matrix products: 3.62 us -> 0 us
    all_gather x3 -> x1, waiting for transfers between devices: 82.8 us -> 10.8 us  [body(): lax.all_gather(jnp.concatenate([feedforward_content_matrix.T, feedforward...]
    gather x5 -> x0, local copies, waits for them, and re-layouts: 22 us -> none  [the longest x1 17.4 us: body(): jnp.take(symbol_vector_lookup, jnp.clip(wanted, 0, vocab_rows - 1), axis=0)]
    pallas_call x3 -> x4, Pallas kernels: 113 us -> 125 us  [the longest x1 76.2 us: embed_exchange(): pl.pallas_call(functools.partial(embed_kernel, sparse, len(inputs)), out_...]
    select_n x8 -> x0, other arithmetic: 9.11 us -> none  [the longest x1 3.59 us: body(): jnp.where(inside[:, None], found, jnp.zeros((), BF16))]
    pallas_call x1, Pallas kernels: 31.2 us -> 37.5 us  [residual_exchange(): pl.pallas_call(residual_kernel, out_shape=(jax.ShapeDtypeStruct((ROWS, HI...]
    dot_general x1 -> x0, matrix products: 3.62 us -> none  [dot(): return jnp.dot(a, b, preferred_element_type=F32)]
    unnamed x33 -> x56, local copies, waits for them, and re-layouts: 5.11 us -> 8.28 us
  transfers between devices with their start and end apart: 3 -> 1, of which waited for: 1 -> 1; matrix products, arithmetic and copies ran while one was open for 14% -> 4% of each run, Pallas kernels for 41% -> 65%
where the time goes in v2:
time: 225 us
  Pallas kernels  179 us (80%)
  between operations  15.1 us (7%)
  local copies, waits for them, and re-layouts  13.5 us (6%)
  waiting for transfers between devices  10.8 us (5%)
  other arithmetic  5.8 us (3%)
    pallas_call x1, Pallas kernels, embed_exchange(): pl.pallas_call(functools.partial(embed_kernel, sparse, len(inputs)), out_...  76.2 us
    pallas_call x1, Pallas kernels, residual_exchange(): pl.pallas_call(residual_kernel, out_shape=(jax.ShapeDtypeStruct((ROWS, HI...  37.5 us
    pallas_call x1, Pallas kernels, attention(): pl.pallas_call(attention_kernel, out_shape=(jax.ShapeDtypeStruct((ROWS, H...  21.5 us
    pallas_call x1, Pallas kernels, feedforward(): pl.pallas_call(feedforward_kernel, out_shape=(jax.ShapeDtypeStruct((ROWS,...  17.1 us
    pallas_call x1, Pallas kernels, final_exchange(): pl.pallas_call(final_kernel, out_shape=(jax.ShapeDtypeStruct((ROWS, WIDTH...  17.1 us
    all_gather x1, waiting for transfers between devices, body(): lax.all_gather(jnp.concatenate([feedforward_content_matrix.T, feedforward...  10.8 us
    pallas_call x1, Pallas kernels, pack(): pl.pallas_call(pack_kernel, out_shape=(jax.ShapeDtypeStruct((TOK * SPACE,...  9.82 us
    unnamed x56, local copies, waits for them, and re-layouts  8.28 us
  transfers between devices with their start and end apart: 1, of which 1 were waited for; matrix products, arithmetic and copies ran while one was open for 4% of the time, Pallas kernels for 65%

profile of v2, /device:TPU:1, one launch (start us, length us, event | category | flops | bytes accessed | tf_op | source)
XLA Modules:
  0.0 224.6 jit_solution(14613494456594155211)
XLA Ops:
  7.2 0.0 copy-start
  7.2 0.0 all-gather.2.cloned.1.call-start
  7.3 1.4 copy.30
  8.7 2.2 pad_maximum_fusion
  10.9 0.0 all-gather.2.cloned.1.call-update
  10.9 0.1 reshape.107
  11.0 0.1 reshape.108
  11.1 0.1 fusion.7
  11.2 0.0 copy-start.27
  11.2 0.1 select_reduce_fusion.2
  11.4 0.3 copy-done.21
  11.6 0.1 fusion.2
  11.8 0.2 dynamic-slice_reduce_fusion
  12.0 0.7 reduce-window.8
  12.7 0.0 copy-start.9
  12.7 0.0 copy-start.13
  12.7 0.0 copy-start.22
  12.8 0.0 copy-start.23
  12.8 9.8 %pack.1 = (bf16[768,512]{1,0:T(8,128)(2,1)}, s32[256,1]{1,0:T(8,128)}, s32[8,128]{1,0:T(8,128)S(1)}) custom-call(s32[1]{0:T(128)} %bitcast.3.place, s32[16,256]{1,0:T(8,128)S(1)} %reshape.113.ids, bf16[2048,512]{1,0:T(8,128)(2,1)S(1)} %copy-done.14), custom_call_target="tpu_custom_call" | custom-call | flops 2147483648 | bytes 4194304 | tf_op jit(solution)/shard_map/pack/pallas_call | solution.py:560
  22.6 0.5 slice.9
  23.8 0.1 copy.29.kept_column
  23.9 0.0 copy-done.22
  23.9 0.6 copy-done.18
  24.5 0.0 copy-start.12
  24.6 77.3 %conditional.1 = (bf16[288,4096]{1,0:T(8,128)(2,1)}, bf16[16,4,64,128]{3,2,1,0:T(8,128)(2,1)}, bf16[4,512,1024]{2,1,0:T(8,128)(2,1)}, bf16[16,4096]{1,0:T(8,128)(2,1)S(1)}) conditional(s32[]{:T(128)} %bitcast.4, (s32[]{:T(128)}, s32[4096]{0:T(1024)S(1)}, bf16[2048,512]{1,0:T(8,128)(2,1)S(1)}, s32[16]{0:T(128)}, f32[16,8,4096]{2,1,0:T(8,128)}, ...), branch_computations={%region_7.8_spmd.clone, %region_8.9_spmd.clone} | conditional | flops 4263937 | bytes 131563936 | solution.py:980
  24.6 76.2 %embed_sparse.2 = (bf16[288,4096]{1,0:T(8,128)(2,1)}, bf16[16,4,64,128]{3,2,1,0:T(8,128)(2,1)}, bf16[4,512,1024]{2,1,0:T(8,128)(2,1)}) custom-call(s32[16]{0:T(128)} %get-tuple-element.118.refs_0_, f32[16,8,4096]{2,1,0:T(8,128)} %get-tuple-element.119.refs_1_, bf16[16,48,512]{2,1,0:T(8,128)(2,1)} %bitcast.22, s32[256,1]{1,0:T(8,128)} %get-tuple-element.121.refs_3_, ...), custom_call_target="tpu_custom_call" | custom-call | bytes 104857600 | tf_op jit(solution)/shard_map/cond/branch_1_fun/embed_sparse/pallas_call | solution.py:481
  100.7 0.9 slice.13
  101.8 0.7 fusion.3.owner_of
  102.5 0.1 select_reduce_fusion
  102.7 0.7 convert_reduce_fusion.request_of
  103.4 0.1 select_reduce_fusion.3
  103.6 21.5 %attention.1 = (bf16[256,4096]{1,0:T(8,128)(2,1)}, bf16[8,4,64,128]{3,2,1,0:T(8,128)(2,1)S(1)}, bf16[16,512]{1,0:T(8,128)(2,1)}) custom-call(s32[1]{0:T(128)} %bitcast.place, s32[8]{0:T(128)S(1)} %fusion.3.owner_of, s32[16]{0:T(128)S(1)} %convert_reduce_fusion.request_of, s32[8]{0:T(128)S(1)} %fusion.4.winner, s32[16]{0:T(128)S(1)} %copy-done.13, ...), custom_call_target="tpu_custom_call" | custom-call | flops 6442450944 | bytes 25165824 | tf_op jit(solution)/shard_map/attention/pallas_call | solution.py:804
  125.1 0.0 copy-start.3
  125.1 1.7 gather_fusion.1
  126.8 1.0 constant_dynamic-slice_fusion.base
  127.8 1.4 broadcast_select_fusion.out_pages
  129.2 37.5 %residual_exchange.1 = (bf16[256,4096]{1,0:T(8,128)(2,1)S(1)}, bf16[256,512]{1,0:T(8,128)(2,1)S(1)}, bf16[16,4,64,128]{3,2,1,0:T(8,128)(2,1)S(1)}) custom-call(bf16[256,4096]{1,0:T(8,128)(2,1)S(1)} %copy-done.3, bf16[256,512]{1,0:T(8,128)(2,1)S(1)} %constant_dynamic-slice_fusion.base, bf16[16,4,64,128]{3,2,1,0:T(8,128)(2,1)S(1)} %broadcast_select_fusion.out_pages), custom_call_target="tpu_custom_call" | custom-call | bytes 83886080 | tf_op jit(solution)/shard_map/residual_exchange/pallas_call | solution.py:587
  166.7 0.0 copy-start.4
  166.8 1.3 copy-done.4
  168.1 1.0 copy-done.6
  169.0 0.1 select_reduce_fusion.1.source
  169.2 10.8 %all-gather.2.cloned.1.call-done.weights = bf16[4096,2304]{1,0:T(8,128)(2,1)} async-done(((bf16[256,2304]{1,0:T(8,128)(2,1)}), bf16[4096,2304]{1,0:T(8,128)(2,1)}) %all-gather.2.cloned.1.call-update) | async-done | bytes 18874384 | tf_op jit(solution)/shard_map/all_gather | solution.py:946
  179.9 17.1 %feedforward.1 = (bf16[256,4096]{1,0:T(8,128)(2,1)}, f32[256,512]{1,0:T(8,128)S(1)}, bf16[16,512]{1,0:T(8,128)(2,1)}) custom-call(s32[1]{0:T(128)} %bitcast.place, bf16[256,4096]{1,0:T(8,128)(2,1)} %copy-done.4, bf16[16,4096]{1,0:T(8,128)(2,1)S(1)} %get-tuple-element.136.prior_ref, f32[3,4096]{1,0:T(4,128)S(1)} %copy-done.9, f32[7,4096]{1,0:T(8,128)S(1)} %copy-done.8, ...), custom_call_target="tpu_custom_call" | custom-call | flops 5368709120 | bytes 25165824 | tf_op jit(solution)/shard_map/feedforward/pallas_call | solution.py:887
  197.1 1.6 copy-done.2
  198.6 17.1 %final_exchange.1 = (bf16[256,512]{1,0:T(8,128)(2,1)S(1)}, f32[16,8,4096]{2,1,0:T(8,128)S(1)}) custom-call(s32[16]{0:T(128)S(1)} %select_reduce_fusion.1.source, s32[16]{0:T(128)S(1)} %convert_element_type.12.hit, bf16[256,4096]{1,0:T(8,128)(2,1)S(1)} %copy-done.2, bf16[256,512]{1,0:T(8,128)(2,1)S(1)} %get-tuple-element.98.base, ...), custom_call_target="tpu_custom_call" | custom-call | bytes 41943040 | tf_op jit(solution)/shard_map/final_exchange/pallas_call | solution.py:633
  215.7 0.0 copy-start.1
  215.7 0.7 copy.43
  216.4 1.3 copy.44
  (47 shorter events, 0.2 us)
Async XLA Ops:
  7.2 4.6 %copy-start = (s32[16,8]{0,1:T(8,128)S(1)}, s32[16,8]{0,1:T(8,128)}, u32[]{:S(2)}) copy-start(s32[16,8]{0,1:T(8,128)} %param.38) | copy-start | bytes 1540
  7.2 3.7 %copy-start.29 = (s32[128]{0:T(128)S(1)}, s32[128]{0:T(128)}, u32[]{:S(2)}) copy-start(s32[128]{0:T(128)} %param.37) | copy-start | bytes 1540
  7.2 5.5 %copy-start.20 = (s32[4096]{0:T(1024)S(1)}, s32[4096]{0:T(1024)}, u32[]{:S(2)}) copy-start(s32[4096]{0:T(1024)} %param.21) | copy-start | bytes 49156
  7.2 5.5 %copy-start.14 = (bf16[2048,512]{1,0:T(8,128)(2,1)S(1)}, bf16[2048,512]{1,0:T(8,128)(2,1)}, u32[]{:S(2)}) copy-start(bf16[2048,512]{1,0:T(8,128)(2,1)} %table.1) | copy-start | bytes 6291460
  7.2 172.7 %all-gather.2.cloned.1.call-start = ((), (), s32[]{:S(2)}) async-start(), calls=%async_computation | async-start | bytes 20054016 | tf_op jit(solution)/shard_map/all_gather | solution.py:946
  11.0 0.6 copy-start.21
  11.2 1.5 copy-start.27
  11.4 1.3 copy-start.24
  12.7 11.0 %copy-start.9 = (f32[3,4096]{1,0:T(4,128)S(1)}, f32[3,4096]{1,0:T(4,128)}, u32[]{:S(2)}) copy-start(f32[3,4096]{1,0:T(4,128)} %gain.1) | copy-start | bytes 147460
  12.7 11.1 %copy-start.13 = (s32[16]{0:T(128)S(1)}, s32[16]{0:T(128)}, u32[]{:S(2)}) copy-start(s32[16]{0:T(128)} %kept.1) | copy-start | bytes 196
  12.7 11.2 %copy-start.22 = (bf16[16,512]{1,0:T(8,128)(2,1)S(1)}, bf16[16,512]{1,0:T(8,128)(2,1)}, u32[]{:S(2)}) copy-start(bf16[16,512]{1,0:T(8,128)(2,1)} %param.23) | copy-start | bytes 49156
  12.8 11.1 %copy-start.23 = (bf16[16,512]{1,0:T(8,128)(2,1)S(1)}, bf16[16,512]{1,0:T(8,128)(2,1)}, u32[]{:S(2)}) copy-start(bf16[16,512]{1,0:T(8,128)(2,1)} %param.24) | copy-start | bytes 49156
  23.9 0.6 copy-start.18
  24.5 79.0 %copy-start.5 = (bf16[4096,128]{1,0:T(8,128)(2,1)S(1)}, bf16[4096,128]{1,0:T(8,128)(2,1)}, u32[]{:S(2)}) copy-start(bf16[4096,128]{1,0:T(8,128)(2,1)} %narrow.1) | copy-start | bytes 3145732
  24.5 79.0 %copy-start.8 = (f32[7,4096]{1,0:T(8,128)S(1)}, f32[7,4096]{1,0:T(8,128)}, u32[]{:S(2)}) copy-start(f32[7,4096]{1,0:T(8,128)} %blend.3) | copy-start | bytes 344068
  24.5 79.0 %copy-start.10 = (bf16[128,512]{1,0:T(8,128)(2,1)S(1)}, bf16[128,512]{1,0:T(8,128)(2,1)}, u32[]{:S(2)}) copy-start(bf16[128,512]{1,0:T(8,128)(2,1)} %widen.1) | copy-start | bytes 393220
  24.5 79.0 %copy-start.11 = (f32[4096]{0:T(1024)S(1)}, f32[4096]{0:T(1024)}, u32[]{:S(2)}) copy-start(f32[4096]{0:T(1024)} %param.28) | copy-start | bytes 49156
  24.5 79.0 %copy-start.12 = (f32[4096]{0:T(1024)S(1)}, f32[4096]{0:T(1024)}, u32[]{:S(2)}) copy-start(f32[4096]{0:T(1024)} %param.31) | copy-start | bytes 49156
  125.1 4.1 %copy-start.3 = (bf16[256,4096]{1,0:T(8,128)(2,1)S(1)}, bf16[256,4096]{1,0:T(8,128)(2,1)}, u32[]{:S(2)}) copy-start(bf16[256,4096]{1,0:T(8,128)(2,1)} %get-tuple-element.94.part) | copy-start | bytes 6291460
  127.8 41.2 %copy-start.25 = (s32[16]{0:T(128)S(1)}, s32[16]{0:T(128)}, u32[]{:S(2)}) copy-start(s32[16]{0:T(128)} %copy-done.24) | copy-start | bytes 196
  127.8 41.2 %copy-start.28 = (pred[16]{0:T(512)(128)(4,1)S(1)}, pred[16]{0:T(512)(128)(4,1)}, u32[]{:S(2)}) copy-start(pred[16]{0:T(512)(128)(4,1)} %copy-done.27) | copy-start | bytes 52
  166.7 1.3 copy-start.4
  168.1 1.0 copy-start.6
  179.9 17.1 %copy-start.7 = (bf16[16,4,64,128]{3,2,1,0:T(8,128)(2,1)S(1)}, bf16[16,4,64,128]{3,2,1,0:T(8,128)(2,1)}, u32[]{:S(2)}) copy-start(bf16[16,4,64,128]{3,2,1,0:T(8,128)(2,1)} %copy-done.6) | copy-start | bytes 3145732
  179.9 17.1 %copy-start.15 = (f32[16,8,4096]{2,1,0:T(8,128)S(1)}, f32[16,8,4096]{2,1,0:T(8,128)}, u32[]{:S(2)}) copy-start(f32[16,8,4096]{2,1,0:T(8,128)} %store.1) | copy-start | bytes 6291460
  197.1 1.6 copy-start.2
  215.7 2.0 copy-start.1
Sparse Core Ops, SparseCore 0:
  11.0 168.8 all-gather.1

commit v3 on v2

v3 whole, which is shorter than its diff:
```python
import functools

import jax
import jax.numpy as jnp
from jax import lax
from jax.experimental import pallas as pl
from jax.experimental.pallas import tpu as pltpu
from jax.sharding import PartitionSpec as P

HIDDEN = 4096
HEAD = 64
DRAFT = 16
BRANCH = 16
ROWS = BRANCH * DRAFT
WIDTH = 512
TOK = 16
GRP = 8
REQ = 8
PAIRS = 4
KEYS = 896
SPACE = 48
EPSILON = 1e-05
HEAD_EPSILON = 0.00064
F32 = jnp.float32
BF16 = jnp.bfloat16
MESH = pl.DeviceIdType.MESH
ANY = pl.BlockSpec(memory_space=pl.ANY)
VMEM = pl.BlockSpec(memory_space=pltpu.VMEM)


def remote(src, dst, send, recv, device):
    return pltpu.make_async_remote_copy(
        src_ref=src, dst_ref=dst, send_sem=send, recv_sem=recv, device_id=device, device_id_type=MESH
    )


def greet(devices):
    barrier = pltpu.get_barrier_semaphore()
    for device in devices:
        pl.semaphore_signal(barrier, inc=1, device_id=device, device_id_type=MESH)
    pl.semaphore_wait(barrier, len(devices))


def grp_places():
    g = lax.axis_index("grp")
    z, core = g // 2, g % 2
    up = lax.rem(z + 1, 4) * 2 + core
    down = lax.rem(z + 3, 4) * 2 + core
    far = lax.rem(z + 2, 4) * 2 + core
    mate = z * 2 + 1 - core
    return g, up, down, far, mate


def block_of(g):
    return pl.ds(pl.multiple_of(g * WIDTH, WIDTH), WIDTH)


def flip(g):
    return g + 1 - 2 * lax.rem(g, 2)


def gather_grp(own, out, send, recv, local, between=()):
    between = list(between)

    def aside():
        if between:
            between.pop(0)()

    rows = out.shape[0]
    half = rows // 2
    g, up, down, far, mate = grp_places()
    first, last, whole = pl.ds(0, half), pl.ds(half, rows - half), pl.ds(0, rows)
    at = lambda part, g_of: out.at[part, block_of(g_of)]
    keep = pltpu.make_async_copy(own, at(whole, g), local)
    keep.start()
    started = []

    def go(index, src, part, g_of, target):
        copy = remote(src, at(part, g_of), send.at[index], recv.at[index], {"grp": target})
        copy.start()
        started.append(copy)

    def came(index, part, g_of):
        remote(at(part, g_of), at(part, g_of), send.at[index], recv.at[index], {"grp": mate}).wait_recv()

    go(0, own, whole, g, up)
    go(1, own, whole, g, down)
    go(2, own, whole, g, mate)
    aside()
    came(0, whole, down)
    go(3, at(first, down), first, down, up)
    go(5, at(whole, down), whole, down, mate)
    came(1, whole, up)
    go(4, at(last, up), last, up, down)
    go(6, at(whole, up), whole, up, mate)
    aside()
    came(3, first, far)
    go(7, at(first, far), first, far, mate)
    came(4, last, far)
    go(8, at(last, far), last, far, mate)
    came(2, whole, mate)
    came(5, whole, flip(down))
    came(6, whole, flip(up))
    came(7, first, flip(far))
    came(8, last, flip(far))
    while between:
        aside()
    keep.wait()
    for copy in started:
        copy.wait_send()


def reduce_grp(part, mated, sums, halves, full, send, recv, meanwhile=lambda: None):
    g, up, down, far, mate = grp_places()
    half = ROWS // 2
    started = []

    def go(index, src, dst, target):
        copy = remote(src, dst, send.at[index], recv.at[index], {"grp": target})
        copy.start()
        started.append(copy)

    def came(index, dst):
        remote(dst, dst, send.at[index], recv.at[index], {"grp": mate}).wait_recv()

    order = (far, up, down, g)
    for k in range(4):
        go(k, part.at[:, block_of(flip(order[k]))], mated.at[k], mate)

    def own(k):
        return part[:, block_of(order[k])].astype(F32) + mated[k].astype(F32)

    came(0, mated.at[0])
    sums[0] = own(0).astype(BF16)
    go(4, sums.at[0, pl.ds(0, half)], halves.at[0], up)
    go(5, sums.at[0, pl.ds(half, half)], halves.at[1], down)
    came(1, mated.at[1])
    came(4, halves.at[0])
    sums[1, :half] = (own(1)[:half] + halves[0].astype(F32)).astype(BF16)
    sums[1, half:] = own(1)[half:].astype(BF16)
    go(6, sums.at[1], full.at[0], up)
    came(2, mated.at[2])
    came(5, halves.at[1])
    sums[2, :half] = own(2)[:half].astype(BF16)
    sums[2, half:] = (own(2)[half:] + halves[1].astype(F32)).astype(BF16)
    go(7, sums.at[2], full.at[1], down)
    meanwhile()
    came(3, mated.at[3])
    came(6, full.at[0])
    came(7, full.at[1])
    total = own(3) + full[0].astype(F32) + full[1].astype(F32)
    for copy in started:
        copy.wait_send()
    return total


REDUCE_SCRATCH = [
    pltpu.VMEM((4, ROWS, WIDTH), BF16),
    pltpu.VMEM((3, ROWS, WIDTH), BF16),
    pltpu.VMEM((2, ROWS // 2, WIDTH), BF16),
    pltpu.VMEM((2, ROWS, WIDTH), BF16),
    pltpu.SemaphoreType.DMA((8,)),
    pltpu.SemaphoreType.DMA((8,)),
]


def result_views(out):
    cols = lambda x_of: pl.ds(pl.multiple_of(x_of * 256, 256), 256)
    return (
        lambda rows, y_of, x_of: out.at[y_of, rows, cols(x_of)],
        lambda rows, y_of: out.at[y_of, rows],
        lambda rows, x_of: out.at[:, rows, cols(x_of)],
    )


def stack_views(out):
    return (
        lambda rows, y_of, x_of: out.at[y_of, x_of, rows],
        lambda rows, y_of: out.at[y_of, :, rows],
        lambda rows, x_of: out.at[:, x_of, rows],
    )


def gather_tok(own, views, send, recv, local):
    t = lax.axis_index("tok")
    y, x = t // 4, lax.rem(t, 4)
    xu, xd, xf = [lax.rem(x + k, 4) for k in (1, 3, 2)]
    yu, yd, yf = [lax.rem(y + k, 4) for k in (1, 3, 2)]
    along_x = lambda x_of: {"tok": y * 4 + x_of}
    along_y = lambda y_of: {"tok": y_of * 4 + x}
    one, wide, tall = views
    count = own.shape[0]
    f0, f1 = pl.ds(0, count // 2), pl.ds(count // 2, count // 2)
    fa, fb = [pl.ds(f0.start + k * (f0.size // 2), f0.size // 2) for k in (0, 1)]
    la, lb = [pl.ds(f1.start + k * (f1.size // 2), f1.size // 2) for k in (0, 1)]
    started = []

    def go(index, src, dst, target):
        copy = remote(src, dst, send.at[index], recv.at[index], target)
        copy.start()
        started.append(copy)

    def came(index, dst):
        remote(dst, dst, send.at[index], recv.at[index], along_x(xu)).wait_recv()

    keep = pltpu.make_async_copy(own, one(pl.ds(0, count), y, x), local)

    def begin():
        keep.start()
        go(0, own.at[f0], one(f0, y, x), along_x(xu))
        go(1, own.at[f0], one(f0, y, x), along_x(xd))
        go(2, own.at[f1], one(f1, y, x), along_y(yu))
        go(3, own.at[f1], one(f1, y, x), along_y(yd))

    def relay():
        came(0, one(f0, y, xd))
        go(4, one(fa, y, xd), one(fa, y, xd), along_x(xu))
        came(2, one(f1, yd, x))
        go(6, one(la, yd, x), one(la, yd, x), along_y(yu))
        came(1, one(f0, y, xu))
        go(5, one(fb, y, xu), one(fb, y, xu), along_x(xd))
        came(3, one(f1, yu, x))
        go(7, one(lb, yu, x), one(lb, yu, x), along_y(yd))

    def turn():
        keep.wait()
        came(4, one(fa, y, xf))
        came(5, one(fb, y, xf))
        go(8, wide(f0, y), wide(f0, y), along_y(yu))
        go(9, wide(f0, y), wide(f0, y), along_y(yd))
        came(6, one(la, yf, x))
        came(7, one(lb, yf, x))
        go(10, tall(f1, x), tall(f1, x), along_x(xu))
        go(11, tall(f1, x), tall(f1, x), along_x(xd))

    def last():
        came(8, wide(f0, yd))
        go(12, wide(fa, yd), wide(fa, yd), along_y(yu))
        came(10, tall(f1, xd))
        go(14, tall(la, xd), tall(la, xd), along_x(xu))
        came(9, wide(f0, yu))
        go(13, wide(fb, yu), wide(fb, yu), along_y(yd))
        came(11, tall(f1, xu))
        go(15, tall(lb, xu), tall(lb, xu), along_x(xd))

    def end():
        came(12, wide(fa, yf))
        came(13, wide(fb, yf))
        came(14, tall(la, xf))
        came(15, tall(lb, xf))
        for copy in started:
            copy.wait_send()

    return begin, relay, turn, last, end


def grp_peers():
    _, up, down, _, mate = grp_places()
    return [{"grp": up}, {"grp": down}, {"grp": mate}]


def tok_peers():
    t = lax.axis_index("tok")
    return [{"tok": lax.rem(t + k, TOK)} for k in range(1, TOK)]


def page_masks():
    even = lax.rem(lax.broadcasted_iota(jnp.int32, (8, 128), 0), 2) == 0
    left = lax.broadcasted_iota(jnp.int32, (8, 128), 1) < HEAD
    return even, left


def pair_page(page, put):
    even, left = page_masks()
    for block in range(4):
        rows = [[] for _ in range(PAIRS)]
        for group in (2 * block, 2 * block + 1):
            pieces = []
            for m in range(4 * group, 4 * group + 4):
                here = page[:, m * 128 : m * 128 + 128]
                swapped = pltpu.roll(here, HEAD, axis=1)
                pieces += [jnp.where(even, here, swapped), jnp.where(even, swapped, here)]
            turned = jnp.swapaxes(jnp.stack(pieces), 0, 1)
            for pair in range(PAIRS):
                rows[pair].append(jnp.where(left, turned[2 * pair], turned[2 * pair + 1]))
        for pair in range(PAIRS):
            put(pair, 16 * block, jnp.concatenate(rows[pair], axis=0))


def flat_page(page, put):
    even, left = page_masks()
    for group in range(8):
        rows = [page[pair, 8 * group : 8 * group + 8] for pair in range(PAIRS)]
        turned = jnp.swapaxes(jnp.stack([rows[h // 2] for h in range(8)]), 0, 1)
        for m in range(4):
            first, second = turned[2 * m], turned[2 * m + 1]
            swapped_first = pltpu.roll(first, HEAD, axis=1)
            swapped_second = pltpu.roll(second, HEAD, axis=1)
            put(
                (4 * group + m) * 128,
                jnp.where(
                    left,
                    jnp.where(even, first, swapped_first),
                    jnp.where(even, swapped_second, second),
                ),
            )


def trade_start(out_pages, in_pages, send, recv, local):
    t = lax.axis_index("tok")
    keep = pltpu.make_async_copy(out_pages.at[t], in_pages.at[t], local)
    keep.start()
    for k in range(1, TOK):
        peer = lax.rem(t + k, TOK)
        remote(out_pages.at[peer], in_pages.at[t], send.at[k - 1], recv.at[k - 1], {"tok": peer}).start()
    return keep


def trade_end(out_pages, in_pages, send, recv, keep):
    t = lax.axis_index("tok")
    keep.wait()
    for k in range(1, TOK):
        peer = lax.rem(t + k, TOK)
        origin = lax.rem(t + TOK - k, TOK)
        copy = remote(out_pages.at[peer], in_pages.at[origin], send.at[k - 1], recv.at[k - 1], {"tok": peer})
        copy.wait_recv()
        copy.wait_send()


TRADE_SEMAPHORES = [
    pltpu.SemaphoreType.DMA((TOK - 1,)),
    pltpu.SemaphoreType.DMA((TOK - 1,)),
    pltpu.SemaphoreType.DMA,
]


def dense_rows(found, own, begin, a1h, a1s, a1f, b1h, b1s, b1f, a2, a2h, a2s, a2f, b2, b2h, b2s, b2f, xsend, xrecv):
    t = lax.axis_index("tok")
    y, x = t // 4, lax.rem(t, 4)
    xu, xd, xf = [lax.rem(x + k, 4) for k in (1, 3, 2)]
    yu, yd, yf = [lax.rem(y + k, 4) for k in (1, 3, 2)]
    along_x = lambda x_of: {"tok": y * 4 + x_of}
    along_y = lambda y_of: {"tok": y_of * 4 + x}
    started = []

    def go(index, src, dst, target):
        copy = remote(src, dst, xsend.at[index], xrecv.at[index], target)
        copy.start()
        started.append(copy)

    def came(index, dst):
        remote(dst, dst, xsend.at[index], xrecv.at[index], along_x(xu)).wait_recv()

    h = WIDTH // 2
    left, right = pl.ds(0, h), pl.ds(h, h)
    low, high = pl.ds(0, 2), pl.ds(2, 2)
    go(0, found.at[low, xf, :, left], a1h.at[0], along_x(xu))
    go(1, found.at[high, xf, :, left], a1h.at[1], along_x(xd))
    go(2, found.at[yf, low, :, right], b1h.at[0], along_y(yu))
    go(3, found.at[yf, high, :, right], b1h.at[1], along_y(yd))
    begin()
    came(0, a1h.at[0])
    a1s[0, :2] = found[:2, xu, :, :h] + a1h[0]
    a1s[0, 2:] = found[2:, xu, :, :h]
    go(4, a1s.at[0], a1f.at[0], along_x(xu))
    came(1, a1h.at[1])
    a1s[1, :2] = found[:2, xd, :, :h]
    a1s[1, 2:] = found[2:, xd, :, :h] + a1h[1]
    go(5, a1s.at[1], a1f.at[1], along_x(xd))
    came(2, b1h.at[0])
    b1s[0, :2] = found[yu, :2, :, h:] + b1h[0]
    b1s[0, 2:] = found[yu, 2:, :, h:]
    go(6, b1s.at[0], b1f.at[0], along_y(yu))
    came(3, b1h.at[1])
    b1s[1, :2] = found[yd, :2, :, h:]
    b1s[1, 2:] = found[yd, 2:, :, h:] + b1h[1]
    go(7, b1s.at[1], b1f.at[1], along_y(yd))
    m = ROWS // 2
    top, bottom = pl.ds(0, m), pl.ds(m, m)
    came(4, a1f.at[0])
    came(5, a1f.at[1])
    a2[...] = found[:, x, :, :h] + a1f[0] + a1f[1]
    go(8, a2.at[yf, top], a2h.at[0], along_y(yu))
    go(9, a2.at[yf, bottom], a2h.at[1], along_y(yd))
    came(6, b1f.at[0])
    came(7, b1f.at[1])
    b2[...] = found[y, :, :, h:] + b1f[0] + b1f[1]
    go(10, b2.at[xf, top], b2h.at[0], along_x(xu))
    go(11, b2.at[xf, bottom], b2h.at[1], along_x(xd))
    came(8, a2h.at[0])
    a2s[0, :m] = a2[yu, :m] + a2h[0]
    a2s[0, m:] = a2[yu, m:]
    go(12, a2s.at[0], a2f.at[0], along_y(yu))
    came(9, a2h.at[1])
    a2s[1, :m] = a2[yd, :m]
    a2s[1, m:] = a2[yd, m:] + a2h[1]
    go(13, a2s.at[1], a2f.at[1], along_y(yd))
    came(10, b2h.at[0])
    b2s[0, :m] = b2[xu, :m] + b2h[0]
    b2s[0, m:] = b2[xu, m:]
    go(14, b2s.at[0], b2f.at[0], along_x(xu))
    came(11, b2h.at[1])
    b2s[1, :m] = b2[xd, :m]
    b2s[1, m:] = b2[xd, m:] + b2h[1]
    go(15, b2s.at[1], b2f.at[1], along_x(xd))
    came(12, a2f.at[0])
    came(13, a2f.at[1])
    own[:ROWS, :h] = a2[y] + a2f[0] + a2f[1]
    came(14, b2f.at[0])
    came(15, b2f.at[1])
    own[:ROWS, h:] = b2[x] + b2f[0] + b2f[1]
    for copy in started:
        copy.wait_send()


def dense_kernel(found, own, *rest):
    greet(tok_peers())
    dense_rows(found, own, lambda: None, *rest)


def dense_exchange(found):
    h, m = WIDTH // 2, ROWS // 2
    return pl.pallas_call(
        dense_kernel,
        out_shape=jax.ShapeDtypeStruct((ROWS, WIDTH), BF16),
        in_specs=[VMEM],
        out_specs=VMEM,
        scratch_shapes=[
            pltpu.VMEM((2, 2, ROWS, h), BF16),
            pltpu.VMEM((2, 4, ROWS, h), BF16),
            pltpu.VMEM((2, 4, ROWS, h), BF16),
            pltpu.VMEM((2, 2, ROWS, h), BF16),
            pltpu.VMEM((2, 4, ROWS, h), BF16),
            pltpu.VMEM((2, 4, ROWS, h), BF16),
            pltpu.VMEM((4, ROWS, h), BF16),
            pltpu.VMEM((2, m, h), BF16),
            pltpu.VMEM((2, ROWS, h), BF16),
            pltpu.VMEM((2, ROWS, h), BF16),
            pltpu.VMEM((4, ROWS, h), BF16),
            pltpu.VMEM((2, m, h), BF16),
            pltpu.VMEM((2, ROWS, h), BF16),
            pltpu.VMEM((2, ROWS, h), BF16),
            pltpu.SemaphoreType.DMA((16,)),
            pltpu.SemaphoreType.DMA((16,)),
        ],
        compiler_params=pltpu.CompilerParams(
            collective_id=1, has_side_effects=True, vmem_limit_bytes=40 << 20
        ),
        name="dense_exchange",
    )(found)


def pack_kernel(place, ids, table, packed, spot, most, slot_s):
    t_at = place[0]
    shape = (ROWS, ROWS)
    sub = lax.broadcasted_iota(jnp.int32, shape, 0)
    lane = lax.broadcasted_iota(jnp.int32, shape, 1)
    vocab_rows = table.shape[0]
    base = t_at * vocab_rows

    def column(row):
        return jnp.sum(jnp.where(sub == lane, jnp.broadcast_to(row, shape), 0), axis=1, keepdims=True)

    def ranks(row):
        col = column(row)
        same = col == row
        first_col = 1 - jnp.max(jnp.where(same & (lane < sub), 1, 0), axis=1, keepdims=True)
        first_row = 1 - jnp.max(jnp.where(same & (sub < lane), 1, 0), axis=0, keepdims=True)
        start = row - lax.rem(row, vocab_rows)
        ahead = (col < row) & (col >= start)
        rank = jnp.sum(jnp.where(ahead, first_col, 0), axis=0, keepdims=True)
        return first_row, start, rank

    def one(t, top):
        row = ids[pl.ds(t, 1), :]
        first_row, start, rank = ranks(row)
        mine = (first_row > 0) & (start == base)
        slot = lax.broadcasted_iota(jnp.int32, (SPACE, ROWS), 0)
        hit = (slot == rank) & mine
        slot_s[pl.ds(pl.multiple_of(t * SPACE, SPACE), SPACE)] = (
            jnp.sum(jnp.where(hit, row - base + 1, 0), axis=1, keepdims=True) - 1
        )

        @pl.when(t == t_at)
        def _():
            owner = start // vocab_rows
            spot[...] = column(owner * SPACE + rank)

        return jnp.maximum(top, rank)

    top = lax.fori_loop(0, TOK, one, jnp.zeros((1, ROWS), jnp.int32))
    most[...] = jnp.broadcast_to(jnp.max(top, axis=1, keepdims=True) + 1, (8, 128))
    step = 256
    for k in range(TOK * SPACE // step):
        rows = pl.ds(k * step, step)
        pick = (
            lax.broadcasted_iota(jnp.int32, (step, vocab_rows), 1) == slot_s[rows]
        ).astype(BF16)
        packed[rows] = dot(pick, table[...]).astype(BF16)


def pack(place, ids, table):
    return pl.pallas_call(
        pack_kernel,
        out_shape=(
            jax.ShapeDtypeStruct((TOK * SPACE, WIDTH), BF16),
            jax.ShapeDtypeStruct((ROWS, 1), jnp.int32),
            jax.ShapeDtypeStruct((8, 128), jnp.int32),
        ),
        in_specs=[pl.BlockSpec(memory_space=pltpu.SMEM), VMEM, VMEM],
        out_specs=(VMEM, VMEM, VMEM),
        scratch_shapes=[pltpu.VMEM((TOK * SPACE, 1), jnp.int32)],
        compiler_params=pltpu.CompilerParams(vmem_limit_bytes=32 << 20),
        cost_estimate=pl.CostEstimate(flops=2 << 30, transcendentals=0, bytes_accessed=4 << 20),
        name="pack",
    )(place, ids, table)


def dot(a, b):
    return jnp.dot(a, b, preferred_element_type=F32)


def normed_and_step(block, prior, mean, scale, gain):
    normed = (block.astype(F32) - mean) * scale * gain
    row = lax.broadcasted_iota(jnp.int32, (ROWS, WIDTH), 0)
    spread = (
        lax.broadcasted_iota(jnp.int32, (ROWS, BRANCH), 0) // DRAFT
        == lax.broadcasted_iota(jnp.int32, (ROWS, BRANCH), 1)
    )
    carried = dot(spread.astype(BF16), prior)
    before = jnp.where(lax.rem(row, DRAFT) == 0, carried, pltpu.roll(normed, 1, axis=0))
    return normed, before - normed


def kept_row(normed, prior, kept_column):
    column = lax.broadcasted_iota(jnp.int32, (BRANCH, ROWS), 1)
    branch = lax.broadcasted_iota(jnp.int32, (BRANCH, ROWS), 0)
    pick = (column == branch * DRAFT + kept_column - 1) & (kept_column > 0)
    picked = dot(pick.astype(BF16), normed.astype(BF16))
    return jnp.where(kept_column > 0, picked, prior.astype(F32)).astype(BF16)


def head_ones(size):
    return (
        lax.broadcasted_iota(jnp.int32, (size, size), 0) // HEAD
        == lax.broadcasted_iota(jnp.int32, (size, size), 1) // HEAD
    ).astype(BF16)


def per_head(value):
    ones = head_ones(256)
    return jnp.concatenate([dot(value[:, :256], ones), dot(value[:, 256:], ones)], axis=1)


def per_head_fine(value):
    top = value.astype(BF16)
    rest = (value - top.astype(F32)).astype(BF16)
    return per_head(top) + per_head(rest)


def two_heads(page):
    side = lax.broadcasted_iota(jnp.int32, (HEAD, 128), 1) < HEAD
    none = jnp.zeros_like(page)
    return jnp.concatenate([jnp.where(side, page, none), jnp.where(side, none, page)], axis=0)


META = ("slots", TOK), ("owner_of", REQ), ("page_of", BRANCH), ("winner", REQ), ("kept", REQ), ("pick", TOK), ("source", TOK), ("hit", TOK), ("dense", 1)


def starts():
    at, result = 0, {}
    for name, count in META:
        result[name] = at
        at += count
    return result


def row_stats(value_ref, mean, scale):
    step = 64

    @pl.loop(0, ROWS // step)
    def _(k):
        rows = pl.ds(pl.multiple_of(k * step, step), step)
        value = value_ref[rows].astype(F32)
        middle = jnp.mean(value, axis=-1, keepdims=True)
        centered = value - middle
        spread = jnp.mean(centered * centered, axis=-1, keepdims=True)
        mean[rows] = middle
        scale[rows] = lax.rsqrt(spread + EPSILON)


def layer_kernel(
    meta, store, packed, spot, dense_own, priors, scales, blends, narrow, widen, baseline, boost, kept_column,
    attention_w, result_w, lookup_w, gating_w, content_w,
    out, shift_att, shift_ffn, store_out,
    whole, residuals, results, lookups, gatings, contents, wbuf, part,
    mated, sums, halves, full, rsend, rrecv,
    own, residual, parcels, psend, precv, plocal, gsend, grecv, glocal,
    out_pages, in_pages, tsend, trecv, tlocal, made, returned, bsend, brecv, blocal,
    acc, low, w_s, y_s, p_s, ffn, mean, scale, wsend, wrecv, wlocal, wsem,
):
    base = starts()
    word = lambda name, index: meta[base[name] + index]
    t, g = lax.axis_index("tok"), lax.axis_index("grp")
    mine = block_of(g)
    greet(tok_peers() + grp_peers())

    def load(k):
        rows = pl.ds(pl.multiple_of(k * WIDTH, WIDTH), WIDTH)
        slot = lax.rem(k, 2)
        return pltpu.make_async_copy(attention_w.at[:, rows], wbuf.at[slot], wsem.at[slot])

    keep = pltpu.make_async_copy(packed.at[t], parcels.at[t], plocal)
    keep.start()
    copies = []
    for k in range(1, TOK):
        peer = lax.rem(t + k, TOK)
        copy = remote(packed.at[peer], parcels.at[t], psend.at[k - 1], precv.at[k - 1], {"tok": peer})
        copy.start()
        copies.append(copy)
    load(0).start()
    load(1).start()
    res, look, gat, con = [
        gather_tok(w, views(all_of), wsend.at[k], wrecv.at[k], wlocal.at[k])
        for k, (w, views, all_of) in enumerate(
            (
                (result_w, result_views, results),
                (lookup_w, stack_views, lookups),
                (gating_w, stack_views, gatings),
                (content_w, result_views, contents),
            )
        )
    ]
    res[0]()

    @pl.loop(0, TOK)
    def _(peer):
        page = store[word("slots", peer)]

        def put(pair, row, value):
            out_pages[peer, pair, pl.ds(row, 16)] = value.astype(BF16)

        pair_page(page, put)

    trade = trade_start(out_pages, in_pages, tsend, trecv, tlocal)
    look[0]()
    own[ROWS:] = priors[...]
    slots = lax.broadcasted_iota(jnp.int32, (ROWS, TOK * SPACE), 1)
    choice = (slots == spot[...]).astype(BF16)
    keep.wait()
    for k in range(1, TOK):
        origin = lax.rem(t + TOK - k, TOK)
        remote(packed.at[t], parcels.at[origin], psend.at[k - 1], precv.at[k - 1], {"tok": origin}).wait_recv()
    picked = dot(choice, parcels[...].reshape(TOK * SPACE, WIDTH)).astype(BF16)
    own[:ROWS] = jnp.where(word("dense", 0) > 0, dense_own[...], picked)
    gather_grp(own, whole, gsend, grecv, glocal, [res[1], look[1]])
    for copy in copies:
        copy.wait_send()

    row_stats(whole, mean, scale)
    acc[...] = jnp.zeros_like(acc)
    low[...] = jnp.zeros_like(low)
    res[2]()
    gat[0]()

    shape3 = (BRANCH, DRAFT, WIDTH)
    flat = lambda value: value.reshape(ROWS, WIDTH)

    def mix(k):
        load(k).wait()
        columns = block_of(k)
        weights = wbuf.at[lax.rem(k, 2)]
        prior = whole[ROWS : ROWS + BRANCH, columns]
        normed, delta = normed_and_step(whole[:ROWS, columns], prior, mean[...], scale[...], scales[0:1, columns])

        @pl.when(k == g)
        def _():
            shift_att[...] = kept_row(normed, prior, kept_column[...])

        blend = blends[:, columns]
        for c in range(4):
            acc[c] += dot((normed + delta * blend[c : c + 1]).astype(BF16), weights[c]).reshape(shape3)
        low[...] += dot((normed + delta * blend[4:5]).astype(BF16), narrow[columns])

        @pl.when(k < GRP - 2)
        def _():
            load(k + 2).start()

    pl.loop(0, 4)(mix)
    look[2]()
    res[3]()
    pl.loop(4, 8)(mix)
    gat[1]()
    trade_end(out_pages, in_pages, tsend, trecv, trade)

    lowrank = jnp.tanh(low[...]).astype(BF16)
    w_s[...] = jnp.exp(-jnp.exp(baseline[:, mine] + dot(lowrank, widen[...]))).reshape(shape3)
    position = lax.broadcasted_iota(jnp.int32, shape3, 1)
    r3, k3, v3, w3 = acc[0], acc[1], acc[2], w_s[...]
    y_s[...] = per_head_fine(flat(r3) * boost[:, mine] * flat(k3)) * flat(v3)
    p_s[...] = jnp.ones_like(p_s)
    for s in range(DRAFT - 2, -1, -1):
        decay = jnp.where(position > s + 1, p_s[...].reshape(shape3) * w3[:, s + 1 : s + 2], 1.0)
        p_s[...] = decay.reshape(ROWS, WIDTH)
        term = jnp.where(position > s, r3 * decay * k3[:, s : s + 1], 0.0)
        score = per_head(term.reshape(ROWS, WIDTH).astype(BF16)).reshape(shape3)
        y_s[...] += (score * v3[:, s : s + 1]).reshape(ROWS, WIDTH)
    decay = jnp.where(position > 0, p_s[...].reshape(shape3) * w3[:, 0:1], 1.0)
    p_s[...] = flat(r3 * decay)

    @pl.loop(0, BRANCH)
    def _(b):
        rows = pl.ds(pl.multiple_of(b * DRAFT, DRAFT), DRAFT)
        page = in_pages[word("page_of", b)]
        for pair in range(PAIRS):
            lanes = pl.ds(pair * 128, 128)
            y_s[rows, lanes] += dot(p_s[rows, lanes].astype(BF16), two_heads(page[pair]))

    con[0]()
    value = y_s[...]
    centered = value - per_head_fine(value) * (1.0 / HEAD)
    spread = per_head_fine(centered * centered) * (1.0 / HEAD)
    gate = flat(acc[3])
    gate = gate * jax.nn.sigmoid(gate)
    attended = (centered * lax.rsqrt(spread + HEAD_EPSILON) * scales[2:3, mine] * gate).astype(BF16)
    res[4]()
    for y_of in range(4):
        part[:, y_of * 1024 : y_of * 1024 + 1024] = dot(attended, results[y_of]).astype(BF16)

    def states():
        eye = (
            lax.broadcasted_iota(jnp.int32, (128, 128), 0)
            == lax.broadcasted_iota(jnp.int32, (128, 128), 1)
        )
        spot16 = lax.broadcasted_iota(jnp.int32, (DRAFT, WIDTH), 0)
        side = lax.broadcasted_iota(jnp.int32, (HEAD, 128), 1) < HEAD

        @pl.loop(0, REQ)
        def _(q):
            b = word("winner", q)
            count = word("kept", q)
            live = spot16 < count
            tail = jnp.where(live, w_s[b], 1.0)
            for hop in (1, 2, 4, 8):
                later = pltpu.roll(tail, DRAFT - hop, axis=0)
                tail = tail * jnp.where(spot16 < DRAFT - hop, later, 1.0)
            after = jnp.where(spot16 < DRAFT - 1, pltpu.roll(tail, DRAFT - 1, axis=0), 1.0)
            keys = jnp.where(live, acc[1, b], 0.0) * after
            values = acc[2, b].astype(BF16)
            page = in_pages[word("owner_of", q)]
            for pair in range(PAIRS):
                lanes = slice(pair * 128, pair * 128 + 128)
                fade = jnp.where(eye, tail[0:1, lanes], 0.0)
                left = jnp.concatenate([keys[:, lanes], fade], axis=0).astype(BF16)
                right = jnp.concatenate([values[:, lanes], two_heads(page[pair])], axis=0)
                both = lax.dot_general(left, right, (((0,), (0,)), ((), ())), preferred_element_type=F32)
                made[q, pair] = jnp.where(side, both[:HEAD], both[HEAD:]).astype(BF16)

        @pl.loop(0, TOK)
        def _(peer):
            out_pages[peer] = made[word("pick", peer)]

        trades.append(trade_start(out_pages, returned, bsend, brecv, blocal))

    trades = []
    total = reduce_grp(part, mated, sums, halves, full, rsend, rrecv, states)
    residual[...] = (own[:ROWS].astype(F32) + total).astype(BF16)
    gather_grp(residual, residuals, gsend, grecv, glocal, [look[3], gat[2]])
    row_stats(residuals, mean, scale)
    con[1]()
    gat[3]()

    ffn[...] = jnp.zeros_like(ffn)
    look[4]()
    con[2]()
    gat[4]()

    @pl.loop(0, GRP)
    def _(k):
        columns = block_of(k)
        prior = whole[ROWS + BRANCH :, columns]
        normed, delta = normed_and_step(residuals[:, columns], prior, mean[...], scale[...], scales[1:2, columns])

        @pl.when(k == g)
        def _():
            shift_ffn[...] = kept_row(normed, prior, kept_column[...])

        blend = blends[:, columns]
        y_of, x_of = k // 2, pl.ds(lax.rem(k, 2) * 2, 2)
        ffn[:, :KEYS] += dot(
            (normed + delta * blend[5:6]).astype(BF16), lookups[y_of, x_of].reshape(WIDTH, KEYS)
        )
        ffn[:, KEYS:] += dot(
            (normed + delta * blend[6:7]).astype(BF16), gatings[y_of, x_of].reshape(WIDTH, WIDTH)
        )

    trade_end(out_pages, returned, bsend, brecv, trades[0])
    hidden = jnp.square(jnp.maximum(ffn[:, :KEYS], 0.0)).astype(BF16)
    con[3]()
    con[4]()
    for y_of in range(4):
        part[:, y_of * 1024 : y_of * 1024 + 1024] = dot(hidden, contents[y_of]).astype(BF16)

    def pages():
        @pl.loop(0, TOK)
        def _(slot):
            page = returned[word("source", slot)].astype(F32)
            taken = word("hit", slot) > 0

            def put(column, value):
                columns = pl.ds(column, 128)
                store_out[slot, :, columns] = jnp.where(taken, value, store[slot, :, columns])

            flat_page(page, put)

    total = reduce_grp(part, mated, sums, halves, full, rsend, rrecv, pages)
    out[...] = (residual[...].astype(F32) + jax.nn.sigmoid(ffn[:, KEYS:]) * total).astype(BF16)


def layer(meta, store, packed, spot, dense_own, priors, scales, blends, narrow, widen, baseline, boost, kept_column, *weights):
    rows = ROWS + 2 * BRANCH
    wide = lambda *shape: pltpu.VMEM(shape, BF16)
    fine = lambda *shape: pltpu.VMEM(shape, F32)
    dma = lambda *shape: pltpu.SemaphoreType.DMA(shape)
    return pl.pallas_call(
        layer_kernel,
        out_shape=(
            jax.ShapeDtypeStruct((ROWS, WIDTH), BF16),
            jax.ShapeDtypeStruct((BRANCH, WIDTH), BF16),
            jax.ShapeDtypeStruct((BRANCH, WIDTH), BF16),
            jax.ShapeDtypeStruct(store.shape, F32),
        ),
        in_specs=[pl.BlockSpec(memory_space=pltpu.SMEM)] + [VMEM] * 12 + [ANY] * 5,
        out_specs=(VMEM, VMEM, VMEM, VMEM),
        scratch_shapes=[
            wide(rows, HIDDEN),
            wide(ROWS, HIDDEN),
            wide(4, WIDTH, 1024),
            wide(4, 4, 256, KEYS),
            wide(4, 4, 256, WIDTH),
            wide(4, KEYS, 1024),
            wide(2, 4, WIDTH, WIDTH),
            wide(ROWS, HIDDEN),
            *REDUCE_SCRATCH,
            wide(rows, WIDTH),
            wide(ROWS, WIDTH),
            wide(TOK, SPACE, WIDTH),
            dma(TOK - 1),
            dma(TOK - 1),
            pltpu.SemaphoreType.DMA,
            dma(9),
            dma(9),
            pltpu.SemaphoreType.DMA,
            wide(TOK, PAIRS, HEAD, 128),
            wide(TOK, PAIRS, HEAD, 128),
            *TRADE_SEMAPHORES,
            wide(REQ, PAIRS, HEAD, 128),
            wide(TOK, PAIRS, HEAD, 128),
            *TRADE_SEMAPHORES,
            fine(4, BRANCH, DRAFT, WIDTH),
            fine(ROWS, 128),
            fine(BRANCH, DRAFT, WIDTH),
            fine(ROWS, WIDTH),
            fine(ROWS, WIDTH),
            fine(ROWS, KEYS + WIDTH),
            fine(ROWS, 1),
            fine(ROWS, 1),
            dma(4, 16),
            dma(4, 16),
            dma(4),
            dma(2),
        ],
        compiler_params=pltpu.CompilerParams(
            collective_id=2, has_side_effects=True, vmem_limit_bytes=60 << 20
        ),
        cost_estimate=pl.CostEstimate(flops=12 << 30, transcendentals=1 << 20, bytes_accessed=60 << 20),
        name="layer",
    )(meta, store, packed, spot, dense_own, priors, scales, blends, narrow, widen, baseline, boost, kept_column, *weights)


def body(
    guess_symbol_ids,
    symbol_vector_lookup,
    prior_attention_normed,
    prior_feedforward_normed,
    layernorm_scales,
    lagged_blend_ratios,
    attention_matrices,
    forgetting_baseline_vector,
    forgetting_narrow_matrix,
    forgetting_widen_matrix,
    diagonal_boost,
    attention_result_matrix,
    feedforward_lookup_matrix,
    feedforward_content_matrix,
    feedforward_gating_matrix,
    memory_matrix_store,
    query_memory_slot,
    candidate_tally_each_query,
    kept_guess_tally,
):
    tok_at = lax.axis_index("tok")
    vocab_rows = symbol_vector_lookup.shape[0]
    slot_count = memory_matrix_store.shape[0]

    priors = jnp.concatenate([prior_attention_normed, prior_feedforward_normed], axis=0)

    owners = (query_memory_slot // slot_count).reshape(TOK, REQ)
    places = (query_memory_slot % slot_count).reshape(TOK, REQ)
    owned_here = owners == tok_at
    send_slot = jnp.sum(jnp.where(owned_here, places, 0), axis=1)
    sending = jnp.any(owned_here, axis=1)
    packed, spot, most = pack(
        tok_at.reshape(1), guess_symbol_ids.reshape(TOK, ROWS), symbol_vector_lookup
    )

    crowded = most[0, 0] > SPACE

    def dense(_):
        wanted = guess_symbol_ids - tok_at * vocab_rows
        inside = (wanted >= 0) & (wanted < vocab_rows)
        found = jnp.take(symbol_vector_lookup, jnp.clip(wanted, 0, vocab_rows - 1), axis=0)
        found = jnp.where(inside[:, None], found, jnp.zeros((), BF16)).reshape(4, 4, ROWS, WIDTH)
        return dense_exchange(found)

    dense_own = lax.cond(crowded, dense, lambda _: jnp.zeros((ROWS, WIDTH), BF16), 0)

    my_owners = lax.dynamic_index_in_dim(owners, tok_at, 0, keepdims=False)
    my_counts = lax.dynamic_index_in_dim(candidate_tally_each_query, tok_at, 0, keepdims=False)
    local_ids = jnp.arange(BRANCH, dtype=jnp.int32)
    request_ends = jnp.cumsum(my_counts)
    request_of = jnp.sum((request_ends[None, :] <= local_ids[:, None]).astype(jnp.int32), axis=1)
    branch_score = kept_guess_tally * BRANCH + (BRANCH - 1 - local_ids)
    member = request_of[None, :] == jnp.arange(REQ, dtype=jnp.int32)[:, None]
    best_score = jnp.max(jnp.where(member, branch_score[None, :], -1), axis=1)
    winner = BRANCH - 1 - best_score % BRANCH

    targets = my_owners[None, :] == jnp.arange(TOK, dtype=jnp.int32)[:, None]
    pick_index = jnp.sum(
        jnp.where(targets, jnp.arange(REQ, dtype=jnp.int32)[None, :], 0), axis=1
    )
    hit = (send_slot[None, :] == jnp.arange(slot_count, dtype=jnp.int32)[:, None]) & sending[None, :]
    source = jnp.sum(jnp.where(hit, jnp.arange(TOK, dtype=jnp.int32)[None, :], 0), axis=1)
    meta = jnp.concatenate(
        [
            send_slot, my_owners, my_owners[request_of], winner, kept_guess_tally[winner], pick_index, source,
            jnp.any(hit, axis=1).astype(jnp.int32), crowded.astype(jnp.int32).reshape(1),
        ]
    )
    layer_out, shift_att_out, shift_ffn_out, store_out = layer(
        meta, memory_matrix_store, packed.reshape(TOK, SPACE, WIDTH), spot, dense_own, priors,
        layernorm_scales, lagged_blend_ratios, forgetting_narrow_matrix, forgetting_widen_matrix,
        forgetting_baseline_vector.reshape(1, HIDDEN), diagonal_boost.reshape(1, HIDDEN),
        kept_guess_tally.reshape(BRANCH, 1), attention_matrices, attention_result_matrix,
        feedforward_lookup_matrix, feedforward_gating_matrix, feedforward_content_matrix,
    )
    return (layer_out, shift_att_out, shift_ffn_out, store_out)


def solution(mesh):
    in_specs = (
        P(),
        P("tok", "grp"),
        P("tok", "grp"),
        P("tok", "grp"),
        P(),
        P(),
        P(None, None, "grp"),
        P(),
        P(),
        P(None, "grp"),
        P(),
        P("grp", "tok"),
        P("tok", "grp"),
        P("grp", "tok"),
        P("tok", "grp"),
        P("tok", "grp", None),
        P(),
        P(),
        P("tok"),
    )
    out_specs = (P("tok", "grp"), P("tok", "grp"), P("tok", "grp"), P("tok", "grp", None))
    return jax.shard_map(body, mesh=mesh, in_specs=in_specs, out_specs=out_specs, check_vma=False)
```

time: 225 us -> 223 us (level)
  Pallas kernels: 179 us -> 203 us
  between operations: 15.1 us -> 1.41 us
  waiting for transfers between devices: 10.8 us -> 0 us
  other arithmetic: 5.8 us -> 2.86 us
    pallas_call x5 -> x1, Pallas kernels: 169 us -> 192 us  [layer(): pl.pallas_call(layer_kernel, out_shape=(jax.ShapeDtypeStruct((ROWS, WIDTH...]
    all_gather x1 -> x0, waiting for transfers between devices: 10.8 us -> none  [body(): lax.all_gather(jnp.concatenate([feedforward_content_matrix.T, feedforward...]
    unnamed x56 -> x20, local copies, waits for them, and re-layouts: 8.28 us -> 9.65 us
  transfers between devices with their start and end apart: 1 -> 0, of which waited for: 1 -> 0; matrix products, arithmetic and copies ran while one was open for 4% -> 0% of each run, Pallas kernels for 65% -> 0%
where the time goes in v3:
time: 223 us; the launch traced here: 222 us
  Pallas kernels  203 us (91%)
  local copies, waits for them, and re-layouts  14.7 us (7%)
  other arithmetic  2.86 us (1%)
    pallas_call x1, Pallas kernels, layer(): pl.pallas_call(layer_kernel, out_shape=(jax.ShapeDtypeStruct((ROWS, WIDTH...  192 us
    pallas_call x1, Pallas kernels, pack(): pl.pallas_call(pack_kernel, out_shape=(jax.ShapeDtypeStruct((TOK * SPACE,...  10.5 us
    unnamed x20, local copies, waits for them, and re-layouts  9.65 us

profile of v3, /device:TPU:1, one launch (start us, length us, event | category | flops | bytes accessed | tf_op | source)
XLA Modules:
  0.0 221.9 jit_solution(12851879268600957577)
XLA Ops:
  0.6 0.0 copy-start
  0.6 0.7 and_select_fusion.2
  1.3 0.1 reshape.147
  1.4 0.1 fusion.8
  1.5 0.1 reshape.148
  1.6 0.1 select_reduce_fusion.1
  1.7 0.0 copy-done
  1.7 0.2 dynamic-slice_reduce_fusion
  1.9 0.2 reduce-window.8
  2.1 0.1 convert_reduce_fusion
  2.2 0.7 gather_fusion.1
  2.9 0.7 subtract_add_fusion
  3.6 0.1 select_reduce_fusion.3
  3.7 0.0 copy-start.4
  3.7 0.0 copy-start.5
  3.7 1.4 gather_fusion.2
  5.2 0.1 select_reduce_fusion
  5.3 0.1 fusion.2
  5.4 0.7 reshape.152.ids
  6.2 10.5 %pack.1 = (bf16[768,512]{1,0:T(8,128)(2,1)S(1)}, s32[256,1]{1,0:T(8,128)S(1)}, s32[8,128]{1,0:T(8,128)S(1)}) custom-call(s32[1]{0:T(128)} %bitcast.7.place, s32[16,256]{1,0:T(8,128)S(1)} %reshape.152.ids, bf16[2048,512]{1,0:T(8,128)(2,1)} %table.1), custom_call_target="tpu_custom_call" | custom-call | flops 2147483648 | bytes 4194304 | tf_op jit(solution)/shard_map/pack/pallas_call | solution.py:503
  16.7 0.0 copy-start.1
  16.7 0.9 copy-done.1
  17.6 0.0 copy-start.2
  17.6 0.7 copy-done.2
  18.2 0.5 slice.3
  19.4 0.6 concatenate.6.meta
  20.0 0.0 copy-done.4
  20.0 0.0 copy-done.5
  20.0 0.0 copy-start.6
  20.0 0.0 copy-start.7
  20.0 0.0 copy-start.3
  20.1 0.6 copy-done.6
  20.7 0.0 copy-done.7
  20.7 0.6 pad_maximum_fusion.priors
  21.3 0.0 copy-done.3
  21.3 0.7 copy.25.kept_column
  22.0 192.5 %layer.1 = (bf16[256,512]{1,0:T(8,128)(2,1)}, bf16[16,512]{1,0:T(8,128)(2,1)}, bf16[16,512]{1,0:T(8,128)(2,1)}, f32[16,8,4096]{2,1,0:T(8,128)}) custom-call(s32[105]{0:T(128)} %concatenate.6.meta, f32[16,8,4096]{2,1,0:T(8,128)} %store.1, bf16[16,48,512]{2,1,0:T(8,128)(2,1)} %bitcast.22, s32[256,1]{1,0:T(8,128)} %copy-done.2, ...), custom_call_target="tpu_custom_call" | custom-call | flops 12884901888 | bytes 62914560 | tf_op jit(solution)/shard_map/layer/pallas_call | solution.py:825
  214.5 1.7 copy.32
  216.2 1.3 copy.33
  217.5 1.3 copy.34
  218.8 3.1 %copy.35 = f32[16,8,4096]{2,1,0:T(8,128)} copy(f32[16,8,4096]{2,1,0:T(8,128)} %get-tuple-element.37) | data formatting | bytes 4194304
  (9 shorter events, 0.1 us)
Async XLA Ops:
  0.6 1.1 copy-start
  3.7 16.3 %copy-start.4 = (bf16[2048,512]{1,0:T(8,128)(2,1)S(1)}, bf16[2048,512]{1,0:T(8,128)(2,1)}, u32[]{:S(2)}) copy-start(bf16[2048,512]{1,0:T(8,128)(2,1)} %table.1) | copy-start | bytes 6291460
  3.7 16.3 %copy-start.5 = (s32[4096]{0:T(1024)S(1)}, s32[4096]{0:T(1024)}, u32[]{:S(2)}) copy-start(s32[4096]{0:T(1024)} %param.21) | copy-start | bytes 49156
  16.7 0.9 copy-start.1
  17.6 0.7 copy-start.2
  20.0 0.7 copy-start.6
  20.0 0.7 copy-start.7
  20.0 1.3 copy-start.3

commit v4 on v3

--- a/solution.py
+++ b/solution.py
@@ -18,7 +18,7 @@
 REQ = 8
 PAIRS = 4
 KEYS = 896
-SPACE = 48
+SPACE = 32
 EPSILON = 1e-05
 HEAD_EPSILON = 0.00064
 F32 = jnp.float32
@@ -450,70 +450,83 @@
     )(found)
 
 
-def pack_kernel(place, ids, table, packed, spot, most, slot_s):
-    t_at = place[0]
+def pack_rows(ids, table, packed, spot_row, slot_s):
+    t_at = lax.axis_index("tok")
     shape = (ROWS, ROWS)
     sub = lax.broadcasted_iota(jnp.int32, shape, 0)
     lane = lax.broadcasted_iota(jnp.int32, shape, 1)
     vocab_rows = table.shape[0]
-    base = t_at * vocab_rows
-
-    def column(row):
-        return jnp.sum(jnp.where(sub == lane, jnp.broadcast_to(row, shape), 0), axis=1, keepdims=True)
-
-    def ranks(row):
-        col = column(row)
-        same = col == row
-        first_col = 1 - jnp.max(jnp.where(same & (lane < sub), 1, 0), axis=1, keepdims=True)
-        first_row = 1 - jnp.max(jnp.where(same & (sub < lane), 1, 0), axis=0, keepdims=True)
-        start = row - lax.rem(row, vocab_rows)
-        ahead = (col < row) & (col >= start)
-        rank = jnp.sum(jnp.where(ahead, first_col, 0), axis=0, keepdims=True)
-        return first_row, start, rank
-
-    def one(t, top):
-        row = ids[pl.ds(t, 1), :]
-        first_row, start, rank = ranks(row)
-        mine = (first_row > 0) & (start == base)
-        slot = lax.broadcasted_iota(jnp.int32, (SPACE, ROWS), 0)
-        hit = (slot == rank) & mine
-        slot_s[pl.ds(pl.multiple_of(t * SPACE, SPACE), SPACE)] = (
-            jnp.sum(jnp.where(hit, row - base + 1, 0), axis=1, keepdims=True) - 1
-        )
-
-        @pl.when(t == t_at)
+    base = (t_at * vocab_rows).astype(F32)
+    symbols = ids[...]
+    owners = symbols // vocab_rows
+    values = symbols.astype(F32)
+    begins = (owners * vocab_rows).astype(F32)
+    columns = jnp.transpose(values)
+    slot = lax.broadcasted_iota(jnp.int32, (SPACE, ROWS), 0).astype(F32)
+    ones = jnp.ones((8, ROWS), BF16)
+    yes = lambda mask: jnp.where(mask, 1.0, 0.0).astype(BF16)
+    for t in range(TOK):
+        row, begin = values[t : t + 1], begins[t : t + 1]
+        col = jnp.broadcast_to(columns[:, t : t + 1], shape)
+        earlier = dot(ones, yes((col == row) & (sub < lane)))
+        first = jnp.where(earlier < 0.5, 1.0, 0.0)
+        rank = dot(first.astype(BF16), yes((col < row) & (col >= begin)))[0:1]
+        mine = (first[0:1] > 0.5) & (begin == base)
+        found = jnp.where((slot == rank) & mine, row - base + 1.0, 0.0)
+        slot_s[t * SPACE : t * SPACE + SPACE] = jnp.sum(found, axis=1, keepdims=True) - 1.0
+
+        @pl.when(t_at == t)
         def _():
-            owner = start // vocab_rows
-            spot[...] = column(owner * SPACE + rank)
-
-        return jnp.maximum(top, rank)
-
-    top = lax.fori_loop(0, TOK, one, jnp.zeros((1, ROWS), jnp.int32))
-    most[...] = jnp.broadcast_to(jnp.max(top, axis=1, keepdims=True) + 1, (8, 128))
+            spot_row[...] = jnp.broadcast_to(begin * (SPACE / vocab_rows) + rank, (8, ROWS))
+
     step = 256
     for k in range(TOK * SPACE // step):
         rows = pl.ds(k * step, step)
-        pick = (
-            lax.broadcasted_iota(jnp.int32, (step, vocab_rows), 1) == slot_s[rows]
-        ).astype(BF16)
-        packed[rows] = dot(pick, table[...]).astype(BF16)
-
-
-def pack(place, ids, table):
+        numbers = lax.broadcasted_iota(jnp.int32, (step, vocab_rows), 1).astype(F32)
+        value = dot(yes(numbers == slot_s[rows]), table[...]).astype(BF16)
+        many = step // SPACE
+        packed[k * many : k * many + many] = value.reshape(many, SPACE, WIDTH)
+    return jnp.transpose(spot_row[...])[:, 0:1]
+
+
+def finish_kernel(source, hit, made_out, made_att, made_ffn, returned, store, out, shift_att, shift_ffn, store_out):
+    step = pl.program_id(0)
+
+    @pl.when(step == 0)
+    def _():
+        out[...] = made_out[...]
+        shift_att[...] = made_att[...]
+        shift_ffn[...] = made_ffn[...]
+
+    for k in range(4):
+        slot = step * 4 + k
+        page = returned[source[slot]].astype(F32)
+        taken = hit[slot] > 0
+
+        def put(column, value):
+            columns = slice(column, column + 128)
+            store_out[k, :, columns] = jnp.where(taken, value, store[k, :, columns])
+
+        flat_page(page, put)
+
+
+def finish(source, hit, made_out, made_att, made_ffn, returned, store):
+    full = lambda *shape: pl.BlockSpec(shape, lambda k, *_: (0,) * len(shape))
+    slots = pl.BlockSpec((4, REQ, HIDDEN), lambda k, *_: (k, 0, 0))
     return pl.pallas_call(
-        pack_kernel,
-        out_shape=(
-            jax.ShapeDtypeStruct((TOK * SPACE, WIDTH), BF16),
-            jax.ShapeDtypeStruct((ROWS, 1), jnp.int32),
-            jax.ShapeDtypeStruct((8, 128), jnp.int32),
+        finish_kernel,
+        out_shape=tuple(jax.ShapeDtypeStruct(v.shape, v.dtype) for v in (made_out, made_att, made_ffn, store)),
+        grid_spec=pltpu.PrefetchScalarGridSpec(
+            num_scalar_prefetch=2,
+            grid=(4,),
+            in_specs=[
+                full(ROWS, WIDTH), full(BRANCH, WIDTH), full(BRANCH, WIDTH),
+                full(TOK, PAIRS, HEAD, 128), slots,
+            ],
+            out_specs=(full(ROWS, WIDTH), full(BRANCH, WIDTH), full(BRANCH, WIDTH), slots),
         ),
-        in_specs=[pl.BlockSpec(memory_space=pltpu.SMEM), VMEM, VMEM],
-        out_specs=(VMEM, VMEM, VMEM),
-        scratch_shapes=[pltpu.VMEM((TOK * SPACE, 1), jnp.int32)],
-        compiler_params=pltpu.CompilerParams(vmem_limit_bytes=32 << 20),
-        cost_estimate=pl.CostEstimate(flops=2 << 30, transcendentals=0, bytes_accessed=4 << 20),
-        name="pack",
-    )(place, ids, table)
+        name="finish",
+    )(source, hit, made_out, made_att, made_ffn, returned, store)
 
 
 def dot(a, b):
@@ -564,7 +577,7 @@
     return jnp.concatenate([jnp.where(side, page, none), jnp.where(side, none, page)], axis=0)
 
 
-META = ("slots", TOK), ("owner_of", REQ), ("page_of", BRANCH), ("winner", REQ), ("kept", REQ), ("pick", TOK), ("source", TOK), ("hit", TOK), ("dense", 1)
+META = ("slots", TOK), ("owner_of", REQ), ("page_of", BRANCH), ("winner", REQ), ("kept", REQ), ("pick", TOK), ("dense", 1)
 
 
 def starts():
@@ -590,19 +603,24 @@
 
 
 def layer_kernel(
-    meta, store, packed, spot, dense_own, priors, scales, blends, narrow, widen, baseline, boost, kept_column,
-    attention_w, result_w, lookup_w, gating_w, content_w,
-    out, shift_att, shift_ffn, store_out,
+    meta, ids, dense_own, priors, scales, blends, narrow, widen, baseline, boost, kept_column,
+    store_w, table_w, attention_w, result_w, lookup_w, gating_w, content_w,
+    out, shift_att, shift_ffn, returned,
+    store, table, packed, spot_row, slot_s, lsem,
     whole, residuals, results, lookups, gatings, contents, wbuf, part,
     mated, sums, halves, full, rsend, rrecv,
     own, residual, parcels, psend, precv, plocal, gsend, grecv, glocal,
-    out_pages, in_pages, tsend, trecv, tlocal, made, returned, bsend, brecv, blocal,
+    out_pages, in_pages, tsend, trecv, tlocal, made, bsend, brecv, blocal,
     acc, low, w_s, y_s, p_s, ffn, mean, scale, wsend, wrecv, wlocal, wsem,
 ):
     base = starts()
     word = lambda name, index: meta[base[name] + index]
     t, g = lax.axis_index("tok"), lax.axis_index("grp")
     mine = block_of(g)
+    bring_table = pltpu.make_async_copy(table_w, table, lsem.at[0])
+    bring_store = pltpu.make_async_copy(store_w, store, lsem.at[1])
+    bring_table.start()
+    bring_store.start()
     greet(tok_peers() + grp_peers())
 
     def load(k):
@@ -610,16 +628,6 @@
         slot = lax.rem(k, 2)
         return pltpu.make_async_copy(attention_w.at[:, rows], wbuf.at[slot], wsem.at[slot])
 
-    keep = pltpu.make_async_copy(packed.at[t], parcels.at[t], plocal)
-    keep.start()
-    copies = []
-    for k in range(1, TOK):
-        peer = lax.rem(t + k, TOK)
-        copy = remote(packed.at[peer], parcels.at[t], psend.at[k - 1], precv.at[k - 1], {"tok": peer})
-        copy.start()
-        copies.append(copy)
-    load(0).start()
-    load(1).start()
     res, look, gat, con = [
         gather_tok(w, views(all_of), wsend.at[k], wrecv.at[k], wlocal.at[k])
         for k, (w, views, all_of) in enumerate(
@@ -632,6 +640,22 @@
         )
     ]
     res[0]()
+    look[0]()
+    load(0).start()
+    load(1).start()
+    bring_table.wait()
+    spot = pack_rows(ids, table, packed, spot_row, slot_s)
+    keep = pltpu.make_async_copy(packed.at[t], parcels.at[t], plocal)
+    keep.start()
+    copies = []
+    for k in range(1, TOK):
+        peer = lax.rem(t + k, TOK)
+        copy = remote(packed.at[peer], parcels.at[t], psend.at[k - 1], precv.at[k - 1], {"tok": peer})
+        copy.start()
+        copies.append(copy)
+    con[0]()
+    gat[0]()
+    bring_store.wait()
 
     @pl.loop(0, TOK)
     def _(peer):
@@ -642,27 +666,30 @@
 
         pair_page(page, put)
 
-    trade = trade_start(out_pages, in_pages, tsend, trecv, tlocal)
-    look[0]()
+    res[1]()
+    look[1]()
     own[ROWS:] = priors[...]
     slots = lax.broadcasted_iota(jnp.int32, (ROWS, TOK * SPACE), 1)
-    choice = (slots == spot[...]).astype(BF16)
+    choice = (slots == spot.astype(jnp.int32)).astype(BF16)
     keep.wait()
     for k in range(1, TOK):
         origin = lax.rem(t + TOK - k, TOK)
         remote(packed.at[t], parcels.at[origin], psend.at[k - 1], precv.at[k - 1], {"tok": origin}).wait_recv()
     picked = dot(choice, parcels[...].reshape(TOK * SPACE, WIDTH)).astype(BF16)
     own[:ROWS] = jnp.where(word("dense", 0) > 0, dense_own[...], picked)
-    gather_grp(own, whole, gsend, grecv, glocal, [res[1], look[1]])
+    trades = []
+
+    def bring():
+        res[2]()
+        trades.append(trade_start(out_pages, in_pages, tsend, trecv, tlocal))
+
+    gather_grp(own, whole, gsend, grecv, glocal, [bring, look[2]])
     for copy in copies:
         copy.wait_send()
 
     row_stats(whole, mean, scale)
     acc[...] = jnp.zeros_like(acc)
     low[...] = jnp.zeros_like(low)
-    res[2]()
-    gat[0]()
-
     shape3 = (BRANCH, DRAFT, WIDTH)
     flat = lambda value: value.reshape(ROWS, WIDTH)
 
@@ -687,11 +714,9 @@
             load(k + 2).start()
 
     pl.loop(0, 4)(mix)
-    look[2]()
     res[3]()
     pl.loop(4, 8)(mix)
-    gat[1]()
-    trade_end(out_pages, in_pages, tsend, trecv, trade)
+    trade_end(out_pages, in_pages, tsend, trecv, trades[0])
 
     lowrank = jnp.tanh(low[...]).astype(BF16)
     w_s[...] = jnp.exp(-jnp.exp(baseline[:, mine] + dot(lowrank, widen[...]))).reshape(shape3)
@@ -716,7 +741,7 @@
             lanes = pl.ds(pair * 128, 128)
             y_s[rows, lanes] += dot(p_s[rows, lanes].astype(BF16), two_heads(page[pair]))
 
-    con[0]()
+    look[3]()
     value = y_s[...]
     centered = value - per_head_fine(value) * (1.0 / HEAD)
     spread = per_head_fine(centered * centered) * (1.0 / HEAD)
@@ -728,6 +753,7 @@
         part[:, y_of * 1024 : y_of * 1024 + 1024] = dot(attended, results[y_of]).astype(BF16)
 
     def states():
+        con[2]()
         eye = (
             lax.broadcasted_iota(jnp.int32, (128, 128), 0)
             == lax.broadcasted_iota(jnp.int32, (128, 128), 1)
@@ -762,18 +788,15 @@
 
         trades.append(trade_start(out_pages, returned, bsend, brecv, blocal))
 
-    trades = []
+    con[1]()
     total = reduce_grp(part, mated, sums, halves, full, rsend, rrecv, states)
     residual[...] = (own[:ROWS].astype(F32) + total).astype(BF16)
-    gather_grp(residual, residuals, gsend, grecv, glocal, [look[3], gat[2]])
+    gather_grp(residual, residuals, gsend, grecv, glocal, [look[4], con[3]])
     row_stats(residuals, mean, scale)
-    con[1]()
-    gat[3]()
+    gat[1]()
 
     ffn[...] = jnp.zeros_like(ffn)
-    look[4]()
-    con[2]()
-    gat[4]()
+    gat[2]()
 
     @pl.loop(0, GRP)
     def _(k):
@@ -787,37 +810,32 @@
 
         blend = blends[:, columns]
         y_of, x_of = k // 2, pl.ds(lax.rem(k, 2) * 2, 2)
-        ffn[:, :KEYS] += dot(
+        ffn[...] += dot(
             (normed + delta * blend[5:6]).astype(BF16), lookups[y_of, x_of].reshape(WIDTH, KEYS)
         )
-        ffn[:, KEYS:] += dot(
-            (normed + delta * blend[6:7]).astype(BF16), gatings[y_of, x_of].reshape(WIDTH, WIDTH)
-        )
-
-    trade_end(out_pages, returned, bsend, brecv, trades[0])
-    hidden = jnp.square(jnp.maximum(ffn[:, :KEYS], 0.0)).astype(BF16)
-    con[3]()
+        residuals[:, columns] = (normed + delta * blend[6:7]).astype(BF16)
+
+    hidden = jnp.square(jnp.maximum(ffn[...], 0.0)).astype(BF16)
     con[4]()
     for y_of in range(4):
         part[:, y_of * 1024 : y_of * 1024 + 1024] = dot(hidden, contents[y_of]).astype(BF16)
 
     def pages():
-        @pl.loop(0, TOK)
-        def _(slot):
-            page = returned[word("source", slot)].astype(F32)
-            taken = word("hit", slot) > 0
-
-            def put(column, value):
-                columns = pl.ds(column, 128)
-                store_out[slot, :, columns] = jnp.where(taken, value, store[slot, :, columns])
-
-            flat_page(page, put)
+        gat[3]()
+        trade_end(out_pages, returned, bsend, brecv, trades[1])
 
     total = reduce_grp(part, mated, sums, halves, full, rsend, rrecv, pages)
-    out[...] = (residual[...].astype(F32) + jax.nn.sigmoid(ffn[:, KEYS:]) * total).astype(BF16)
-
-
-def layer(meta, store, packed, spot, dense_own, priors, scales, blends, narrow, widen, baseline, boost, kept_column, *weights):
+    gat[4]()
+    received = jnp.zeros((ROWS, WIDTH), F32)
+    for k in range(GRP):
+        received += dot(
+            residuals[:, k * WIDTH : k * WIDTH + WIDTH],
+            gatings[k // 2, k % 2 * 2 : k % 2 * 2 + 2].reshape(WIDTH, WIDTH),
+        )
+    out[...] = (residual[...].astype(F32) + jax.nn.sigmoid(received) * total).astype(BF16)
+
+
+def layer(meta, ids, dense_own, priors, scales, blends, narrow, widen, baseline, boost, kept_column, *weights):
     rows = ROWS + 2 * BRANCH
     wide = lambda *shape: pltpu.VMEM(shape, BF16)
     fine = lambda *shape: pltpu.VMEM(shape, F32)
@@ -828,11 +846,17 @@
             jax.ShapeDtypeStruct((ROWS, WIDTH), BF16),
             jax.ShapeDtypeStruct((BRANCH, WIDTH), BF16),
             jax.ShapeDtypeStruct((BRANCH, WIDTH), BF16),
-            jax.ShapeDtypeStruct(store.shape, F32),
+            jax.ShapeDtypeStruct((TOK, PAIRS, HEAD, 128), BF16),
         ),
-        in_specs=[pl.BlockSpec(memory_space=pltpu.SMEM)] + [VMEM] * 12 + [ANY] * 5,
+        in_specs=[pl.BlockSpec(memory_space=pltpu.SMEM)] + [VMEM] * 10 + [ANY] * 7,
         out_specs=(VMEM, VMEM, VMEM, VMEM),
         scratch_shapes=[
+            fine(*weights[0].shape),
+            wide(*weights[1].shape),
+            wide(TOK, SPACE, WIDTH),
+            fine(8, ROWS),
+            fine(TOK * SPACE, 1),
+            dma(2),
             wide(rows, HIDDEN),
             wide(ROWS, HIDDEN),
             wide(4, WIDTH, 1024),
@@ -855,14 +879,13 @@
             wide(TOK, PAIRS, HEAD, 128),
             *TRADE_SEMAPHORES,
             wide(REQ, PAIRS, HEAD, 128),
-            wide(TOK, PAIRS, HEAD, 128),
             *TRADE_SEMAPHORES,
             fine(4, BRANCH, DRAFT, WIDTH),
             fine(ROWS, 128),
             fine(BRANCH, DRAFT, WIDTH),
             fine(ROWS, WIDTH),
             fine(ROWS, WIDTH),
-            fine(ROWS, KEYS + WIDTH),
+            fine(ROWS, KEYS),
             fine(ROWS, 1),
             fine(ROWS, 1),
             dma(4, 16),
@@ -875,7 +898,7 @@
         ),
         cost_estimate=pl.CostEstimate(flops=12 << 30, transcendentals=1 << 20, bytes_accessed=60 << 20),
         name="layer",
-    )(meta, store, packed, spot, dense_own, priors, scales, blends, narrow, widen, baseline, boost, kept_column, *weights)
+    )(meta, ids, dense_own, priors, scales, blends, narrow, widen, baseline, boost, kept_column, *weights)
 
 
 def body(
@@ -910,11 +933,13 @@
     owned_here = owners == tok_at
     send_slot = jnp.sum(jnp.where(owned_here, places, 0), axis=1)
     sending = jnp.any(owned_here, axis=1)
-    packed, spot, most = pack(
-        tok_at.reshape(1), guess_symbol_ids.reshape(TOK, ROWS), symbol_vector_lookup
-    )
-
-    crowded = most[0, 0] > SPACE
+    ids = guess_symbol_ids.reshape(TOK, ROWS)
+    order = jnp.arange(ROWS, dtype=jnp.int32)
+    again = (ids[:, :, None] == ids[:, None, :]) & (order[:, None] > order[None, :])
+    first = ~jnp.any(again, axis=2)
+    shard = (ids // vocab_rows)[:, None, :] == jnp.arange(TOK, dtype=jnp.int32)[None, :, None]
+    need = jnp.sum((shard & first[:, None, :]).astype(jnp.int32), axis=2)
+    crowded = jnp.max(need) > SPACE
 
     def dense(_):
         wanted = guess_symbol_ids - tok_at * vocab_rows
@@ -943,18 +968,21 @@
     source = jnp.sum(jnp.where(hit, jnp.arange(TOK, dtype=jnp.int32)[None, :], 0), axis=1)
     meta = jnp.concatenate(
         [
-            send_slot, my_owners, my_owners[request_of], winner, kept_guess_tally[winner], pick_index, source,
-            jnp.any(hit, axis=1).astype(jnp.int32), crowded.astype(jnp.int32).reshape(1),
+            send_slot, my_owners, my_owners[request_of], winner, kept_guess_tally[winner], pick_index,
+            crowded.astype(jnp.int32).reshape(1),
         ]
     )
-    layer_out, shift_att_out, shift_ffn_out, store_out = layer(
-        meta, memory_matrix_store, packed.reshape(TOK, SPACE, WIDTH), spot, dense_own, priors,
+    made_out, made_att, made_ffn, returned = layer(
+        meta, ids, dense_own, priors,
         layernorm_scales, lagged_blend_ratios, forgetting_narrow_matrix, forgetting_widen_matrix,
         forgetting_baseline_vector.reshape(1, HIDDEN), diagonal_boost.reshape(1, HIDDEN),
-        kept_guess_tally.reshape(BRANCH, 1), attention_matrices, attention_result_matrix,
+        kept_guess_tally.reshape(BRANCH, 1), memory_matrix_store, symbol_vector_lookup, attention_matrices, attention_result_matrix,
         feedforward_lookup_matrix, feedforward_gating_matrix, feedforward_content_matrix,
     )
-    return (layer_out, shift_att_out, shift_ffn_out, store_out)
+    return finish(
+        source, jnp.any(hit, axis=1).astype(jnp.int32), made_out, made_att, made_ffn, returned,
+        memory_matrix_store,
+    )
 
 
 def solution(mesh):

time: 223 us -> 188 us (0.84)
  Pallas kernels: 203 us -> 175 us
  local copies, waits for them, and re-layouts: 14.7 us -> 5.03 us
  other arithmetic: 2.86 us -> 6.29 us
    pallas_call x1, Pallas kernels: 192 us -> 169 us  [layer(): pl.pallas_call(layer_kernel, out_shape=(jax.ShapeDtypeStruct((ROWS, WIDTH...]
    unnamed x20 -> x10, local copies, waits for them, and re-layouts: 9.65 us -> 0.69 us
    pallas_call x1, Pallas kernels: 10.5 us -> 5.61 us  [finish(): pl.pallas_call(finish_kernel, out_shape=tuple((jax.ShapeDtypeStruct(v.sha...]
where the time goes in v4:
time: 188 us
  Pallas kernels  175 us (93%)
  other arithmetic  6.29 us (3%)
  local copies, waits for them, and re-layouts  5.03 us (3%)
    pallas_call x1, Pallas kernels, layer(): pl.pallas_call(layer_kernel, out_shape=(jax.ShapeDtypeStruct((ROWS, WIDTH...  169 us
    pallas_call x1, Pallas kernels, finish(): pl.pallas_call(finish_kernel, out_shape=tuple((jax.ShapeDtypeStruct(v.sha...  5.61 us

profile of v4, /device:TPU:1, one launch (start us, length us, event | category | flops | bytes accessed | tf_op | source)
XLA Modules:
  0.0 187.6 jit_solution(2845617448121780066)
XLA Ops:
  0.6 0.0 copy-start
  0.6 0.7 and_select_fusion.2
  1.3 0.1 reshape.182
  1.4 0.1 fusion.11
  1.5 0.1 reshape.183
  1.6 0.1 select_reduce_fusion
  1.7 0.6 select_reduce_fusion.1.source
  2.4 0.1 fusion.5
  2.5 0.5 convert_element_type.13.hit
  3.1 0.0 copy-done
  3.1 0.2 dynamic-slice_reduce_fusion
  3.2 0.2 reduce-window.8
  3.4 0.1 convert_reduce_fusion.1
  3.5 0.7 gather_fusion.1
  4.2 0.7 subtract_add_fusion
  4.9 0.1 select_reduce_fusion.3
  5.0 1.3 gather_fusion.2
  6.3 0.7 reshape.186.ids
  7.0 0.0 copy-start.2
  7.1 1.3 and_reduce_fusion
  8.4 0.4 convert_reduce_fusion
  8.8 0.6 reduce_max.22
  10.1 0.6 concatenate.6.meta
  10.7 0.0 copy-start.4
  10.7 0.0 copy-start.5
  10.7 0.0 copy-start.1
  10.7 0.0 copy-done.2
  10.7 0.7 copy-done.4
  11.4 0.0 copy-done.5
  11.4 0.6 pad_maximum_fusion.priors
  12.0 0.0 copy-done.1
  12.0 0.7 copy.25.kept_column
  12.7 169.2 %layer.1 = (bf16[256,512]{1,0:T(8,128)(2,1)}, bf16[16,512]{1,0:T(8,128)(2,1)}, bf16[16,512]{1,0:T(8,128)(2,1)}, bf16[16,4,64,128]{3,2,1,0:T(8,128)(2,1)}) custom-call(s32[73]{0:T(128)} %concatenate.6.meta, s32[16,256]{1,0:T(8,128)} %copy-done.2, bf16[256,512]{1,0:T(8,128)(2,1)S(1)} %get-tuple-element.32.dense_own, bf16[32,512]{1,0:T(8,128)(2,1)} %pad_maximum_fusion.priors, ...), custom_call_target="tpu_custom_call" | custom-call | flops 12884901888 | bytes 62914560 | tf_op jit(solution)/shard_map/layer/pallas_call | solution.py:843
  181.9 5.6 %finish.1 = (bf16[256,512]{1,0:T(8,128)(2,1)}, bf16[16,512]{1,0:T(8,128)(2,1)}, bf16[16,512]{1,0:T(8,128)(2,1)}, f32[16,8,4096]{2,1,0:T(8,128)}) custom-call(s32[16]{0:T(128)} %select_reduce_fusion.1.source, s32[16]{0:T(128)} %convert_element_type.13.hit, bf16[256,512]{1,0:T(8,128)(2,1)} %get-tuple-element.20.made_out, ...), custom_call_target="tpu_custom_call" | custom-call | tf_op jit(solution)/shard_map/finish/pallas_call | solution.py:516
  (11 shorter events, 0.2 us)
Async XLA Ops:
  0.6 2.4 %copy-start = (s32[16,8]{0,1:T(8,128)S(1)}, s32[16,8]{0,1:T(8,128)}, u32[]{:S(2)}) copy-start(s32[16,8]{0,1:T(8,128)} %param.38) | copy-start | bytes 1540
  7.0 3.6 %copy-start.2 = (s32[16,256]{1,0:T(8,128)}, s32[16,256]{1,0:T(8,128)S(1)}, u32[]{:S(2)}) copy-start(s32[16,256]{1,0:T(8,128)S(1)} %reshape.186.ids) | copy-start | bytes 49156
  10.7 0.7 copy-start.4
  10.7 0.7 copy-start.5
  10.7 1.4 copy-start.1

commit v5 on v4

--- a/solution.py
+++ b/solution.py
@@ -489,7 +489,7 @@
     return jnp.transpose(spot_row[...])[:, 0:1]
 
 
-def finish_kernel(source, hit, made_out, made_att, made_ffn, returned, store, out, shift_att, shift_ffn, store_out):
+def finish_kernel(writes, made_out, made_att, made_ffn, returned, store, out, shift_att, shift_ffn, store_out):
     step = pl.program_id(0)
 
     @pl.when(step == 0)
@@ -500,8 +500,8 @@
 
     for k in range(4):
         slot = step * 4 + k
-        page = returned[source[slot]].astype(F32)
-        taken = hit[slot] > 0
+        page = returned[writes[slot]].astype(F32)
+        taken = writes[TOK + slot] > 0
 
         def put(column, value):
             columns = slice(column, column + 128)
@@ -510,14 +510,14 @@
         flat_page(page, put)
 
 
-def finish(source, hit, made_out, made_att, made_ffn, returned, store):
+def finish(writes, made_out, made_att, made_ffn, returned, store):
     full = lambda *shape: pl.BlockSpec(shape, lambda k, *_: (0,) * len(shape))
     slots = pl.BlockSpec((4, REQ, HIDDEN), lambda k, *_: (k, 0, 0))
     return pl.pallas_call(
         finish_kernel,
         out_shape=tuple(jax.ShapeDtypeStruct(v.shape, v.dtype) for v in (made_out, made_att, made_ffn, store)),
         grid_spec=pltpu.PrefetchScalarGridSpec(
-            num_scalar_prefetch=2,
+            num_scalar_prefetch=1,
             grid=(4,),
             in_specs=[
                 full(ROWS, WIDTH), full(BRANCH, WIDTH), full(BRANCH, WIDTH),
@@ -526,7 +526,7 @@
             out_specs=(full(ROWS, WIDTH), full(BRANCH, WIDTH), full(BRANCH, WIDTH), slots),
         ),
         name="finish",
-    )(source, hit, made_out, made_att, made_ffn, returned, store)
+    )(writes, made_out, made_att, made_ffn, returned, store)
 
 
 def dot(a, b):
@@ -577,7 +577,7 @@
     return jnp.concatenate([jnp.where(side, page, none), jnp.where(side, none, page)], axis=0)
 
 
-META = ("slots", TOK), ("owner_of", REQ), ("page_of", BRANCH), ("winner", REQ), ("kept", REQ), ("pick", TOK), ("dense", 1)
+META = ("slots", TOK), ("sent", TOK), ("owner_of", REQ), ("page_of", BRANCH), ("request_of", BRANCH), ("winner", REQ), ("kept", REQ), ("pick", TOK)
 
 
 def starts():
@@ -603,10 +603,10 @@
 
 
 def layer_kernel(
-    meta, ids, dense_own, priors, scales, blends, narrow, widen, baseline, boost, kept_column,
+    page_ids, counts, kept, crowded, ids, dense_own, prior_att, prior_ffn, scales, blends, narrow, widen, baseline, boost,
     store_w, table_w, attention_w, result_w, lookup_w, gating_w, content_w,
-    out, shift_att, shift_ffn, returned,
-    store, table, packed, spot_row, slot_s, lsem,
+    out, shift_att, shift_ffn, returned, writes,
+    meta, store, table, packed, spot_row, slot_s, lsem,
     whole, residuals, results, lookups, gatings, contents, wbuf, part,
     mated, sums, halves, full, rsend, rrecv,
     own, residual, parcels, psend, precv, plocal, gsend, grecv, glocal,
@@ -615,6 +615,62 @@
 ):
     base = starts()
     word = lambda name, index: meta[base[name] + index]
+
+    def note(name, index, value):
+        meta[base[name] + index] = value
+
+    def when(test, value):
+        return jnp.where(test, value, 0)
+
+    def note_slots():
+        @pl.loop(0, TOK)
+        def _(peer):
+            slot, sent = 0, 0
+            for q in range(REQ):
+                page = page_ids[peer * REQ + q]
+                here = (page >> 4) == t
+                slot = jnp.maximum(slot, when(here, page & 15))
+                sent = jnp.maximum(sent, when(here, 1))
+            note("slots", peer, slot)
+            note("sent", peer, sent)
+
+    def note_rest():
+        for q in range(REQ):
+            note("owner_of", q, page_ids[t * REQ + q] >> 4)
+
+        @pl.loop(0, TOK)
+        def _(peer):
+            pick, source, hit = 0, 0, 0
+            for q in range(REQ):
+                pick = jnp.maximum(pick, when(word("owner_of", q) == peer, q))
+            for group in range(TOK):
+                match = when(word("slots", group) == peer, word("sent", group))
+                source = jnp.maximum(source, match * group)
+                hit = jnp.maximum(hit, match)
+            note("pick", peer, pick)
+            writes[peer] = source
+            writes[TOK + peer] = hit
+
+        @pl.loop(0, BRANCH)
+        def _(b):
+            end, request, owner = 0, 0, 0
+            for q in range(REQ):
+                end += counts[t, q]
+                request += when(end <= b, 1)
+            for q in range(REQ):
+                owner += when(request == q, word("owner_of", q))
+            note("request_of", b, request)
+            note("page_of", b, owner)
+
+        @pl.loop(0, REQ)
+        def _(q):
+            best = 0
+            for b in range(BRANCH):
+                score = kept[b] * BRANCH + (BRANCH - 1 - b)
+                best = jnp.maximum(best, when(word("request_of", b) == q, score))
+            note("winner", q, BRANCH - 1 - (best & 15))
+            note("kept", q, best >> 4)
+
     t, g = lax.axis_index("tok"), lax.axis_index("grp")
     mine = block_of(g)
     bring_table = pltpu.make_async_copy(table_w, table, lsem.at[0])
@@ -655,6 +711,7 @@
         copies.append(copy)
     con[0]()
     gat[0]()
+    note_slots()
     bring_store.wait()
 
     @pl.loop(0, TOK)
@@ -668,7 +725,13 @@
 
     res[1]()
     look[1]()
-    own[ROWS:] = priors[...]
+    own[ROWS : ROWS + BRANCH] = prior_att[...]
+    own[ROWS + BRANCH :] = prior_ffn[...]
+    note_rest()
+    branch = lax.broadcasted_iota(jnp.int32, (BRANCH, 1), 0)
+    kept_column = jnp.zeros((BRANCH, 1), jnp.int32)
+    for b in range(BRANCH):
+        kept_column = jnp.where(branch == b, kept[b], kept_column)
     slots = lax.broadcasted_iota(jnp.int32, (ROWS, TOK * SPACE), 1)
     choice = (slots == spot.astype(jnp.int32)).astype(BF16)
     keep.wait()
@@ -676,7 +739,7 @@
         origin = lax.rem(t + TOK - k, TOK)
         remote(packed.at[t], parcels.at[origin], psend.at[k - 1], precv.at[k - 1], {"tok": origin}).wait_recv()
     picked = dot(choice, parcels[...].reshape(TOK * SPACE, WIDTH)).astype(BF16)
-    own[:ROWS] = jnp.where(word("dense", 0) > 0, dense_own[...], picked)
+    own[:ROWS] = jnp.where(crowded[0] > 0, dense_own[...], picked)
     trades = []
 
     def bring():
@@ -702,7 +765,7 @@
 
         @pl.when(k == g)
         def _():
-            shift_att[...] = kept_row(normed, prior, kept_column[...])
+            shift_att[...] = kept_row(normed, prior, kept_column)
 
         blend = blends[:, columns]
         for c in range(4):
@@ -806,7 +869,7 @@
 
         @pl.when(k == g)
         def _():
-            shift_ffn[...] = kept_row(normed, prior, kept_column[...])
+            shift_ffn[...] = kept_row(normed, prior, kept_column)
 
         blend = blends[:, columns]
         y_of, x_of = k // 2, pl.ds(lax.rem(k, 2) * 2, 2)
@@ -835,7 +898,7 @@
     out[...] = (residual[...].astype(F32) + jax.nn.sigmoid(received) * total).astype(BF16)
 
 
-def layer(meta, ids, dense_own, priors, scales, blends, narrow, widen, baseline, boost, kept_column, *weights):
+def layer(page_ids, counts, kept, crowded, ids, dense_own, prior_att, prior_ffn, scales, blends, narrow, widen, baseline, boost, *weights):
     rows = ROWS + 2 * BRANCH
     wide = lambda *shape: pltpu.VMEM(shape, BF16)
     fine = lambda *shape: pltpu.VMEM(shape, F32)
@@ -847,10 +910,12 @@
             jax.ShapeDtypeStruct((BRANCH, WIDTH), BF16),
             jax.ShapeDtypeStruct((BRANCH, WIDTH), BF16),
             jax.ShapeDtypeStruct((TOK, PAIRS, HEAD, 128), BF16),
+            jax.ShapeDtypeStruct((2 * TOK,), jnp.int32),
         ),
-        in_specs=[pl.BlockSpec(memory_space=pltpu.SMEM)] + [VMEM] * 10 + [ANY] * 7,
-        out_specs=(VMEM, VMEM, VMEM, VMEM),
+        in_specs=[pl.BlockSpec(memory_space=pltpu.SMEM)] * 4 + [VMEM] * 10 + [ANY] * 7,
+        out_specs=(VMEM, VMEM, VMEM, VMEM, pl.BlockSpec(memory_space=pltpu.SMEM)),
         scratch_shapes=[
+            pltpu.SMEM((sum(count for _, count in META),), jnp.int32),
             fine(*weights[0].shape),
             wide(*weights[1].shape),
             wide(TOK, SPACE, WIDTH),
@@ -898,7 +963,7 @@
         ),
         cost_estimate=pl.CostEstimate(flops=12 << 30, transcendentals=1 << 20, bytes_accessed=60 << 20),
         name="layer",
-    )(meta, ids, dense_own, priors, scales, blends, narrow, widen, baseline, boost, kept_column, *weights)
+    )(page_ids, counts, kept, crowded, ids, dense_own, prior_att, prior_ffn, scales, blends, narrow, widen, baseline, boost, *weights)
 
 
 def body(
@@ -924,15 +989,7 @@
 ):
     tok_at = lax.axis_index("tok")
     vocab_rows = symbol_vector_lookup.shape[0]
-    slot_count = memory_matrix_store.shape[0]
-
-    priors = jnp.concatenate([prior_attention_normed, prior_feedforward_normed], axis=0)
-
-    owners = (query_memory_slot // slot_count).reshape(TOK, REQ)
-    places = (query_memory_slot % slot_count).reshape(TOK, REQ)
-    owned_here = owners == tok_at
-    send_slot = jnp.sum(jnp.where(owned_here, places, 0), axis=1)
-    sending = jnp.any(owned_here, axis=1)
+
     ids = guess_symbol_ids.reshape(TOK, ROWS)
     order = jnp.arange(ROWS, dtype=jnp.int32)
     again = (ids[:, :, None] == ids[:, None, :]) & (order[:, None] > order[None, :])
@@ -950,39 +1007,17 @@
 
     dense_own = lax.cond(crowded, dense, lambda _: jnp.zeros((ROWS, WIDTH), BF16), 0)
 
-    my_owners = lax.dynamic_index_in_dim(owners, tok_at, 0, keepdims=False)
-    my_counts = lax.dynamic_index_in_dim(candidate_tally_each_query, tok_at, 0, keepdims=False)
-    local_ids = jnp.arange(BRANCH, dtype=jnp.int32)
-    request_ends = jnp.cumsum(my_counts)
-    request_of = jnp.sum((request_ends[None, :] <= local_ids[:, None]).astype(jnp.int32), axis=1)
-    branch_score = kept_guess_tally * BRANCH + (BRANCH - 1 - local_ids)
-    member = request_of[None, :] == jnp.arange(REQ, dtype=jnp.int32)[:, None]
-    best_score = jnp.max(jnp.where(member, branch_score[None, :], -1), axis=1)
-    winner = BRANCH - 1 - best_score % BRANCH
-
-    targets = my_owners[None, :] == jnp.arange(TOK, dtype=jnp.int32)[:, None]
-    pick_index = jnp.sum(
-        jnp.where(targets, jnp.arange(REQ, dtype=jnp.int32)[None, :], 0), axis=1
-    )
-    hit = (send_slot[None, :] == jnp.arange(slot_count, dtype=jnp.int32)[:, None]) & sending[None, :]
-    source = jnp.sum(jnp.where(hit, jnp.arange(TOK, dtype=jnp.int32)[None, :], 0), axis=1)
-    meta = jnp.concatenate(
-        [
-            send_slot, my_owners, my_owners[request_of], winner, kept_guess_tally[winner], pick_index,
-            crowded.astype(jnp.int32).reshape(1),
-        ]
-    )
-    made_out, made_att, made_ffn, returned = layer(
-        meta, ids, dense_own, priors,
+    made_out, made_att, made_ffn, returned, writes = layer(
+        query_memory_slot, candidate_tally_each_query, kept_guess_tally,
+        crowded.astype(jnp.int32).reshape(1), ids, dense_own,
+        prior_attention_normed, prior_feedforward_normed,
         layernorm_scales, lagged_blend_ratios, forgetting_narrow_matrix, forgetting_widen_matrix,
         forgetting_baseline_vector.reshape(1, HIDDEN), diagonal_boost.reshape(1, HIDDEN),
-        kept_guess_tally.reshape(BRANCH, 1), memory_matrix_store, symbol_vector_lookup, attention_matrices, attention_result_matrix,
-        feedforward_lookup_matrix, feedforward_gating_matrix, feedforward_content_matrix,
+        memory_matrix_store, symbol_vector_lookup, attention_matrices,
+        attention_result_matrix, feedforward_lookup_matrix, feedforward_gating_matrix,
+        feedforward_content_matrix,
     )
-    return finish(
-        source, jnp.any(hit, axis=1).astype(jnp.int32), made_out, made_att, made_ffn, returned,
-        memory_matrix_store,
-    )
+    return finish(writes, made_out, made_att, made_ffn, returned, memory_matrix_store)
 
 
 def solution(mesh):

time: 188 us -> 181 us (0.963)
  other arithmetic: 6.29 us -> 2.34 us
  local copies, waits for them, and re-layouts: 5.03 us -> 2.04 us
    gather x2 -> x0, local copies, waits for them, and re-layouts: 1.96 us -> none  [the longest x1 1.3 us: body(): kept_guess_tally[winner]]
where the time goes in v5:
time: 181 us
  Pallas kernels  175 us (97%)
  other arithmetic  2.34 us (1%)
  local copies, waits for them, and re-layouts  2.04 us (1%)
    pallas_call x1, Pallas kernels, layer(): pl.pallas_call(layer_kernel, out_shape=(jax.ShapeDtypeStruct((ROWS, WIDTH...  169 us
    pallas_call x1, Pallas kernels, finish(): pl.pallas_call(finish_kernel, out_shape=tuple((jax.ShapeDtypeStruct(v.sha...  5.6 us

profile of v5, /device:TPU:1, one launch (start us, length us, event | category | flops | bytes accessed | tf_op | source)
XLA Modules:
  0.0 180.6 jit_solution(12043804284642464426)
XLA Ops:
  0.6 0.7 reshape.83.ids
  1.4 0.0 copy-start
  1.4 1.3 and_reduce_fusion
  2.7 0.4 convert_reduce_fusion
  3.1 0.6 reduce_max.9
  4.4 0.0 copy-start.1
  4.4 0.0 copy-done
  4.5 0.6 copy-done.1
  5.1 0.7 copy.24.counts
  5.7 169.2 %layer.1 = (bf16[256,512]{1,0:T(8,128)(2,1)}, bf16[16,512]{1,0:T(8,128)(2,1)}, bf16[16,512]{1,0:T(8,128)(2,1)}, bf16[16,4,64,128]{3,2,1,0:T(8,128)(2,1)}, s32[32]{0:T(128)}) custom-call(s32[128]{0:T(128)} %page_ids.1, s32[16,8]{1,0:T(8,128)} %copy.24.counts, s32[16]{0:T(128)} %kept.1, s32[1]{0:T(128)} %bitcast.1.crowded, s32[16,256]{1,0:T(8,128)} %copy-done, ...), custom_call_target="tpu_custom_call" | custom-call | flops 12884901888 | bytes 62914560 | tf_op jit(solution)/shard_map/layer/pallas_call | solution.py:906
  175.0 5.6 %finish.1 = (bf16[256,512]{1,0:T(8,128)(2,1)}, bf16[16,512]{1,0:T(8,128)(2,1)}, bf16[16,512]{1,0:T(8,128)(2,1)}, f32[16,8,4096]{2,1,0:T(8,128)}) custom-call(s32[32]{0:T(128)} %get-tuple-element.21.writes, bf16[256,512]{1,0:T(8,128)(2,1)} %get-tuple-element.22.made_out, bf16[16,512]{1,0:T(8,128)(2,1)} %get-tuple-element.23.made_att, ...), custom_call_target="tpu_custom_call" | custom-call | tf_op jit(solution)/shard_map/finish/pallas_call | solution.py:516
  (5 shorter events, 0.1 us)
Async XLA Ops:
  1.4 3.0 %copy-start = (s32[16,256]{1,0:T(8,128)}, s32[16,256]{1,0:T(8,128)S(1)}, u32[]{:S(2)}) copy-start(s32[16,256]{1,0:T(8,128)S(1)} %reshape.83.ids) | copy-start | bytes 49156
  4.4 0.7 copy-start.1

commit v6 on v5

--- a/solution.py
+++ b/solution.py
@@ -489,7 +489,7 @@
     return jnp.transpose(spot_row[...])[:, 0:1]
 
 
-def finish_kernel(writes, made_out, made_att, made_ffn, returned, store, out, shift_att, shift_ffn, store_out):
+def finish_kernel(writes, made_out, made_att, made_ffn, pages, store, out, shift_att, shift_ffn, store_out):
     step = pl.program_id(0)
 
     @pl.when(step == 0)
@@ -500,14 +500,7 @@
 
     for k in range(4):
         slot = step * 4 + k
-        page = returned[writes[slot]].astype(F32)
-        taken = writes[TOK + slot] > 0
-
-        def put(column, value):
-            columns = slice(column, column + 128)
-            store_out[k, :, columns] = jnp.where(taken, value, store[k, :, columns])
-
-        flat_page(page, put)
+        store_out[k] = jnp.where(writes[TOK + slot] > 0, pages[k].astype(F32), store[k])
 
 
 def finish(writes, made_out, made_att, made_ffn, returned, store):
@@ -521,7 +514,7 @@
             grid=(4,),
             in_specs=[
                 full(ROWS, WIDTH), full(BRANCH, WIDTH), full(BRANCH, WIDTH),
-                full(TOK, PAIRS, HEAD, 128), slots,
+                slots, slots,
             ],
             out_specs=(full(ROWS, WIDTH), full(BRANCH, WIDTH), full(BRANCH, WIDTH), slots),
         ),
@@ -605,8 +598,8 @@
 def layer_kernel(
     page_ids, counts, kept, crowded, ids, dense_own, prior_att, prior_ffn, scales, blends, narrow, widen, baseline, boost,
     store_w, table_w, attention_w, result_w, lookup_w, gating_w, content_w,
-    out, shift_att, shift_ffn, returned, writes,
-    meta, store, table, packed, spot_row, slot_s, lsem,
+    out, shift_att, shift_ffn, flat_pages, writes,
+    returned, meta, store, table, packed, spot_row, slot_s, lsem,
     whole, residuals, results, lookups, gatings, contents, wbuf, part,
     mated, sums, halves, full, rsend, rrecv,
     own, residual, parcels, psend, precv, plocal, gsend, grecv, glocal,
@@ -887,6 +880,15 @@
         gat[3]()
         trade_end(out_pages, returned, bsend, brecv, trades[1])
 
+        @pl.loop(0, TOK)
+        def _(slot):
+            page = returned[writes[slot]].astype(F32)
+
+            def put(column, value):
+                flat_pages[slot, :, pl.ds(column, 128)] = value.astype(BF16)
+
+            flat_page(page, put)
+
     total = reduce_grp(part, mated, sums, halves, full, rsend, rrecv, pages)
     gat[4]()
     received = jnp.zeros((ROWS, WIDTH), F32)
@@ -909,12 +911,13 @@
             jax.ShapeDtypeStruct((ROWS, WIDTH), BF16),
             jax.ShapeDtypeStruct((BRANCH, WIDTH), BF16),
             jax.ShapeDtypeStruct((BRANCH, WIDTH), BF16),
-            jax.ShapeDtypeStruct((TOK, PAIRS, HEAD, 128), BF16),
+            jax.ShapeDtypeStruct((TOK, REQ, HIDDEN), BF16),
             jax.ShapeDtypeStruct((2 * TOK,), jnp.int32),
         ),
         in_specs=[pl.BlockSpec(memory_space=pltpu.SMEM)] * 4 + [VMEM] * 10 + [ANY] * 7,
         out_specs=(VMEM, VMEM, VMEM, VMEM, pl.BlockSpec(memory_space=pltpu.SMEM)),
         scratch_shapes=[
+            wide(TOK, PAIRS, HEAD, 128),
             pltpu.SMEM((sum(count for _, count in META),), jnp.int32),
             fine(*weights[0].shape),
             wide(*weights[1].shape),

time: 181 us -> 180 us (level)
  no operation moved by 1% of the time
where the time goes in v6:
time: 180 us
  Pallas kernels  174 us (97%)
  other arithmetic  2.34 us (1%)
  local copies, waits for them, and re-layouts  2.04 us (1%)
    pallas_call x1, Pallas kernels, layer(): pl.pallas_call(layer_kernel, out_shape=(jax.ShapeDtypeStruct((ROWS, WIDTH...  169 us
    pallas_call x1, Pallas kernels, finish(): pl.pallas_call(finish_kernel, out_shape=tuple((jax.ShapeDtypeStruct(v.sha...  4.85 us

profile of v6, /device:TPU:1, one launch (start us, length us, event | category | flops | bytes accessed | tf_op | source)
XLA Modules:
  0.0 179.5 jit_solution(466223236458911375)
XLA Ops:
  0.6 0.7 reshape.83.ids
  1.4 0.0 copy-start
  1.4 1.3 and_reduce_fusion
  2.7 0.4 convert_reduce_fusion
  3.1 0.6 reduce_max.9
  4.4 0.0 copy-start.1
  4.4 0.0 copy-done
  4.5 0.6 copy-done.1
  5.1 0.7 copy.24.counts
  5.7 168.9 %layer.1 = (bf16[256,512]{1,0:T(8,128)(2,1)}, bf16[16,512]{1,0:T(8,128)(2,1)}, bf16[16,512]{1,0:T(8,128)(2,1)}, bf16[16,8,4096]{2,1,0:T(8,128)(2,1)}, s32[32]{0:T(128)}) custom-call(s32[128]{0:T(128)} %page_ids.1, s32[16,8]{1,0:T(8,128)} %copy.24.counts, s32[16]{0:T(128)} %kept.1, s32[1]{0:T(128)} %bitcast.1.crowded, s32[16,256]{1,0:T(8,128)} %copy-done, ...), custom_call_target="tpu_custom_call" | custom-call | flops 12884901888 | bytes 62914560 | tf_op jit(solution)/shard_map/layer/pallas_call | solution.py:908
  174.7 4.9 %finish.1 = (bf16[256,512]{1,0:T(8,128)(2,1)}, bf16[16,512]{1,0:T(8,128)(2,1)}, bf16[16,512]{1,0:T(8,128)(2,1)}, f32[16,8,4096]{2,1,0:T(8,128)}) custom-call(s32[32]{0:T(128)} %get-tuple-element.21.writes, bf16[256,512]{1,0:T(8,128)(2,1)} %get-tuple-element.22.made_out, bf16[16,512]{1,0:T(8,128)(2,1)} %get-tuple-element.23.made_att, ...), custom_call_target="tpu_custom_call" | custom-call | tf_op jit(solution)/shard_map/finish/pallas_call | solution.py:509
  (5 shorter events, 0.1 us)
Async XLA Ops:
  1.4 3.0 %copy-start = (s32[16,256]{1,0:T(8,128)}, s32[16,256]{1,0:T(8,128)S(1)}, u32[]{:S(2)}) copy-start(s32[16,256]{1,0:T(8,128)S(1)} %reshape.83.ids) | copy-start | bytes 49156
  4.4 0.7 copy-start.1
